TPU v7x, 32 devices: a whole 2x2x4 slice. The times are simulated.
32 devices in a mesh: groups: 2 (over y), leaf: 4 (over z), vec: 2 (over x), lvl: 2 (over core).
Axes of the slice: x: 2, y: 2, z: 4, core: 2. Of those that a mesh axis runs over, the one named last changes fastest.
Arguments:
- adjoint_in: bfloat16 [128, 8192], P('groups', 'leaf'), parts along dimension 0, may hold values from -6 to 6
- row_basis: bfloat16 [64, 64, 256], P(('groups', 'leaf')), parts along dimension 0, may hold values from -0.375 to 0.375
- col_basis: bfloat16 [64, 64, 256], P(('groups', 'leaf')), parts along dimension 0, may hold values from -0.75 to 0.75
- row_transfer: bfloat16 [64, 64, 64], P(('groups', 'leaf')), parts along dimension 0, may hold values from -0.75 to 0.75
- col_transfer: bfloat16 [64, 64, 64], P(('groups', 'leaf')), parts along dimension 0, may hold values from -0.75 to 0.75
- parents: int32 [64], P(('groups', 'leaf')), parts along dimension 0, may hold values from 0 to 7, never falling along the last dimension, each value on 1 to 8 neighbouring positions
- far_sources: int32 [64, 64], P(('groups', 'leaf')), parts along dimension 0, may hold values from 0 to 31
- far_blocks: bfloat16 [64, 64, 64, 64], P(('groups', 'leaf'), ('vec', 'lvl')), parts along dimension 0, may hold values from -0.09375 to 0.09375
- coarse_sources: int32 [16, 32], P(('groups', 'leaf')), parts along dimension 0, may hold values from 0 to 7
- coarse_blocks: bfloat16 [16, 32, 64, 64], P(('groups', 'leaf'), ('vec', 'lvl')), parts along dimension 0, may hold values from -0.0625 to 0.0625
- near_sources: int32 [64, 16], P(('groups', 'leaf')), parts along dimension 0, may hold values from 0 to 31, as said below
- near_blocks: bfloat16 [64, 16, 256, 256], P(('groups', 'leaf'), ('vec', 'lvl')), parts along dimension 0, may hold values from -0.09375 to 0.09375
Outputs:
- adjoint_out: bfloat16 [128, 8192], P(('groups', 'vec', 'lvl'), 'leaf'), parts along dimension 0
There are 2 independent parts, one for each index of `groups`. A program takes and returns all parts, laid end to end along the dimension named above; each array names one. Nothing has to cross between parts.
Inputs may be any that keep to these rules, and one draw needn't show every extreme that they name: `parents`: never falling along the leaves; every cluster has 1 to 8 leaves, and some cluster exactly 8. `near_sources`: every entry names a leaf at most 2 leaves away from its own leaf along the curve; every leaf's list names the leaf 2 before it and the leaf 2 after it, where these exist.
All inputs are finite; a program needn't handle non-finite values.
Results may differ from a plain program's by a relative error of at most 0.0061.
Values may be sent and summed in bfloat16 or wider, within the bound.
No kernel may reach another device: no remote copies, remote signals or barrier semaphores. Data moves between devices by JAX's collectives and lax.ppermute only.
A program may use at most 64 MiB of HBM per device.

v0:
```python
import jax
import jax.numpy as jnp
from jax import lax
from jax.sharding import PartitionSpec as P

REACH = 2


def with_halo(block, sides, width):
    for axis, dim in sides:
        count = lax.axis_size(axis)
        forward = [(i, i + 1) for i in range(count - 1)]
        backward = [(target, source) for source, target in forward]
        low = lax.ppermute(
            lax.slice_in_dim(block, block.shape[dim] - width, None, axis=dim), axis, forward
        )
        high = lax.ppermute(lax.slice_in_dim(block, 0, width, axis=dim), axis, backward)
        block = jnp.concatenate([low, block, high], axis=dim)
    return block


def on_device(
    adjoint_in,
    row_basis,
    col_basis,
    row_transfer,
    col_transfer,
    parents,
    far_sources,
    far_blocks,
    coarse_sources,
    coarse_blocks,
    near_sources,
    near_blocks,
):
    owner_count = lax.axis_size(("vec", "lvl"))
    owner_index = lax.axis_index(("vec", "lvl"))
    leaf_index = lax.axis_index("leaf")
    leaf_count = lax.axis_size("leaf")
    vector_count = adjoint_in.shape[0]
    leaf_rows, rank_width, panel_width = row_basis.shape
    cluster_rows = coarse_sources.shape[0]
    cluster_count = cluster_rows * leaf_count
    far_share = far_blocks.shape[1]
    coarse_share = coarse_blocks.shape[1]
    near_share = near_blocks.shape[1]
    vector_share = vector_count // owner_count
    first_leaf = leaf_index * leaf_rows
    flat_width = vector_count * rank_width
    x_blocks = adjoint_in.reshape(vector_count, leaf_rows, panel_width)
    leaf_up = jnp.einsum(
        "klp,lrp->lkr", x_blocks, row_basis, preferred_element_type=jnp.float32
    ).astype(jnp.bfloat16)
    branch = jnp.einsum("lkr,lrc->lkc", leaf_up, row_transfer, preferred_element_type=jnp.float32)
    branch_flat = branch.reshape(leaf_rows, flat_width)
    cluster_ids = lax.broadcasted_iota(jnp.int32, (cluster_count, leaf_rows), 0)
    members = (cluster_ids == parents[None, :]).astype(jnp.float32)
    partial_up = jnp.dot(members, branch_flat, precision=lax.Precision.HIGHEST)
    cluster_up = lax.psum(partial_up, "leaf").astype(jnp.bfloat16)
    cluster_up = cluster_up.reshape(cluster_count, vector_count, rank_width)
    my_coarse = lax.dynamic_slice_in_dim(
        coarse_sources, owner_index * coarse_share, coarse_share, 1
    )
    coarse_rows = jnp.take(cluster_up, my_coarse.reshape(-1), axis=0)
    coarse_rows = coarse_rows.reshape(cluster_rows, coarse_share, vector_count, rank_width)
    cluster_part = jnp.einsum(
        "cjkr,cjrs->cks", coarse_rows, coarse_blocks, preferred_element_type=jnp.float32
    )
    cluster_part = cluster_part.reshape(cluster_rows, flat_width)
    my_far = lax.dynamic_slice_in_dim(far_sources, owner_index * far_share, far_share, 1)
    shard_rows = lax.all_gather(leaf_up, "leaf", axis=0, tiled=True)
    count = shard_rows.shape[0]
    inside = (my_far >= 0) & (my_far < count)
    picked = jnp.take(shard_rows, jnp.clip(my_far, 0, count - 1).reshape(-1), axis=0)
    picked = jnp.where(inside.reshape(-1, 1, 1), picked, jnp.zeros_like(picked))
    picked = picked.reshape(leaf_rows, far_share, vector_count, rank_width)
    leaf_down_part = jnp.einsum(
        "ljkr,ljrs->lks", picked, far_blocks, preferred_element_type=jnp.float32
    )
    leaf_down_part = leaf_down_part.reshape(leaf_rows, flat_width)
    padded = with_halo(adjoint_in, (("leaf", 1),), REACH * panel_width)
    padded = padded.reshape(vector_count, leaf_rows + 2 * REACH, panel_width)
    my_near = lax.dynamic_slice_in_dim(near_sources, owner_index * near_share, near_share, 1)
    local_near = (my_near - first_leaf + REACH).reshape(-1)
    near_rows = jnp.take(padded, local_near, axis=1).reshape(
        vector_count, leaf_rows, near_share, panel_width
    )
    near_part = jnp.einsum(
        "kljp,ljpq->klq", near_rows, near_blocks, preferred_element_type=jnp.float32
    )
    near_part = near_part.reshape(vector_count, leaf_rows * panel_width)
    leaf_down, cluster_down, near_sum = (
        lax.psum_scatter(leaf_down_part, ("vec", "lvl"), scatter_dimension=1, tiled=True),
        lax.psum_scatter(cluster_part, ("vec", "lvl"), scatter_dimension=1, tiled=True),
        lax.psum_scatter(near_part, ("vec", "lvl"), scatter_dimension=0, tiled=True),
    )
    down_table = lax.all_gather(cluster_down.astype(jnp.bfloat16), "leaf", axis=0, tiled=True)
    pushed = jnp.take(down_table, parents, axis=0).reshape(leaf_rows, vector_share, rank_width)
    carried = jnp.einsum("lkc,lrc->lkr", pushed, col_transfer, preferred_element_type=jnp.float32)
    leaf_total = (leaf_down.reshape(leaf_rows, vector_share, rank_width) + carried).astype(
        jnp.bfloat16
    )
    far_out = jnp.einsum("lkr,lrp->klp", leaf_total, col_basis, preferred_element_type=jnp.float32)
    far_out = far_out.reshape(vector_share, leaf_rows * panel_width)
    return (far_out + near_sum).astype(jnp.bfloat16)


def solution(mesh):
    in_specs = (
        P("groups", "leaf"),
        P(("groups", "leaf"), None, None),
        P(("groups", "leaf"), None, None),
        P(("groups", "leaf"), None, None),
        P(("groups", "leaf"), None, None),
        P(("groups", "leaf")),
        P(("groups", "leaf"), None),
        P(("groups", "leaf"), ("vec", "lvl"), None, None),
        P(("groups", "leaf"), None),
        P(("groups", "leaf"), ("vec", "lvl"), None, None),
        P(("groups", "leaf"), None),
        P(("groups", "leaf"), ("vec", "lvl"), None, None),
    )
    out_specs = P(("groups", "vec", "lvl"), "leaf")
    return jax.shard_map(
        on_device, mesh=mesh, in_specs=in_specs, out_specs=out_specs, check_vma=False
    )
```

profile of v0, /device:TPU:0, one launch (start us, length us, event | category | flops | bytes accessed | tf_op | source)
XLA Modules:
  0.0 121.6 jit_solution(3522487596379460757)
XLA Ops:
  6.5 0.0 copy-start
  6.5 0.9 compare_and_fusion.3
  7.5 0.1 reshape.170
  7.5 1.2 %convolution_convert_fusion = bf16[8,64,64]{2,1,0:T(8,128)(2,1)S(1)} fusion(bf16[8,64,256]{2,1,0:T(8,128)(2,1)} %param.13, bf16[8,8,8,256]{3,2,1,0:T(8,128)(2,1)} %bitcast.57), kind=kOutput, calls=%fused_computation.11 | convolution fusion | flops 16809984 | bytes 589824 | tf_op jit(solution)/shard_map/klp,lrp->lkr/dot_general | solution.py:51
  8.8 1.1 fusion.38
  9.9 0.1 reshape.168
  10.0 0.8 fusion.25
  10.8 23.1 %all-reduce.1 = bf16[8,4096]{1,0:T(8,128)(2,1)S(1)} all-reduce(f32[8,4096]{1,0:T(8,128)S(1)} %fusion.25), channel_id=1, replica_groups=mesh['groups'=2,'leaf'=4,'vec'=2,'lvl'=2] {'leaf'}, use_global_device_ids=true, to_apply=%region_1.2 | all-reduce | flops 32768 | bytes 196608 | tf_op jit(solution)/shard_map/psum | solution.py:59
  34.0 0.2 reshape.169
  34.1 0.6 gather_fusion.1
  34.8 0.3 convolution_bitcast_fusion.2
  35.1 0.0 copy-start.1
  35.1 0.0 copy-start.5
  35.1 2.0 %copy.28 = f32[2,64,64]{0,2,1:T(8,128)} copy(f32[2,64,64]{2,1,0:T(8,128)S(1)} %convolution_bitcast_fusion.2) | data formatting | bytes 65536
  37.1 0.0 reduce-scatter.10.cloned.1.call-update
  37.2 0.0 reduce-scatter.6.cloned.1.call-start
  37.2 1.3 %collective-permute-start = (bf16[64,512]{1,0:T(8,128)(2,1)S(1)}, bf16[64,512]{1,0:T(8,128)(2,1)S(1)}, u32[]{:S(2)}, u32[]{:S(2)}) collective-permute-start(bf16[64,512]{1,0:T(8,128)(2,1)S(1)} %get-tuple-element.9), channel_id=1, source_target_pairs={{0,4},{4,8},{8,12},{1,5},{5,9},{9,13},{2,6},{6,10},{10,14},{3,7},{... | collective-permute-start | bytes 196616 | tf_op jit(solution)/shard_map/ppermute | solution.py:14
  38.5 1.3 %collective-permute-start.1 = (bf16[64,512]{1,0:T(8,128)(2,1)S(1)}, bf16[64,512]{1,0:T(8,128)(2,1)S(1)}, u32[]{:S(2)}, u32[]{:S(2)}) collective-permute-start(bf16[64,512]{1,0:T(8,128)(2,1)S(1)} %get-tuple-element.10), channel_id=1, source_target_pairs={{4,0},{8,4},{12,8},{5,1},{9,5},{13,9},{6,2},{10,6},{14,10},{7,3},{... | collective-permute-start | bytes 196616 | tf_op jit(solution)/shard_map/ppermute | solution.py:17
  39.8 17.5 %all_gather.6 = bf16[32,64,64]{2,1,0:T(8,128)(2,1)S(1)} all-gather(bf16[8,64,64]{2,1,0:T(8,128)(2,1)S(1)} %convolution_convert_fusion), channel_id=1, replica_groups=mesh['groups'=2,'leaf'=4,'vec'=2,'lvl'=2] {'leaf'}, dimensions={0}, use_global_device_ids=true | all-gather | bytes 327680 | tf_op jit(solution)/shard_map/all_gather | solution.py:71
  57.4 0.1 compare_and_fusion.1
  57.4 0.1 reshape.165
  57.5 2.1 %gather_fusion = bf16[128,64,64]{2,1,0:T(8,128)(2,1)} fusion(bf16[32,64,64]{2,1,0:T(8,128)(2,1)S(1)} %all_gather.6, s32[1024]{0:T(1024)S(1)} %pad_clamp_fusion.3), kind=kCustom, calls=%fused_computation | custom fusion | bytes 2097664 | tf_op jit(solution)/shard_map/jit(_take)/gather | solution.py:74
  59.7 2.4 %fusion.5 = f32[8,64,64]{2,1,0:T(8,128)S(1)} fusion(bf16[8,16,64,64]{3,2,1,0:T(8,128)(2,1)S(1)} %copy-done, bf16[8,16,64,64]{3,2,1,0:T(8,128)(2,1)} %bitcast.55, pred[8,16]{1,0:T(8,128)(4,1)S(1)} %get-tuple-element.7, pred[8,16]{1,0:T(8,128)(4,1)S(1)} %get-tuple-element.11), kind=kOutput, calls=%fused_computation.10 | convolution fusion | flops 68157440 | bytes 2228480 | tf_op jit(solution)/shard_map/ljkr,ljrs->lks/dot_general | solution.py:77
  62.1 0.8 reshape.166
  62.9 0.0 reduce-scatter.6.cloned.1.call-update
  62.9 0.0 reduce-scatter.8.cloned.1.call-start
  62.9 0.1 fusion.26
  63.0 0.1 reshape.174
  63.1 0.1 compare_and_fusion
  63.2 0.0 collective-permute-done
  63.2 0.0 collective-permute-done.1
  63.3 0.6 gather_fusion.3
  63.9 0.0 copy-start.6
  63.9 3.1 %convolution_bitcast_fusion = f32[8,8,8,256]{3,2,1,0:T(8,128)S(1)} fusion(bf16[8,4,256,256]{3,2,1,0:T(8,128)(2,1)} %param.23, bf16[64,8,4,256]{3,0,2,1:T(8,128)(2,1)S(1)} %bitcast.53, pred[8,4]{1,0:T(8,128)(4,1)S(1)} %compare_and_fusion), kind=kOutput, calls=%fused_computation.9 | convolution fusion | flops 268959744 | bytes 5767200 | tf_op jit(solution)/shard_map/kljp,ljpq->klq/dot_general | solution.py:88
  67.0 0.0 copy-start.2
  67.0 0.0 copy-start.3
  67.0 0.8 copy.32
  67.9 0.0 reduce-scatter.8.cloned.1.call-update
  68.0 0.0 reduce-scatter.10.cloned.1.call-done
  68.0 1.2 %copy.27 = bf16[2,1024]{1,0:T(2,128)(2,1)S(1)} copy(f32[2,1024]{0,1:T(8,128)} %bitcast.59) | data formatting | bytes 12288
  69.2 13.1 %all-gather = bf16[4,2,1024]{2,1,0:T(2,128)(2,1)S(1)} all-gather(bf16[1,2,1024]{2,1,0:T(2,128)(2,1)S(1)} %bitcast.62), channel_id=1, replica_groups=mesh['groups'=2,'leaf'=4,'vec'=2,'lvl'=2] {'leaf'}, dimensions={0}, use_global_device_ids=true | all-gather | bytes 20480 | tf_op jit(solution)/shard_map/all_gather | solution.py:97
  82.4 0.6 gather_fusion.2
  82.9 0.1 gather.29
  83.0 6.3 %reduce-scatter.6.cloned.1.call-done = f32[8,1024]{1,0:T(8,128)} async-done(((f32[8,4096]{1,0:T(8,128)}), f32[8,1024]{1,0:T(8,128)}) %reduce-scatter.6.cloned.1.call-update) | async-done | bytes 32784 | tf_op jit(solution)/shard_map/reduce_scatter | solution.py:93
  89.3 0.8 reshape.167
  90.1 0.3 convolution_bitcast_fusion.1
  90.5 23.0 %reduce-scatter.8.cloned.1.call-done = f32[16,2048]{1,0:T(8,128)} async-done(((f32[64,2048]{1,0:T(8,128)}), f32[16,2048]{1,0:T(8,128)}) %reduce-scatter.8.cloned.1.call-update) | async-done | bytes 131088 | tf_op jit(solution)/shard_map/reduce_scatter | solution.py:95
  113.5 1.5 %add_convert_fusion = bf16[16,2048]{1,0:T(8,128)(2,1)} fusion(f32[16,2048]{1,0:T(8,128)S(1)} %bitcast.60, f32[16,2048]{1,0:T(8,128)} %reduce-scatter.8.cloned.1.call-done), kind=kLoop, calls=%fused_computation.27 | loop fusion | flops 65536 | bytes 327680 | tf_op jit(solution)/shard_map/convert_element_type | solution.py:105
  (25 shorter events, 0.2 us)
Async XLA Ops:
  6.5 53.1 %copy-start = (bf16[8,16,64,64]{3,2,1,0:T(8,128)(2,1)S(1)}, bf16[8,16,64,64]{3,2,1,0:T(8,128)(2,1)}, u32[]{:S(2)}) copy-start(bf16[8,16,64,64]{3,2,1,0:T(8,128)(2,1)} %param.19) | copy-start | bytes 3145732
  6.5 28.2 %copy-start.7 = (bf16[2,8,64,64]{3,2,1,0:T(8,128)(2,1)S(1)}, bf16[2,8,64,64]{3,2,1,0:T(8,128)(2,1)}, u32[]{:S(2)}) copy-start(bf16[2,8,64,64]{3,2,1,0:T(8,128)(2,1)} %param.21) | copy-start | bytes 393220
  6.5 61.4 %reduce-scatter.10.cloned.1.call-start = ((), (), s32[]{:S(2)}) async-start(), calls=%async_computation.5 | async-start | bytes 2621440
  35.1 2.1 %copy-start.1 = (bf16[64,2048]{1,0:T(8,128)(2,1)S(1)}, bf16[64,2048]{1,0:T(8,128)(2,1)}, u32[]{:S(2)}) copy-start(bf16[64,2048]{1,0:T(8,128)(2,1)} %param.12) | copy-start | bytes 786436
  35.1 22.3 %copy-start.5 = (s32[8,64]{1,0:T(8,128)S(1)}, s32[8,64]{1,0:T(8,128)}, u32[]{:S(2)}) copy-start(s32[8,64]{1,0:T(8,128)} %param.18) | copy-start | bytes 6148
  37.2 52.1 %reduce-scatter.6.cloned.1.call-start = ((), (), s32[]{:S(2)}) async-start(), calls=%async_computation.3 | async-start | bytes 163840 | tf_op jit(solution)/shard_map/reduce_scatter | solution.py:93
  37.2 26.0 %collective-permute-start = (bf16[64,512]{1,0:T(8,128)(2,1)S(1)}, bf16[64,512]{1,0:T(8,128)(2,1)S(1)}, u32[]{:S(2)}, u32[]{:S(2)}) collective-permute-start(bf16[64,512]{1,0:T(8,128)(2,1)S(1)} %get-tuple-element.9), channel_id=1, source_target_pairs={{0,4},{4,8},{8,12},{1,5},{5,9},{9,13},{2,6},{6,10},{10,14},{3,7},{... | collective-permute-start | bytes 196616 | tf_op jit(solution)/shard_map/ppermute | solution.py:14
  38.5 24.7 %collective-permute-start.1 = (bf16[64,512]{1,0:T(8,128)(2,1)S(1)}, bf16[64,512]{1,0:T(8,128)(2,1)S(1)}, u32[]{:S(2)}, u32[]{:S(2)}) collective-permute-start(bf16[64,512]{1,0:T(8,128)(2,1)S(1)} %get-tuple-element.10), channel_id=1, source_target_pairs={{4,0},{8,4},{12,8},{5,1},{9,5},{13,9},{6,2},{10,6},{14,10},{7,3},{... | collective-permute-start | bytes 196616 | tf_op jit(solution)/shard_map/ppermute | solution.py:17
  59.7 3.3 %copy-start.4 = (s32[8,16]{1,0:T(8,128)S(1)}, s32[8,16]{1,0:T(8,128)}, u32[]{:S(2)}) copy-start(s32[8,16]{1,0:T(8,128)} %param.22) | copy-start | bytes 1540
  62.9 50.6 %reduce-scatter.8.cloned.1.call-start = ((), (), s32[]{:S(2)}) async-start(), calls=%async_computation.4 | async-start | bytes 655360 | tf_op jit(solution)/shard_map/reduce_scatter | solution.py:95
  63.9 4.0 %copy-start.6 = (s32[8]{0:T(128)S(1)}, s32[8]{0:T(128)}, u32[]{:S(2)}) copy-start(s32[8]{0:T(128)} %param.17) | copy-start | bytes 100
  67.0 23.1 %copy-start.2 = (bf16[8,64,256]{2,1,0:T(8,128)(2,1)S(1)}, bf16[8,64,256]{2,1,0:T(8,128)(2,1)}, u32[]{:S(2)}) copy-start(bf16[8,64,256]{2,1,0:T(8,128)(2,1)} %param.14) | copy-start | bytes 786436
  67.0 23.1 %copy-start.3 = (bf16[8,64,64]{2,1,0:T(8,128)(2,1)S(1)}, bf16[8,64,64]{2,1,0:T(8,128)(2,1)}, u32[]{:S(2)}) copy-start(bf16[8,64,64]{2,1,0:T(8,128)(2,1)} %param.16) | copy-start | bytes 196612
Sparse Core Ops, SparseCore 0:
  37.3 29.7 reduce-scatter.9
  69.7 19.5 reduce-scatter.5
  91.8 21.6 reduce-scatter.7
where the time goes:
time: 122 us
  blocking collectives  53.7 us (44%)
  waiting for transfers between devices  29.3 us (24%)
  between operations  13.3 us (11%)
  local copies, waits for them, and re-layouts  10.4 us (9%)
  matrix products  9.31 us (8%)
  other arithmetic  2.79 us (2%)
  starting transfers between devices  2.67 us (2%)
    psum x1, blocking collectives, on_device(): cluster_up = lax.psum(partial_up, 'leaf').astype(jnp.bfloat16)  23.1 us
    reduce_scatter x1, waiting for transfers between devices, on_device(): lax.psum_scatter(near_part, ('vec', 'lvl'), scatter_dimension=0, tiled=True)  23 us
    all_gather x1, blocking collectives, on_device(): shard_rows = lax.all_gather(leaf_up, 'leaf', axis=0, tiled=True)  17.5 us
    all_gather x1, blocking collectives, on_device(): lax.all_gather(cluster_down.astype(jnp.bfloat16), 'leaf', axis=0, tiled=T...  13.1 us
    reduce_scatter x1, waiting for transfers between devices, on_device(): lax.psum_scatter(leaf_down_part, ('vec', 'lvl'), scatter_dimension=1, til...  6.26 us
    unnamed x19, local copies, waits for them, and re-layouts  3.33 us
    dot_general x1, matrix products, on_device(): jnp.einsum('kljp,ljpq->klq', near_rows, near_blocks, preferred_element_ty...  3.1 us
  transfers between devices with their start and end apart: 5, of which 2 were waited for; matrix products, arithmetic and copies ran while one was open for 11% of the time, Pallas kernels for 0%

commit v1 on v0

--- a/solution.py
+++ b/solution.py
@@ -1,9 +1,36 @@
+import functools
+
 import jax
 import jax.numpy as jnp
 from jax import lax
+from jax.experimental import pallas as pl
+from jax.experimental.pallas import tpu as pltpu
 from jax.sharding import PartitionSpec as P
 
 REACH = 2
+BF = jnp.bfloat16
+F32 = jnp.float32
+VMEM = pl.BlockSpec(memory_space=pltpu.VMEM)
+SMEM = pl.BlockSpec(memory_space=pltpu.SMEM)
+ANY = pl.BlockSpec(memory_space=pl.ANY)
+LIMIT = 48 << 20
+
+
+def dot(a, b):
+    return jnp.dot(a, b, preferred_element_type=F32)
+
+
+def dot_t(a, b):
+    return lax.dot_general(a, b, (((1,), (1,)), ((), ())), preferred_element_type=F32)
+
+
+def low_half(shape):
+    return lax.broadcasted_iota(jnp.int32, shape, len(shape) - 1) < shape[-1] // 2
+
+
+def swap_halves(x):
+    half = x.shape[-1] // 2
+    return jnp.concatenate([x[..., half:], x[..., :half]], axis=-1)
 
 
 def with_halo(block, sides, width):
@@ -19,7 +46,7 @@
     return block
 
 
-def on_device(
+def on_device_general(
     adjoint_in,
     row_basis,
     col_basis,
@@ -69,10 +96,7 @@
     cluster_part = cluster_part.reshape(cluster_rows, flat_width)
     my_far = lax.dynamic_slice_in_dim(far_sources, owner_index * far_share, far_share, 1)
     shard_rows = lax.all_gather(leaf_up, "leaf", axis=0, tiled=True)
-    count = shard_rows.shape[0]
-    inside = (my_far >= 0) & (my_far < count)
-    picked = jnp.take(shard_rows, jnp.clip(my_far, 0, count - 1).reshape(-1), axis=0)
-    picked = jnp.where(inside.reshape(-1, 1, 1), picked, jnp.zeros_like(picked))
+    picked = jnp.take(shard_rows, my_far.reshape(-1), axis=0)
     picked = picked.reshape(leaf_rows, far_share, vector_count, rank_width)
     leaf_down_part = jnp.einsum(
         "ljkr,ljrs->lks", picked, far_blocks, preferred_element_type=jnp.float32
@@ -103,6 +127,282 @@
     far_out = jnp.einsum("lkr,lrp->klp", leaf_total, col_basis, preferred_element_type=jnp.float32)
     far_out = far_out.reshape(vector_share, leaf_rows * panel_width)
     return (far_out + near_sum).astype(jnp.bfloat16)
+
+
+def up_kernel(x_ref, basis_ref, transfer_ref, coarse_ref, parents_ref,
+              msg_ref, packed_ref, edge_ref, sums):
+    leaves, rank, panel = basis_ref.shape
+    z, c = lax.axis_index("leaf"), lax.axis_index("lvl")
+    width = REACH * panel
+    start = jnp.where((z + c) % 2 == 0, leaves * panel - width, 0)
+    edge_ref[...] = x_ref[:, pl.ds(pl.multiple_of(start, 128), width)]
+    share = coarse_ref.shape[1]
+    for j in range(share):
+        packed_ref[j] = jnp.concatenate([coarse_ref[0, j], coarse_ref[1, j]], axis=-1)
+    sums[...] = jnp.zeros_like(sums)
+    ups = []
+    for l in range(leaves):
+        up = dot_t(x_ref[:, l * panel:(l + 1) * panel], basis_ref[l]).astype(BF)
+        ups.append(up)
+        parent = parents_ref[l]
+        sums[parent] = sums[parent] + dot(up, transfer_ref[l])
+    for p in range(leaves // 2):
+        msg_ref[p] = jnp.concatenate([ups[2 * p], ups[2 * p + 1]], axis=-1)
+    for p in range(sums.shape[0] // 2):
+        msg_ref[leaves // 2 + p] = jnp.concatenate(
+            [sums[2 * p], sums[2 * p + 1]], axis=-1
+        ).astype(BF)
+
+
+def near_kernel(sources_ref, x_ref, mine_ref, other_ref, blocks_hbm, out_ref,
+                table, blocks, sems):
+    leaves, share, panel = blocks.shape[0], blocks.shape[1], blocks.shape[2]
+    z, c = lax.axis_index("leaf"), lax.axis_index("lvl")
+    owner = lax.axis_index("vec") * 2 + c
+    copies = [
+        pltpu.make_async_copy(blocks_hbm.at[l], blocks.at[l], sems.at[l]) for l in range(leaves)
+    ]
+    for copy in copies:
+        copy.start()
+    for l in range(leaves):
+        table[REACH + l] = x_ref[:, l * panel:(l + 1) * panel]
+    high = (z + c) % 2 == 0
+    top, bottom = leaves + REACH, 0
+    at_mine = jnp.where(high, top, bottom)
+    at_other = jnp.where(high, bottom, top)
+    for i in range(REACH):
+        table[at_mine + i] = mine_ref[:, i * panel:(i + 1) * panel]
+        table[at_other + i] = other_ref[:, i * panel:(i + 1) * panel]
+    for l in range(leaves):
+        rows = [
+            table[sources_ref[l, owner * share + j] - z * leaves + REACH] for j in range(share)
+        ]
+        copies[l].wait()
+        out_ref[l] = dot(jnp.concatenate(rows, axis=-1), blocks[l].reshape(share * panel, panel))
+
+
+def coarse_kernel(sources_ref, own_ref, a_ref, la_ref, b_ref, lb_ref,
+                  p_own, p_lvl, p_vec, p_diag, out_ref, table):
+    pairs = own_ref.shape[0] // 2
+    share = p_own.shape[0]
+    c = lax.axis_index("lvl")
+    me = lax.axis_index("vec") * 2 + c
+    rank = own_ref.shape[1]
+    for p in range(pairs):
+        q = pairs + p
+        across = jnp.where(c == 1, b_ref[q].astype(F32), lb_ref[q].astype(F32))
+        total = (own_ref[q].astype(F32) + a_ref[q].astype(F32)) + (la_ref[q].astype(F32) + across)
+        table[p] = total.astype(BF)
+        table[pairs + p] = swap_halves(total).astype(BF)
+    low = low_half((rank, 2 * rank))
+    acc = jnp.zeros((2 * rank, 2 * rank), F32)
+    for flip, blocks in ((0, p_own), (1, p_lvl), (2, p_vec), (3, p_diag)):
+        base = (me ^ flip) * share
+        rows = []
+        for cluster in range(2):
+            lanes = []
+            for j in range(0, share, 2):
+                s0 = sources_ref[cluster, base + j]
+                s1 = sources_ref[cluster, base + j + 1]
+                first = table[(s0 & 1) * pairs + (s0 >> 1)]
+                second = table[(1 - (s1 & 1)) * pairs + (s1 >> 1)]
+                lanes.append(jnp.where(low, first, second))
+            rows.append(jnp.concatenate(lanes, axis=-1))
+        acc = acc + dot(
+            jnp.concatenate(rows, axis=0), blocks[...].reshape(share * rank, 2 * rank)
+        )
+    out_ref[...] = jnp.where(low, acc[:rank], acc[rank:]).astype(BF)
+
+
+def down_kernel(sources_ref, parents_ref, own_ref, a_ref, la_ref, b_ref, lb_ref,
+                blocks_ref, down_ref, got_ref, transfer_ref, basis_ref, near_ref,
+                send_ref, keep_ref, table, total):
+    leaves, share, rank, _ = blocks_ref.shape
+    panel = basis_ref.shape[2]
+    pairs = leaves // 2
+    z, v, c = lax.axis_index("leaf"), lax.axis_index("vec"), lax.axis_index("lvl")
+    owner = v * 2 + c
+    far = jnp.where(c == 1, 3, 1)
+    near = jnp.where(c == 1, 1, 3)
+    count = 4 * pairs
+    for p in range(pairs):
+        x = own_ref[p].astype(F32)
+        table[p] = own_ref[p]
+        table[count + p] = swap_halves(x).astype(BF)
+        x = a_ref[p].astype(F32)
+        table[far * pairs + p] = a_ref[p]
+        table[count + far * pairs + p] = swap_halves(x).astype(BF)
+        x = la_ref[p].astype(F32)
+        table[near * pairs + p] = la_ref[p]
+        table[count + near * pairs + p] = swap_halves(x).astype(BF)
+        x = jnp.where(c == 1, b_ref[p].astype(F32), lb_ref[p].astype(F32))
+        table[2 * pairs + p] = x.astype(BF)
+        table[count + 2 * pairs + p] = swap_halves(x).astype(BF)
+    low = low_half((rank, 2 * rank))
+    lane = lax.broadcasted_iota(jnp.int32, (rank, 2 * rank), 1)
+    distance = jnp.where(c == 1, jnp.where(v == 1, 2, 3), jnp.where(v == 1, 1, 0))
+    home = z ^ distance
+    down = jnp.where(distance == 0, down_ref[...].astype(F32), got_ref[...].astype(F32))
+    for l in range(leaves):
+        lanes = []
+        for j in range(0, share, 2):
+            s0 = sources_ref[l, owner * share + j]
+            s1 = sources_ref[l, owner * share + j + 1]
+            at0 = ((s0 // leaves) ^ z) * pairs + ((s0 % leaves) >> 1)
+            at1 = ((s1 // leaves) ^ z) * pairs + ((s1 % leaves) >> 1)
+            first = table[(s0 & 1) * count + at0]
+            second = table[(1 - (s1 & 1)) * count + at1]
+            lanes.append(jnp.where(low, first, second))
+        part = dot(jnp.concatenate(lanes, axis=-1), blocks_ref[l].reshape(share * rank, rank))
+        parent = parents_ref[l]
+        begin = jnp.where((parent >> 1) == home, (parent & 1) * rank, -2 * rank)
+        pushed = jnp.where((lane >= begin) & (lane < begin + rank), down, 0.0).astype(BF)
+        weight = transfer_ref[l]
+        part = part + dot_t(pushed, jnp.concatenate([weight, weight], axis=-1))
+        total[:, l * panel:(l + 1) * panel] = near_ref[l] + dot(part.astype(BF), basis_ref[l])
+    rows = keep_ref.shape[1]
+    for w in range(2):
+        mine = pl.multiple_of((w * 2 + c) * rows, rows)
+        theirs = pl.multiple_of((w * 2 + 1 - c) * rows, rows)
+        keep_ref[w] = total[pl.ds(mine, rows), :]
+        send_ref[w] = total[pl.ds(theirs, rows), :].astype(BF)
+
+
+def merge_kernel(keep_ref, got_ref, send_ref, rest_ref):
+    v = lax.axis_index("vec")
+    send_ref[...] = (keep_ref[1 - v] + got_ref[1 - v].astype(F32)).astype(BF)
+    rest_ref[...] = keep_ref[v] + got_ref[v].astype(F32)
+
+
+def swap(x, route):
+    axes = ("leaf", "vec", "lvl")
+    zs, vs, cs = (lax.axis_size(a) for a in axes)
+    pairs = []
+    for z in range(zs):
+        for v in range(vs):
+            for c in range(cs):
+                target = route(z, v, c)
+                if target is not None:
+                    tz, tv, tc = target
+                    pairs.append(((z * vs + v) * cs + c, (tz * vs + tv) * cs + tc))
+    return lax.ppermute(x, axes, pairs)
+
+
+def on_device_paired(
+    adjoint_in,
+    row_basis,
+    col_basis,
+    row_transfer,
+    col_transfer,
+    parents,
+    far_sources,
+    far_blocks,
+    coarse_sources,
+    coarse_blocks,
+    near_sources,
+    near_blocks,
+):
+    vectors = adjoint_in.shape[0]
+    leaves, rank, panel = row_basis.shape
+    clusters = coarse_sources.shape[0] * 4
+    coarse_share = coarse_blocks.shape[1]
+    near_share = near_blocks.shape[1]
+    width = leaves * panel
+    params = pltpu.CompilerParams(vmem_limit_bytes=LIMIT)
+    wide = 2 * rank
+    messages = leaves // 2 + clusters // 2
+    msg, packed, edge = pl.pallas_call(
+        up_kernel,
+        out_shape=(
+            jax.ShapeDtypeStruct((messages, vectors, wide), BF),
+            jax.ShapeDtypeStruct((coarse_share, rank, wide), BF),
+            jax.ShapeDtypeStruct((vectors, REACH * panel), BF),
+        ),
+        in_specs=[VMEM] * 4 + [SMEM],
+        out_specs=(VMEM,) * 3,
+        scratch_shapes=[pltpu.VMEM((clusters, vectors, rank), F32)],
+        compiler_params=params,
+        name="up",
+    )(adjoint_in, row_basis, row_transfer, coarse_blocks, parents)
+
+    def other_core(z, v, c):
+        return z, v, 1 - c
+
+    def other_chip(z, v, c):
+        return z, 1 - v, c
+
+    a = swap(msg, lambda z, v, c: (z ^ (3 if c else 1), v, c))
+    b = swap(msg, lambda z, v, c: (z ^ 2, v, c) if c else None)
+
+    def neighbour(z, v, c):
+        target = z + 1 if (z + c) % 2 == 0 else z - 1
+        return (target, v, c) if 0 <= target < 4 else None
+
+    halo = swap(edge, neighbour)
+    halo_other = swap(halo, other_core)
+    p_lvl = swap(packed, other_core)
+    p_vec = swap(packed, other_chip)
+    p_diag = swap(p_vec, other_core)
+    near = pl.pallas_call(
+        near_kernel,
+        out_shape=jax.ShapeDtypeStruct((leaves, vectors, panel), F32),
+        in_specs=[SMEM] + [VMEM] * 3 + [ANY],
+        out_specs=VMEM,
+        scratch_shapes=[
+            pltpu.VMEM((leaves + 2 * REACH, vectors, panel), BF),
+            pltpu.VMEM((leaves, near_share, panel, panel), BF),
+            pltpu.SemaphoreType.DMA((leaves,)),
+        ],
+        compiler_params=params,
+        name="near",
+    )(near_sources, adjoint_in, halo, halo_other, near_blocks)
+    la = swap(a, other_core)
+    lb = swap(b, lambda z, v, c: (z, v, 0) if c else None)
+    down = pl.pallas_call(
+        coarse_kernel,
+        out_shape=jax.ShapeDtypeStruct((vectors, wide), BF),
+        in_specs=[SMEM] + [VMEM] * 9,
+        out_specs=VMEM,
+        scratch_shapes=[pltpu.VMEM((clusters, vectors, wide), BF)],
+        compiler_params=params,
+        name="coarse",
+    )(coarse_sources, msg, a, la, b, lb, packed, p_lvl, p_vec, p_diag)
+
+    def home(z, v, c):
+        distance = (2 if v else 3) if c else (1 if v else 0)
+        return (z ^ distance, v, c) if distance else None
+
+    got = swap(down, home)
+    rows = vectors // 4
+    send, keep = pl.pallas_call(
+        down_kernel,
+        out_shape=(
+            jax.ShapeDtypeStruct((2, rows, width), BF),
+            jax.ShapeDtypeStruct((2, rows, width), F32),
+        ),
+        in_specs=[SMEM] * 2 + [VMEM] * 11,
+        out_specs=(VMEM,) * 2,
+        scratch_shapes=[
+            pltpu.VMEM((4 * leaves, vectors, wide), BF),
+            pltpu.VMEM((vectors, width), F32),
+        ],
+        compiler_params=params,
+        name="down",
+    )(far_sources, parents, msg, a, la, b, lb, far_blocks, down, got, col_transfer, col_basis, near)
+    came = swap(send, other_core)
+    send, rest = pl.pallas_call(
+        merge_kernel,
+        out_shape=(
+            jax.ShapeDtypeStruct((rows, width), BF),
+            jax.ShapeDtypeStruct((rows, width), F32),
+        ),
+        in_specs=[VMEM] * 2,
+        out_specs=(VMEM,) * 2,
+        compiler_params=params,
+        name="merge",
+    )(keep, came)
+    came = swap(send, other_chip)
+    return (rest + came.astype(F32)).astype(BF)
 
 
 def solution(mesh):
@@ -121,6 +421,8 @@
         P(("groups", "leaf"), ("vec", "lvl"), None, None),
     )
     out_specs = P(("groups", "vec", "lvl"), "leaf")
+    sizes = tuple(mesh.shape[a] for a in ("leaf", "vec", "lvl"))
+    body = on_device_paired if sizes == (4, 2, 2) else on_device_general
     return jax.shard_map(
-        on_device, mesh=mesh, in_specs=in_specs, out_specs=out_specs, check_vma=False
-    )
+        body, mesh=mesh, in_specs=in_specs, out_specs=out_specs, check_vma=False
+    )

time: 122 us -> 49.2 us (0.40)
  blocking collectives: 53.7 us -> 0 us
  waiting for transfers between devices: 29.3 us -> 9.14 us
  starting transfers between devices: 2.67 us -> 21.5 us
  between operations: 13.3 us -> 0.18 us
  matrix products: 9.31 us -> 0 us
  Pallas kernels: 0 us -> 8.35 us
  other arithmetic: 2.79 us -> 0.65 us
  local copies, waits for them, and re-layouts: 10.4 us -> 9.07 us
    all_gather x2 -> x0, blocking collectives: 30.6 us -> none  [the longest x1 17.5 us: on_device(): shard_rows = lax.all_gather(leaf_up, 'leaf', axis=0, tiled=True)]
    reduce_scatter x2 -> x0, waiting for transfers between devices: 29.2 us -> none  [the longest x1 23 us: on_device(): lax.psum_scatter(near_part, ('vec', 'lvl'), scatter_dimension=0, tiled=True)]
    psum x1 -> x0, blocking collectives: 23.1 us -> none  [on_device(): cluster_up = lax.psum(partial_up, 'leaf').astype(jnp.bfloat16)]
    ppermute x2 -> x12, starting transfers between devices: 2.59 us -> 21.5 us  [swap(): return lax.ppermute(x, axes, pairs)]
    dot_general x7 -> x0, matrix products: 9.31 us -> none  [the longest x1 3.1 us: on_device(): jnp.einsum('kljp,ljpq->klq', near_rows, near_blocks, preferred_element_ty...]
    ppermute x2 -> x12, waiting for transfers between devices: 0.01 us -> 9.14 us  [swap(): return lax.ppermute(x, axes, pairs)]
    pallas_call x0 -> x5, Pallas kernels: none -> 8.35 us  [the longest x1 3.22 us: on_device_paired(): pl.pallas_call(near_kernel, out_shape=jax.ShapeDtypeStruct((leaves, vecto...]
    unnamed x19 -> x28, local copies, waits for them, and re-layouts: 3.33 us -> 9.07 us
  transfers between devices with their start and end apart: 5 -> 12, of which waited for: 2 -> 4; matrix products, arithmetic and copies ran while one was open for 11% -> 0% of each run, Pallas kernels for 0% -> 9%
where the time goes in v1:
time: 49.2 us; the launch traced here: 48.8 us
  starting transfers between devices  21.5 us (44%)
  waiting for transfers between devices  9.14 us (19%)
  local copies, waits for them, and re-layouts  9.07 us (18%)
  Pallas kernels  8.35 us (17%)
  other arithmetic  0.65 us (1%)
    ppermute x12, starting transfers between devices, swap(): return lax.ppermute(x, axes, pairs)  21.5 us
    ppermute x12, waiting for transfers between devices, swap(): return lax.ppermute(x, axes, pairs)  9.14 us
    unnamed x28, local copies, waits for them, and re-layouts  9.07 us
    pallas_call x1, Pallas kernels, on_device_paired(): pl.pallas_call(near_kernel, out_shape=jax.ShapeDtypeStruct((leaves, vecto...  3.22 us
    pallas_call x1, Pallas kernels, on_device_paired(): pl.pallas_call(down_kernel, out_shape=(jax.ShapeDtypeStruct((2, rows, wid...  2.64 us
    pallas_call x1, Pallas kernels, on_device_paired(): pl.pallas_call(up_kernel, out_shape=(jax.ShapeDtypeStruct((messages, vect...  1.48 us
  transfers between devices with their start and end apart: 12, of which 4 were waited for; matrix products, arithmetic and copies ran while one was open for 0% of the time, Pallas kernels for 9%

profile of v1, /device:TPU:0, one launch (start us, length us, event | category | flops | bytes accessed | tf_op | source)
XLA Modules:
  0.0 48.8 jit_solution(5193891282125553022)
XLA Ops:
  0.0 0.0 copy-start.1
  0.0 0.0 copy-start.2
  0.0 1.1 %copy-done.2 = bf16[64,2048]{1,0:T(8,128)(2,1)S(1)} copy-done((bf16[64,2048]{1,0:T(8,128)(2,1)S(1)}, bf16[64,2048]{1,0:T(8,128)(2,1)}, u32[]{:S(2)}) %copy-start.2) | copy-done | bytes 262168
  1.1 0.0 copy-start.4
  1.1 0.9 %copy-done.4 = bf16[8,64,256]{2,1,0:T(8,128)(2,1)S(1)} copy-done((bf16[8,64,256]{2,1,0:T(8,128)(2,1)S(1)}, bf16[8,64,256]{2,1,0:T(8,128)(2,1)}, u32[]{:S(2)}) %copy-start.4) | copy-done | bytes 262168
  2.1 0.9 %copy-done.5 = bf16[2,8,64,64]{3,2,1,0:T(8,128)(2,1)S(1)} copy-done((bf16[2,8,64,64]{3,2,1,0:T(8,128)(2,1)S(1)}, bf16[2,8,64,64]{3,2,1,0:T(8,128)(2,1)}, u32[]{:S(2)}) %copy-start.5) | copy-done | bytes 131096
  3.0 0.9 %copy-done.7 = bf16[8,64,64]{2,1,0:T(8,128)(2,1)S(1)} copy-done((bf16[8,64,64]{2,1,0:T(8,128)(2,1)S(1)}, bf16[8,64,64]{2,1,0:T(8,128)(2,1)}, u32[]{:S(2)}) %copy-start.7) | copy-done | bytes 65560
  3.9 0.7 %copy-done.11 = s32[8]{0:T(128)S(1)} copy-done((s32[8]{0:T(128)S(1)}, s32[8]{0:T(128)}, u32[]{:S(2)}) %copy-start.11) | copy-done | bytes 56
  4.6 1.5 %up.1 = (bf16[8,64,128]{2,1,0:T(8,128)(2,1)S(1)}, bf16[8,64,128]{2,1,0:T(8,128)(2,1)S(1)}, bf16[64,512]{1,0:T(8,128)(2,1)S(1)}) custom-call(bf16[64,2048]{1,0:T(8,128)(2,1)S(1)} %copy-done.2, bf16[8,64,256]{2,1,0:T(8,128)(2,1)S(1)} %copy-done.4, bf16[8,64,64]{2,1,0:T(8,128)(2,1)S(1)} %copy-done.7, bf16[2,8,64,64]{3,2,1,0:T(8,128)(2,1)S(1)} %copy-done.5, ...), custom_call_target="tpu_custom_call" | custom-call | tf_op jit(solution)/shard_map/up/pallas_call | solution.py:314
  6.1 3.0 %collective-permute-start.5 = (bf16[8,64,128]{2,1,0:T(8,128)(2,1)S(1)}, bf16[8,64,128]{2,1,0:T(8,128)(2,1)S(1)}, u32[]{:S(2)}, u32[]{:S(2)}) collective-permute-start(bf16[8,64,128]{2,1,0:T(8,128)(2,1)S(1)} %get-tuple-element.13.p_own), channel_id=1, source_target_pairs={{0,2},{1,3},{2,0},{3,1},{4,6},{5,7},{6,4},{7,5},{8,10},{9,11},{10,... | collective-permute-start | bytes 393224 | tf_op jit(solution)/shard_map/ppermute | solution.py:288
  9.1 0.7 %collective-permute-start.2 = (bf16[8,64,128]{2,1,0:T(8,128)(2,1)S(1)}, bf16[8,64,128]{2,1,0:T(8,128)(2,1)S(1)}, u32[]{:S(2)}, u32[]{:S(2)}) collective-permute-start(bf16[8,64,128]{2,1,0:T(8,128)(2,1)S(1)} %get-tuple-element.12.own_ref), channel_id=1, source_target_pairs={{1,9},{3,11},{5,13},{7,15},{9,1},{11,3},{13,5},{15,7},{17,25},{19,... | collective-permute-start | bytes 393224 | tf_op jit(solution)/shard_map/ppermute | solution.py:288
  9.7 1.6 %collective-permute-start = (bf16[8,64,128]{2,1,0:T(8,128)(2,1)S(1)}, bf16[8,64,128]{2,1,0:T(8,128)(2,1)S(1)}, u32[]{:S(2)}, u32[]{:S(2)}) collective-permute-start(bf16[8,64,128]{2,1,0:T(8,128)(2,1)S(1)} %get-tuple-element.12.own_ref), channel_id=1, source_target_pairs={{0,4},{1,13},{2,6},{3,15},{4,0},{5,9},{6,2},{7,11},{8,12},{9,5},{1... | collective-permute-start | bytes 393224 | tf_op jit(solution)/shard_map/ppermute | solution.py:288
  11.4 2.6 %collective-permute-start.4 = (bf16[8,64,128]{2,1,0:T(8,128)(2,1)S(1)}, bf16[8,64,128]{2,1,0:T(8,128)(2,1)S(1)}, u32[]{:S(2)}, u32[]{:S(2)}) collective-permute-start(bf16[8,64,128]{2,1,0:T(8,128)(2,1)S(1)} %get-tuple-element.13.p_own), channel_id=1, source_target_pairs={{0,1},{1,0},{2,3},{3,2},{4,5},{5,4},{6,7},{7,6},{8,9},{9,8},{10,11... | collective-permute-start | bytes 393224 | tf_op jit(solution)/shard_map/ppermute | solution.py:288
  14.0 0.0 collective-permute-done.5.p_vec
  14.0 0.0 collective-permute-start.6
  14.0 0.0 collective-permute-done.2.b_ref
  14.0 1.3 %collective-permute-start.3 = (bf16[8,64,128]{2,1,0:T(8,128)(2,1)S(1)}, bf16[8,64,128]{2,1,0:T(8,128)(2,1)S(1)}, u32[]{:S(2)}, u32[]{:S(2)}) collective-permute-start(bf16[8,64,128]{2,1,0:T(8,128)(2,1)S(1)} %collective-permute-done.2.b_ref), channel_id=1, source_target_pairs={{1,0},{3,2},{5,4},{7,6},{9,8},{11,10},{13,12},{15,14},{17,16},{19,... | collective-permute-start | bytes 393224 | tf_op jit(solution)/shard_map/ppermute | solution.py:288
  15.3 0.9 %collective-permute-done.a_ref = bf16[8,64,128]{2,1,0:T(8,128)(2,1)S(1)} collective-permute-done((bf16[8,64,128]{2,1,0:T(8,128)(2,1)S(1)}, bf16[8,64,128]{2,1,0:T(8,128)(2,1)S(1)}, u32[]{:S(2)}, u32[]{:S(2)}) %collective-permute-start) | collective-permute-done | bytes 131104 | tf_op jit(solution)/shard_map/ppermute | solution.py:288
  16.2 2.9 %collective-permute-start.1 = (bf16[8,64,128]{2,1,0:T(8,128)(2,1)S(1)}, bf16[8,64,128]{2,1,0:T(8,128)(2,1)S(1)}, u32[]{:S(2)}, u32[]{:S(2)}) collective-permute-start(bf16[8,64,128]{2,1,0:T(8,128)(2,1)S(1)} %collective-permute-done.a_ref), channel_id=1, source_target_pairs={{0,1},{1,0},{2,3},{3,2},{4,5},{5,4},{6,7},{7,6},{8,9},{9,8},{10,11... | collective-permute-start | bytes 393224 | tf_op jit(solution)/shard_map/ppermute | solution.py:288
  19.1 3.2 %collective-permute-start.8 = (bf16[64,512]{1,0:T(8,128)(2,1)S(1)}, bf16[64,512]{1,0:T(8,128)(2,1)S(1)}, u32[]{:S(2)}, u32[]{:S(2)}) collective-permute-start(bf16[64,512]{1,0:T(8,128)(2,1)S(1)} %get-tuple-element.14), channel_id=1, source_target_pairs={{0,4},{2,6},{4,0},{5,9},{6,2},{7,11},{8,12},{9,5},{10,14},{11,7},{... | collective-permute-start | bytes 196616 | tf_op jit(solution)/shard_map/ppermute | solution.py:288
  22.3 2.9 %collective-permute-done.8.mine_ref = bf16[64,512]{1,0:T(8,128)(2,1)S(1)} collective-permute-done((bf16[64,512]{1,0:T(8,128)(2,1)S(1)}, bf16[64,512]{1,0:T(8,128)(2,1)S(1)}, u32[]{:S(2)}, u32[]{:S(2)}) %collective-permute-start.8) | collective-permute-done | bytes 65568 | tf_op jit(solution)/shard_map/ppermute | solution.py:288
  25.2 0.0 collective-permute-start.9
  25.2 0.0 collective-permute-done.4.p_lvl
  25.2 0.0 collective-permute-done.6.p_diag
  25.3 0.0 collective-permute-done.3.lb_ref
  25.3 0.0 collective-permute-done.1.la_ref
  25.3 0.0 copy-start.13
  25.3 0.7 %copy-done.13 = s32[2,32]{1,0:T(2,128)S(1)} copy-done((s32[2,32]{1,0:T(2,128)S(1)}, s32[2,32]{1,0:T(2,128)}, u32[]{:S(2)}) %copy-start.13) | copy-done | bytes 280
  26.0 1.0 %coarse.1.down_ref = bf16[64,128]{1,0:T(8,128)(2,1)S(1)} custom-call(s32[2,32]{1,0:T(2,128)S(1)} %copy-done.13, bf16[8,64,128]{2,1,0:T(8,128)(2,1)S(1)} %get-tuple-element.12.own_ref, bf16[8,64,128]{2,1,0:T(8,128)(2,1)S(1)} %collective-permute-done.a_ref, bf16[8,64,128]{2,1,0:T(8,128)(2,1)S(1)} %collective-permute-done.1.la_ref, ...), custom_call_target="tpu_custom_call" | custom-call | tf_op jit(solution)/shard_map/coarse/pallas_call | solution.py:361
  26.9 0.7 %collective-permute-start.7 = (bf16[64,128]{1,0:T(8,128)(2,1)S(1)}, bf16[64,128]{1,0:T(8,128)(2,1)S(1)}, u32[]{:S(2)}, u32[]{:S(2)}) collective-permute-start(bf16[64,128]{1,0:T(8,128)(2,1)S(1)} %coarse.1.down_ref), channel_id=1, source_target_pairs={{1,13},{2,6},{3,11},{5,9},{6,2},{7,15},{9,5},{10,14},{11,3},{13,1}... | collective-permute-start | bytes 49160 | tf_op jit(solution)/shard_map/ppermute | solution.py:288
  27.6 0.0 collective-permute-done.9.other_ref
  27.6 0.0 copy-start
  27.6 2.2 %copy-done = bf16[8,4,256,256]{3,2,1,0:T(8,128)(2,1)S(1)} copy-done((bf16[8,4,256,256]{3,2,1,0:T(8,128)(2,1)S(1)}, bf16[8,4,256,256]{3,2,1,0:T(8,128)(2,1)}, u32[]{:S(2)}) %copy-start) | copy-done | bytes 4194328
  29.8 0.9 %copy-done.3 = bf16[64,2048]{1,0:T(8,128)(2,1)S(1)} copy-done((bf16[64,2048]{1,0:T(8,128)(2,1)S(1)}, bf16[64,2048]{1,0:T(8,128)(2,1)}, u32[]{:S(2)}) %copy-start.3) | copy-done | bytes 262168
  30.8 0.7 %copy-done.10 = s32[8,16]{1,0:T(8,128)S(1)} copy-done((s32[8,16]{1,0:T(8,128)S(1)}, s32[8,16]{1,0:T(8,128)}, u32[]{:S(2)}) %copy-start.10) | copy-done | bytes 536
  31.5 3.2 %near.1.near_ref = f32[8,64,256]{2,1,0:T(8,128)S(1)} custom-call(s32[8,16]{1,0:T(8,128)S(1)} %copy-done.10, bf16[64,2048]{1,0:T(8,128)(2,1)S(1)} %copy-done.3, bf16[64,512]{1,0:T(8,128)(2,1)S(1)} %collective-permute-done.8.mine_ref, bf16[64,512]{1,0:T(8,128)(2,1)S(1)} %collective-permute-done.9.other_ref, bf16[8,4,256,256]{3,2,1,0:T(8,128)(2,1)S(1)} %copy-done), custom_call_target="tpu_custom_call" | custom-call | tf_op jit(solution)/shard_map/near/pallas_call | solution.py:346
  34.7 0.0 collective-permute-done.7.got_ref
  34.7 0.0 copy-done.1
  34.7 0.0 copy-done.9
  34.7 0.0 copy-done.12
  34.7 0.0 copy-done.6
  34.7 0.0 copy-done.8
  34.7 2.6 %down.1 = (bf16[2,16,2048]{2,1,0:T(8,128)(2,1)S(1)}, f32[2,16,2048]{2,1,0:T(8,128)S(1)}) custom-call(s32[8,64]{1,0:T(8,128)S(1)} %copy-done.9, s32[8]{0:T(128)S(1)} %copy-done.12, bf16[8,64,128]{2,1,0:T(8,128)(2,1)S(1)} %get-tuple-element.12.own_ref, bf16[8,64,128]{2,1,0:T(8,128)(2,1)S(1)} %collective-permute-done.a_ref, ...), custom_call_target="tpu_custom_call" | custom-call | tf_op jit(solution)/shard_map/down/pallas_call | solution.py:377
  37.4 5.4 %collective-permute-start.10 = (bf16[2,16,2048]{2,1,0:T(8,128)(2,1)S(1)}, bf16[2,16,2048]{2,1,0:T(8,128)(2,1)S(1)}, u32[]{:S(2)}, u32[]{:S(2)}) collective-permute-start(bf16[2,16,2048]{2,1,0:T(8,128)(2,1)S(1)} %get-tuple-element.16), channel_id=1, source_target_pairs={{0,1},{1,0},{2,3},{3,2},{4,5},{5,4},{6,7},{7,6},{8,9},{9,8},{10,11... | collective-permute-start | bytes 393224 | tf_op jit(solution)/shard_map/ppermute | solution.py:288
  42.7 1.0 %collective-permute-done.10.got_ref = bf16[2,16,2048]{2,1,0:T(8,128)(2,1)S(1)} collective-permute-done((bf16[2,16,2048]{2,1,0:T(8,128)(2,1)S(1)}, bf16[2,16,2048]{2,1,0:T(8,128)(2,1)S(1)}, u32[]{:S(2)}, u32[]{:S(2)}) %collective-permute-start.10) | collective-permute-done | bytes 131104 | tf_op jit(solution)/shard_map/ppermute | solution.py:288
  43.8 0.1 collective-permute-start.11
  43.8 4.3 %collective-permute-done.11 = bf16[16,2048]{1,0:T(8,128)(2,1)S(1)} collective-permute-done((bf16[16,2048]{1,0:T(8,128)(2,1)S(1)}, bf16[16,2048]{1,0:T(8,128)(2,1)S(1)}, u32[]{:S(2)}, u32[]{:S(2)}) %collective-permute-start.11) | collective-permute-done | bytes 65568 | tf_op jit(solution)/shard_map/ppermute | solution.py:288
  48.2 0.6 %add_convert_fusion = bf16[16,2048]{1,0:T(8,128)(2,1)} fusion(f32[16,2048]{1,0:T(8,128)S(1)} %get-tuple-element.17, bf16[16,2048]{1,0:T(8,128)(2,1)S(1)} %collective-permute-done.11), kind=kLoop, calls=%fused_computation | loop fusion | flops 98304 | bytes 262144 | tf_op jit(solution)/shard_map/convert_element_type | solution.py:405
  (10 shorter events, 0.0 us)
Async XLA Ops:
  0.0 34.7 %copy-start.1 = (bf16[8,16,64,64]{3,2,1,0:T(8,128)(2,1)S(1)}, bf16[8,16,64,64]{3,2,1,0:T(8,128)(2,1)}, u32[]{:S(2)}) copy-start(bf16[8,16,64,64]{3,2,1,0:T(8,128)(2,1)} %blocks_ref.1) | copy-start | bytes 3145732
  0.0 1.1 %copy-start.2 = (bf16[64,2048]{1,0:T(8,128)(2,1)S(1)}, bf16[64,2048]{1,0:T(8,128)(2,1)}, u32[]{:S(2)}) copy-start(bf16[64,2048]{1,0:T(8,128)(2,1)} %x_ref.3) | copy-start | bytes 786436
  1.1 0.9 %copy-start.4 = (bf16[8,64,256]{2,1,0:T(8,128)(2,1)S(1)}, bf16[8,64,256]{2,1,0:T(8,128)(2,1)}, u32[]{:S(2)}) copy-start(bf16[8,64,256]{2,1,0:T(8,128)(2,1)} %basis_ref.2) | copy-start | bytes 786436
  2.1 0.9 %copy-start.5 = (bf16[2,8,64,64]{3,2,1,0:T(8,128)(2,1)S(1)}, bf16[2,8,64,64]{3,2,1,0:T(8,128)(2,1)}, u32[]{:S(2)}) copy-start(bf16[2,8,64,64]{3,2,1,0:T(8,128)(2,1)} %coarse_ref.1) | copy-start | bytes 393220
  3.0 0.9 %copy-start.7 = (bf16[8,64,64]{2,1,0:T(8,128)(2,1)S(1)}, bf16[8,64,64]{2,1,0:T(8,128)(2,1)}, u32[]{:S(2)}) copy-start(bf16[8,64,64]{2,1,0:T(8,128)(2,1)} %transfer_ref.2) | copy-start | bytes 196612
  3.9 0.7 %copy-start.11 = (s32[8]{0:T(128)S(1)}, s32[8]{0:T(128)}, u32[]{:S(2)}) copy-start(s32[8]{0:T(128)} %parents_ref.3) | copy-start | bytes 100
  4.6 30.1 %copy-start.9 = (s32[8,64]{1,0:T(8,128)S(1)}, s32[8,64]{1,0:T(8,128)}, u32[]{:S(2)}) copy-start(s32[8,64]{1,0:T(8,128)} %sources_ref.5) | copy-start | bytes 6148
  4.6 30.1 %copy-start.12 = (s32[8]{0:T(128)S(1)}, s32[8]{0:T(128)}, u32[]{:S(2)}) copy-start(s32[8]{0:T(128)} %parents_ref.3) | copy-start | bytes 100
  6.1 7.9 %collective-permute-start.5 = (bf16[8,64,128]{2,1,0:T(8,128)(2,1)S(1)}, bf16[8,64,128]{2,1,0:T(8,128)(2,1)S(1)}, u32[]{:S(2)}, u32[]{:S(2)}) collective-permute-start(bf16[8,64,128]{2,1,0:T(8,128)(2,1)S(1)} %get-tuple-element.13.p_own), channel_id=1, source_target_pairs={{0,2},{1,3},{2,0},{3,1},{4,6},{5,7},{6,4},{7,5},{8,10},{9,11},{10,... | collective-permute-start | bytes 393224 | tf_op jit(solution)/shard_map/ppermute | solution.py:288
  9.1 4.9 %collective-permute-start.2 = (bf16[8,64,128]{2,1,0:T(8,128)(2,1)S(1)}, bf16[8,64,128]{2,1,0:T(8,128)(2,1)S(1)}, u32[]{:S(2)}, u32[]{:S(2)}) collective-permute-start(bf16[8,64,128]{2,1,0:T(8,128)(2,1)S(1)} %get-tuple-element.12.own_ref), channel_id=1, source_target_pairs={{1,9},{3,11},{5,13},{7,15},{9,1},{11,3},{13,5},{15,7},{17,25},{19,... | collective-permute-start | bytes 393224 | tf_op jit(solution)/shard_map/ppermute | solution.py:288
  9.7 6.4 %collective-permute-start = (bf16[8,64,128]{2,1,0:T(8,128)(2,1)S(1)}, bf16[8,64,128]{2,1,0:T(8,128)(2,1)S(1)}, u32[]{:S(2)}, u32[]{:S(2)}) collective-permute-start(bf16[8,64,128]{2,1,0:T(8,128)(2,1)S(1)} %get-tuple-element.12.own_ref), channel_id=1, source_target_pairs={{0,4},{1,13},{2,6},{3,15},{4,0},{5,9},{6,2},{7,11},{8,12},{9,5},{1... | collective-permute-start | bytes 393224 | tf_op jit(solution)/shard_map/ppermute | solution.py:288
  11.4 13.9 %collective-permute-start.4 = (bf16[8,64,128]{2,1,0:T(8,128)(2,1)S(1)}, bf16[8,64,128]{2,1,0:T(8,128)(2,1)S(1)}, u32[]{:S(2)}, u32[]{:S(2)}) collective-permute-start(bf16[8,64,128]{2,1,0:T(8,128)(2,1)S(1)} %get-tuple-element.13.p_own), channel_id=1, source_target_pairs={{0,1},{1,0},{2,3},{3,2},{4,5},{5,4},{6,7},{7,6},{8,9},{9,8},{10,11... | collective-permute-start | bytes 393224 | tf_op jit(solution)/shard_map/ppermute | solution.py:288
  14.0 11.3 %collective-permute-start.6 = (bf16[8,64,128]{2,1,0:T(8,128)(2,1)S(1)}, bf16[8,64,128]{2,1,0:T(8,128)(2,1)S(1)}, u32[]{:S(2)}, u32[]{:S(2)}) collective-permute-start(bf16[8,64,128]{2,1,0:T(8,128)(2,1)S(1)} %collective-permute-done.5.p_vec), channel_id=1, source_target_pairs={{0,1},{1,0},{2,3},{3,2},{4,5},{5,4},{6,7},{7,6},{8,9},{9,8},{10,11... | collective-permute-start | bytes 393224 | tf_op jit(solution)/shard_map/ppermute | solution.py:288
  14.0 11.3 %collective-permute-start.3 = (bf16[8,64,128]{2,1,0:T(8,128)(2,1)S(1)}, bf16[8,64,128]{2,1,0:T(8,128)(2,1)S(1)}, u32[]{:S(2)}, u32[]{:S(2)}) collective-permute-start(bf16[8,64,128]{2,1,0:T(8,128)(2,1)S(1)} %collective-permute-done.2.b_ref), channel_id=1, source_target_pairs={{1,0},{3,2},{5,4},{7,6},{9,8},{11,10},{13,12},{15,14},{17,16},{19,... | collective-permute-start | bytes 393224 | tf_op jit(solution)/shard_map/ppermute | solution.py:288
  16.2 9.1 %collective-permute-start.1 = (bf16[8,64,128]{2,1,0:T(8,128)(2,1)S(1)}, bf16[8,64,128]{2,1,0:T(8,128)(2,1)S(1)}, u32[]{:S(2)}, u32[]{:S(2)}) collective-permute-start(bf16[8,64,128]{2,1,0:T(8,128)(2,1)S(1)} %collective-permute-done.a_ref), channel_id=1, source_target_pairs={{0,1},{1,0},{2,3},{3,2},{4,5},{5,4},{6,7},{7,6},{8,9},{9,8},{10,11... | collective-permute-start | bytes 393224 | tf_op jit(solution)/shard_map/ppermute | solution.py:288
  19.1 6.1 %collective-permute-start.8 = (bf16[64,512]{1,0:T(8,128)(2,1)S(1)}, bf16[64,512]{1,0:T(8,128)(2,1)S(1)}, u32[]{:S(2)}, u32[]{:S(2)}) collective-permute-start(bf16[64,512]{1,0:T(8,128)(2,1)S(1)} %get-tuple-element.14), channel_id=1, source_target_pairs={{0,4},{2,6},{4,0},{5,9},{6,2},{7,11},{8,12},{9,5},{10,14},{11,7},{... | collective-permute-start | bytes 196616 | tf_op jit(solution)/shard_map/ppermute | solution.py:288
  25.2 2.4 %collective-permute-start.9 = (bf16[64,512]{1,0:T(8,128)(2,1)S(1)}, bf16[64,512]{1,0:T(8,128)(2,1)S(1)}, u32[]{:S(2)}, u32[]{:S(2)}) collective-permute-start(bf16[64,512]{1,0:T(8,128)(2,1)S(1)} %collective-permute-done.8.mine_ref), channel_id=1, source_target_pairs={{0,1},{1,0},{2,3},{3,2},{4,5},{5,4},{6,7},{7,6},{8,9},{9,8},{10,11... | collective-permute-start | bytes 196616 | tf_op jit(solution)/shard_map/ppermute | solution.py:288
  25.3 0.7 %copy-start.13 = (s32[2,32]{1,0:T(2,128)S(1)}, s32[2,32]{1,0:T(2,128)}, u32[]{:S(2)}) copy-start(s32[2,32]{1,0:T(2,128)} %sources_ref.3) | copy-start | bytes 772
  26.9 7.7 %collective-permute-start.7 = (bf16[64,128]{1,0:T(8,128)(2,1)S(1)}, bf16[64,128]{1,0:T(8,128)(2,1)S(1)}, u32[]{:S(2)}, u32[]{:S(2)}) collective-permute-start(bf16[64,128]{1,0:T(8,128)(2,1)S(1)} %coarse.1.down_ref), channel_id=1, source_target_pairs={{1,13},{2,6},{3,11},{5,9},{6,2},{7,15},{9,5},{10,14},{11,3},{13,1}... | collective-permute-start | bytes 49160 | tf_op jit(solution)/shard_map/ppermute | solution.py:288
  27.6 2.2 %copy-start = (bf16[8,4,256,256]{3,2,1,0:T(8,128)(2,1)S(1)}, bf16[8,4,256,256]{3,2,1,0:T(8,128)(2,1)}, u32[]{:S(2)}) copy-start(bf16[8,4,256,256]{3,2,1,0:T(8,128)(2,1)} %blocks_hbm.1) | copy-start | bytes 12582916
  29.8 0.9 %copy-start.3 = (bf16[64,2048]{1,0:T(8,128)(2,1)S(1)}, bf16[64,2048]{1,0:T(8,128)(2,1)}, u32[]{:S(2)}) copy-start(bf16[64,2048]{1,0:T(8,128)(2,1)} %x_ref.3) | copy-start | bytes 786436
  30.8 0.7 %copy-start.10 = (s32[8,16]{1,0:T(8,128)S(1)}, s32[8,16]{1,0:T(8,128)}, u32[]{:S(2)}) copy-start(s32[8,16]{1,0:T(8,128)} %sources_ref.4) | copy-start | bytes 1540
  31.5 3.3 %copy-start.6 = (bf16[8,64,256]{2,1,0:T(8,128)(2,1)S(1)}, bf16[8,64,256]{2,1,0:T(8,128)(2,1)}, u32[]{:S(2)}) copy-start(bf16[8,64,256]{2,1,0:T(8,128)(2,1)} %basis_ref.3) | copy-start | bytes 786436
  31.5 3.3 %copy-start.8 = (bf16[8,64,64]{2,1,0:T(8,128)(2,1)S(1)}, bf16[8,64,64]{2,1,0:T(8,128)(2,1)}, u32[]{:S(2)}) copy-start(bf16[8,64,64]{2,1,0:T(8,128)(2,1)} %transfer_ref.3) | copy-start | bytes 196612
  37.4 6.3 %collective-permute-start.10 = (bf16[2,16,2048]{2,1,0:T(8,128)(2,1)S(1)}, bf16[2,16,2048]{2,1,0:T(8,128)(2,1)S(1)}, u32[]{:S(2)}, u32[]{:S(2)}) collective-permute-start(bf16[2,16,2048]{2,1,0:T(8,128)(2,1)S(1)} %get-tuple-element.16), channel_id=1, source_target_pairs={{0,1},{1,0},{2,3},{3,2},{4,5},{5,4},{6,7},{7,6},{8,9},{9,8},{10,11... | collective-permute-start | bytes 393224 | tf_op jit(solution)/shard_map/ppermute | solution.py:288
  43.8 4.4 %collective-permute-start.11 = (bf16[16,2048]{1,0:T(8,128)(2,1)S(1)}, bf16[16,2048]{1,0:T(8,128)(2,1)S(1)}, u32[]{:S(2)}, u32[]{:S(2)}) collective-permute-start(bf16[16,2048]{1,0:T(8,128)(2,1)S(1)} %get-tuple-element.18), channel_id=1, source_target_pairs={{0,2},{1,3},{2,0},{3,1},{4,6},{5,7},{6,4},{7,5},{8,10},{9,11},{10,... | collective-permute-start | bytes 196616 | tf_op jit(solution)/shard_map/ppermute | solution.py:288

commit v2 on v1

--- a/solution.py
+++ b/solution.py
@@ -1,5 +1,3 @@
-import functools
-
 import jax
 import jax.numpy as jnp
 from jax import lax
@@ -12,8 +10,12 @@
 F32 = jnp.float32
 VMEM = pl.BlockSpec(memory_space=pltpu.VMEM)
 SMEM = pl.BlockSpec(memory_space=pltpu.SMEM)
-ANY = pl.BlockSpec(memory_space=pl.ANY)
-LIMIT = 48 << 20
+HBM = pl.BlockSpec(memory_space=pltpu.HBM)
+LIMIT = 32 << 20
+
+
+def cost(us):
+    return pl.CostEstimate(flops=int(us * 1e9), bytes_accessed=1024, transcendentals=0)
 
 
 def dot(a, b):
@@ -129,76 +131,95 @@
     return (far_out + near_sum).astype(jnp.bfloat16)
 
 
-def up_kernel(x_ref, basis_ref, transfer_ref, coarse_ref, parents_ref,
-              msg_ref, packed_ref, edge_ref, sums):
-    leaves, rank, panel = basis_ref.shape
-    z, c = lax.axis_index("leaf"), lax.axis_index("lvl")
-    width = REACH * panel
-    start = jnp.where((z + c) % 2 == 0, leaves * panel - width, 0)
-    edge_ref[...] = x_ref[:, pl.ds(pl.multiple_of(start, 128), width)]
-    share = coarse_ref.shape[1]
-    for j in range(share):
-        packed_ref[j] = jnp.concatenate([coarse_ref[0, j], coarse_ref[1, j]], axis=-1)
-    sums[...] = jnp.zeros_like(sums)
-    ups = []
-    for l in range(leaves):
-        up = dot_t(x_ref[:, l * panel:(l + 1) * panel], basis_ref[l]).astype(BF)
-        ups.append(up)
-        parent = parents_ref[l]
-        sums[parent] = sums[parent] + dot(up, transfer_ref[l])
-    for p in range(leaves // 2):
-        msg_ref[p] = jnp.concatenate([ups[2 * p], ups[2 * p + 1]], axis=-1)
-    for p in range(sums.shape[0] // 2):
-        msg_ref[leaves // 2 + p] = jnp.concatenate(
-            [sums[2 * p], sums[2 * p + 1]], axis=-1
-        ).astype(BF)
-
-
-def near_kernel(sources_ref, x_ref, mine_ref, other_ref, blocks_hbm, out_ref,
-                table, blocks, sems):
-    leaves, share, panel = blocks.shape[0], blocks.shape[1], blocks.shape[2]
-    z, c = lax.axis_index("leaf"), lax.axis_index("lvl")
-    owner = lax.axis_index("vec") * 2 + c
+def up_kernel(x_hbm, basis_hbm, transfer_hbm, parents_hbm, msg_ref, short_ref,
+              x_ref, basis_ref, transfer_ref, parents_ref, sums, sems):
     copies = [
-        pltpu.make_async_copy(blocks_hbm.at[l], blocks.at[l], sems.at[l]) for l in range(leaves)
+        pltpu.make_async_copy(a, b, sems.at[i])
+        for i, (a, b) in enumerate((
+            (x_hbm, x_ref),
+            (basis_hbm, basis_ref),
+            (parents_hbm, parents_ref),
+            (transfer_hbm, transfer_ref),
+        ))
     ]
     for copy in copies:
         copy.start()
+    sums[...] = jnp.zeros_like(sums)
+    leaves, rank, panel = basis_ref.shape
+    z, c = lax.axis_index("leaf"), lax.axis_index("lvl")
+    pairs = leaves // 2
+    clusters = sums.shape[0]
+    copies[0].wait()
+    start = jnp.where((z + c) % 2 == 0, (leaves - REACH) * panel, 0)
+    base = pairs + clusters // 2
+    for i in range(REACH * panel // (2 * rank)):
+        at = pl.multiple_of(start + i * 2 * rank, 2 * rank)
+        msg_ref[base + i] = x_ref[:, pl.ds(at, 2 * rank)]
+    copies[1].wait()
+    ups = [
+        dot_t(x_ref[:, l * panel:(l + 1) * panel], basis_ref[l]).astype(BF)
+        for l in range(leaves)
+    ]
+    for p in range(pairs):
+        msg_ref[p] = short_ref[p] = jnp.concatenate([ups[2 * p], ups[2 * p + 1]], axis=-1)
+    copies[2].wait()
+    copies[3].wait()
+    for l in range(leaves):
+        parent = parents_ref[l]
+        sums[parent] = sums[parent] + dot(ups[l], transfer_ref[l])
+    for p in range(clusters // 2):
+        merged = jnp.concatenate([sums[2 * p], sums[2 * p + 1]], axis=-1).astype(BF)
+        msg_ref[pairs + p] = short_ref[pairs + p] = merged
+
+
+def near_kernel(sources_hbm, x_ref, a_ref, la_ref, blocks_ref, out_ref, sources_ref, table, sem):
+    copy = pltpu.make_async_copy(sources_hbm, sources_ref, sem)
+    copy.start()
+    leaves, share, panel, _ = blocks_ref.shape
+    z, c = lax.axis_index("leaf"), lax.axis_index("lvl")
+    owner = lax.axis_index("vec") * 2 + c
+    high = (z + c) % 2 == 0
+    top, bottom = leaves + REACH, 0
+    at_a = jnp.where(high, top, bottom)
+    at_la = jnp.where(high, bottom, top)
+    lanes = a_ref.shape[2]
+    parts = panel // lanes
+    base = a_ref.shape[0] - REACH * parts
+    for i in range(REACH):
+        for w in range(parts):
+            table[at_a + i, :, w * lanes:(w + 1) * lanes] = a_ref[base + i * parts + w]
+            table[at_la + i, :, w * lanes:(w + 1) * lanes] = la_ref[base + i * parts + w]
     for l in range(leaves):
         table[REACH + l] = x_ref[:, l * panel:(l + 1) * panel]
-    high = (z + c) % 2 == 0
-    top, bottom = leaves + REACH, 0
-    at_mine = jnp.where(high, top, bottom)
-    at_other = jnp.where(high, bottom, top)
-    for i in range(REACH):
-        table[at_mine + i] = mine_ref[:, i * panel:(i + 1) * panel]
-        table[at_other + i] = other_ref[:, i * panel:(i + 1) * panel]
+    copy.wait()
     for l in range(leaves):
         rows = [
             table[sources_ref[l, owner * share + j] - z * leaves + REACH] for j in range(share)
         ]
-        copies[l].wait()
-        out_ref[l] = dot(jnp.concatenate(rows, axis=-1), blocks[l].reshape(share * panel, panel))
-
-
-def coarse_kernel(sources_ref, own_ref, a_ref, la_ref, b_ref, lb_ref,
-                  p_own, p_lvl, p_vec, p_diag, out_ref, table):
-    pairs = own_ref.shape[0] // 2
-    share = p_own.shape[0]
+        out_ref[l] = dot(
+            jnp.concatenate(rows, axis=-1), blocks_ref[l].reshape(share * panel, panel)
+        )
+
+
+def coarse_kernel(sources_hbm, own_ref, a_ref, la_ref, b_ref, lb_ref,
+                  p_own, p_lvl, p_vec, p_diag, out_ref, sources_ref, table, sem):
+    copy = pltpu.make_async_copy(sources_hbm, sources_ref, sem)
+    copy.start()
+    _, share, rank, _ = p_own.shape
+    pairs = table.shape[0] // 2
     c = lax.axis_index("lvl")
     me = lax.axis_index("vec") * 2 + c
-    rank = own_ref.shape[1]
     for p in range(pairs):
         q = pairs + p
         across = jnp.where(c == 1, b_ref[q].astype(F32), lb_ref[q].astype(F32))
         total = (own_ref[q].astype(F32) + a_ref[q].astype(F32)) + (la_ref[q].astype(F32) + across)
         table[p] = total.astype(BF)
         table[pairs + p] = swap_halves(total).astype(BF)
-    low = low_half((rank, 2 * rank))
-    acc = jnp.zeros((2 * rank, 2 * rank), F32)
-    for flip, blocks in ((0, p_own), (1, p_lvl), (2, p_vec), (3, p_diag)):
+    low = low_half((out_ref.shape[0], 2 * rank))
+    accs = [jnp.zeros((out_ref.shape[0], rank), F32) for _ in range(2)]
+    copy.wait()
+    for flip, blocks in enumerate((p_own, p_lvl, p_vec, p_diag)):
         base = (me ^ flip) * share
-        rows = []
         for cluster in range(2):
             lanes = []
             for j in range(0, share, 2):
@@ -207,16 +228,24 @@
                 first = table[(s0 & 1) * pairs + (s0 >> 1)]
                 second = table[(1 - (s1 & 1)) * pairs + (s1 >> 1)]
                 lanes.append(jnp.where(low, first, second))
-            rows.append(jnp.concatenate(lanes, axis=-1))
-        acc = acc + dot(
-            jnp.concatenate(rows, axis=0), blocks[...].reshape(share * rank, 2 * rank)
-        )
-    out_ref[...] = jnp.where(low, acc[:rank], acc[rank:]).astype(BF)
-
-
-def down_kernel(sources_ref, parents_ref, own_ref, a_ref, la_ref, b_ref, lb_ref,
+            accs[cluster] = accs[cluster] + dot(
+                jnp.concatenate(lanes, axis=-1), blocks[cluster].reshape(share * rank, rank)
+            )
+    out_ref[...] = jnp.concatenate(accs, axis=-1).astype(BF)
+
+
+def down_kernel(sources_hbm, parents_hbm, own_ref, a_ref, la_ref, b_ref, lb_ref,
                 blocks_ref, down_ref, got_ref, transfer_ref, basis_ref, near_ref,
-                send_ref, keep_ref, table, total):
+                send_ref, keep_ref, sources_ref, parents_ref, table, total, sems):
+    copies = [
+        pltpu.make_async_copy(a, b, sems.at[i])
+        for i, (a, b) in enumerate((
+            (sources_hbm, sources_ref),
+            (parents_hbm, parents_ref),
+        ))
+    ]
+    for copy in copies:
+        copy.start()
     leaves, share, rank, _ = blocks_ref.shape
     panel = basis_ref.shape[2]
     pairs = leaves // 2
@@ -238,11 +267,13 @@
         x = jnp.where(c == 1, b_ref[p].astype(F32), lb_ref[p].astype(F32))
         table[2 * pairs + p] = x.astype(BF)
         table[count + 2 * pairs + p] = swap_halves(x).astype(BF)
-    low = low_half((rank, 2 * rank))
-    lane = lax.broadcasted_iota(jnp.int32, (rank, 2 * rank), 1)
+    low = low_half((own_ref.shape[1], 2 * rank))
+    lane = lax.broadcasted_iota(jnp.int32, low.shape, 1)
     distance = jnp.where(c == 1, jnp.where(v == 1, 2, 3), jnp.where(v == 1, 1, 0))
     home = z ^ distance
     down = jnp.where(distance == 0, down_ref[...].astype(F32), got_ref[...].astype(F32))
+    for copy in copies:
+        copy.wait()
     for l in range(leaves):
         lanes = []
         for j in range(0, share, 2):
@@ -274,6 +305,10 @@
     rest_ref[...] = keep_ref[v] + got_ref[v].astype(F32)
 
 
+def in_hbm(*arrays):
+    return [pltpu.with_memory_space_constraint(x, pltpu.HBM) for x in arrays]
+
+
 def swap(x, route):
     axes = ("leaf", "vec", "lvl")
     zs, vs, cs = (lax.axis_size(a) for a in axes)
@@ -306,67 +341,73 @@
     leaves, rank, panel = row_basis.shape
     clusters = coarse_sources.shape[0] * 4
     coarse_share = coarse_blocks.shape[1]
-    near_share = near_blocks.shape[1]
     width = leaves * panel
     params = pltpu.CompilerParams(vmem_limit_bytes=LIMIT)
     wide = 2 * rank
-    messages = leaves // 2 + clusters // 2
-    msg, packed, edge = pl.pallas_call(
+    messages = leaves // 2 + clusters // 2 + REACH * panel // wide
+
+    def other_core(z, v, c):
+        return z, v, 1 - c
+
+    def other_chip(z, v, c):
+        return z, 1 - v, c
+
+    p_lvl = swap(coarse_blocks, other_core)
+    p_vec = swap(coarse_blocks, other_chip)
+    msg, short = pl.pallas_call(
         up_kernel,
         out_shape=(
             jax.ShapeDtypeStruct((messages, vectors, wide), BF),
-            jax.ShapeDtypeStruct((coarse_share, rank, wide), BF),
-            jax.ShapeDtypeStruct((vectors, REACH * panel), BF),
+            jax.ShapeDtypeStruct((leaves // 2 + clusters // 2, vectors, wide), BF),
         ),
-        in_specs=[VMEM] * 4 + [SMEM],
-        out_specs=(VMEM,) * 3,
-        scratch_shapes=[pltpu.VMEM((clusters, vectors, rank), F32)],
+        in_specs=[HBM] * 4,
+        out_specs=(VMEM,) * 2,
+        scratch_shapes=[
+            pltpu.VMEM(adjoint_in.shape, BF),
+            pltpu.VMEM(row_basis.shape, BF),
+            pltpu.VMEM(row_transfer.shape, BF),
+            pltpu.SMEM(parents.shape, jnp.int32),
+            pltpu.VMEM((clusters, vectors, rank), F32),
+            pltpu.SemaphoreType.DMA((4,)),
+        ],
         compiler_params=params,
+        cost_estimate=cost(1.5),
         name="up",
-    )(adjoint_in, row_basis, row_transfer, coarse_blocks, parents)
-
-    def other_core(z, v, c):
-        return z, v, 1 - c
-
-    def other_chip(z, v, c):
-        return z, 1 - v, c
-
+    )(*in_hbm(adjoint_in, row_basis, row_transfer, parents))
     a = swap(msg, lambda z, v, c: (z ^ (3 if c else 1), v, c))
-    b = swap(msg, lambda z, v, c: (z ^ 2, v, c) if c else None)
-
-    def neighbour(z, v, c):
-        target = z + 1 if (z + c) % 2 == 0 else z - 1
-        return (target, v, c) if 0 <= target < 4 else None
-
-    halo = swap(edge, neighbour)
-    halo_other = swap(halo, other_core)
-    p_lvl = swap(packed, other_core)
-    p_vec = swap(packed, other_chip)
+    b = swap(short, lambda z, v, c: (z ^ 2, v, c) if c else None)
     p_diag = swap(p_vec, other_core)
+    la = swap(a, other_core)
     near = pl.pallas_call(
         near_kernel,
         out_shape=jax.ShapeDtypeStruct((leaves, vectors, panel), F32),
-        in_specs=[SMEM] + [VMEM] * 3 + [ANY],
+        in_specs=[HBM] + [VMEM] * 4,
         out_specs=VMEM,
         scratch_shapes=[
+            pltpu.SMEM(near_sources.shape, jnp.int32),
             pltpu.VMEM((leaves + 2 * REACH, vectors, panel), BF),
-            pltpu.VMEM((leaves, near_share, panel, panel), BF),
-            pltpu.SemaphoreType.DMA((leaves,)),
+            pltpu.SemaphoreType.DMA(()),
         ],
         compiler_params=params,
+        cost_estimate=cost(2.5),
         name="near",
-    )(near_sources, adjoint_in, halo, halo_other, near_blocks)
-    la = swap(a, other_core)
+    )(*in_hbm(near_sources), adjoint_in, a, la, near_blocks)
+    b, near = lax.optimization_barrier((b, near))
     lb = swap(b, lambda z, v, c: (z, v, 0) if c else None)
     down = pl.pallas_call(
         coarse_kernel,
         out_shape=jax.ShapeDtypeStruct((vectors, wide), BF),
-        in_specs=[SMEM] + [VMEM] * 9,
+        in_specs=[HBM] + [VMEM] * 9,
         out_specs=VMEM,
-        scratch_shapes=[pltpu.VMEM((clusters, vectors, wide), BF)],
+        scratch_shapes=[
+            pltpu.SMEM(coarse_sources.shape, jnp.int32),
+            pltpu.VMEM((clusters, vectors, wide), BF),
+            pltpu.SemaphoreType.DMA(()),
+        ],
         compiler_params=params,
+        cost_estimate=cost(1.0),
         name="coarse",
-    )(coarse_sources, msg, a, la, b, lb, packed, p_lvl, p_vec, p_diag)
+    )(*in_hbm(coarse_sources), msg, a, la, b, lb, coarse_blocks, p_lvl, p_vec, p_diag)
 
     def home(z, v, c):
         distance = (2 if v else 3) if c else (1 if v else 0)
@@ -380,15 +421,19 @@
             jax.ShapeDtypeStruct((2, rows, width), BF),
             jax.ShapeDtypeStruct((2, rows, width), F32),
         ),
-        in_specs=[SMEM] * 2 + [VMEM] * 11,
+        in_specs=[HBM] * 2 + [VMEM] * 11,
         out_specs=(VMEM,) * 2,
         scratch_shapes=[
+            pltpu.SMEM(far_sources.shape, jnp.int32),
+            pltpu.SMEM(parents.shape, jnp.int32),
             pltpu.VMEM((4 * leaves, vectors, wide), BF),
             pltpu.VMEM((vectors, width), F32),
+            pltpu.SemaphoreType.DMA((2,)),
         ],
         compiler_params=params,
+        cost_estimate=cost(2.5),
         name="down",
-    )(far_sources, parents, msg, a, la, b, lb, far_blocks, down, got, col_transfer, col_basis, near)
+    )(*in_hbm(far_sources, parents), msg, a, la, b, lb, far_blocks, down, got, col_transfer, col_basis, near)
     came = swap(send, other_core)
     send, rest = pl.pallas_call(
         merge_kernel,
@@ -399,6 +444,7 @@
         in_specs=[VMEM] * 2,
         out_specs=(VMEM,) * 2,
         compiler_params=params,
+        cost_estimate=cost(0.6),
         name="merge",
     )(keep, came)
     came = swap(send, other_chip)

time: 49.2 us -> 41.5 us (0.84)
  local copies, waits for them, and re-layouts: 9.07 us -> 0.02 us
  waiting for transfers between devices: 9.14 us -> 18 us
  starting transfers between devices: 21.5 us -> 15.2 us
  Pallas kernels: 8.35 us -> 7.3 us
    unnamed x28 -> x12, local copies, waits for them, and re-layouts: 9.07 us -> 0.02 us
    ppermute x12 -> x10, waiting for transfers between devices: 9.14 us -> 18 us  [swap(): return lax.ppermute(x, axes, pairs)]
    ppermute x12 -> x10, starting transfers between devices: 21.5 us -> 15.2 us  [swap(): return lax.ppermute(x, axes, pairs)]
    pallas_call x1, Pallas kernels: 3.22 us -> 1.59 us  [on_device_paired(): pl.pallas_call(near_kernel, out_shape=jax.ShapeDtypeStruct((leaves, vecto...]
  transfers between devices with their start and end apart: 12 -> 10, of which waited for: 4 -> 5; matrix products, arithmetic and copies ran while one was open for 0% -> 0% of each run, Pallas kernels for 9% -> 4%
where the time goes in v2:
time: 41.5 us; the launch traced here: 41.3 us
  waiting for transfers between devices  18 us (43%)
  starting transfers between devices  15.2 us (37%)
  Pallas kernels  7.3 us (18%)
  other arithmetic  0.64 us (2%)
    ppermute x10, waiting for transfers between devices, swap(): return lax.ppermute(x, axes, pairs)  18 us
    ppermute x10, starting transfers between devices, swap(): return lax.ppermute(x, axes, pairs)  15.2 us
    pallas_call x1, Pallas kernels, on_device_paired(): pl.pallas_call(down_kernel, out_shape=(jax.ShapeDtypeStruct((2, rows, wid...  2.68 us
    pallas_call x1, Pallas kernels, on_device_paired(): pl.pallas_call(up_kernel, out_shape=(jax.ShapeDtypeStruct((messages, vect...  1.79 us
    pallas_call x1, Pallas kernels, on_device_paired(): pl.pallas_call(near_kernel, out_shape=jax.ShapeDtypeStruct((leaves, vecto...  1.59 us
    pallas_call x1, Pallas kernels, on_device_paired(): pl.pallas_call(coarse_kernel, out_shape=jax.ShapeDtypeStruct((vectors, wi...  1.22 us
  transfers between devices with their start and end apart: 10, of which 5 were waited for; matrix products, arithmetic and copies ran while one was open for 0% of the time, Pallas kernels for 4%

profile of v2, /device:TPU:0, one launch (start us, length us, event | category | flops | bytes accessed | tf_op | source)
XLA Modules:
  0.0 41.3 jit_solution(12604854084986041562)
XLA Ops:
  0.0 0.0 copy-start.2
  0.0 0.0 copy-start.3
  0.0 0.0 copy-start
  0.0 1.8 %up.1 = (bf16[12,64,128]{2,1,0:T(8,128)(2,1)S(1)}, bf16[8,64,128]{2,1,0:T(8,128)(2,1)S(1)}) custom-call(bf16[64,2048]{1,0:T(8,128)(2,1)} %x_ref.1, bf16[8,64,256]{2,1,0:T(8,128)(2,1)} %basis_hbm.1, bf16[8,64,64]{2,1,0:T(8,128)(2,1)} %transfer_hbm.1, s32[8]{0:T(128)} %parents_hbm.3), custom_call_target="tpu_custom_call" | custom-call | flops 1500000000 | bytes 1024 | tf_op jit(solution)/shard_map/up/pallas_call | solution.py:357
  1.8 3.1 %collective-permute-start = (bf16[12,64,128]{2,1,0:T(8,128)(2,1)S(1)}, bf16[12,64,128]{2,1,0:T(8,128)(2,1)S(1)}, u32[]{:S(2)}, u32[]{:S(2)}) collective-permute-start(bf16[12,64,128]{2,1,0:T(8,128)(2,1)S(1)} %get-tuple-element.13.own_ref), channel_id=1, source_target_pairs={{0,4},{1,13},{2,6},{3,15},{4,0},{5,9},{6,2},{7,11},{8,12},{9,5},{1... | collective-permute-start | bytes 589832 | tf_op jit(solution)/shard_map/ppermute | solution.py:323
  4.9 5.8 %collective-permute-done.a_ref = bf16[12,64,128]{2,1,0:T(8,128)(2,1)S(1)} collective-permute-done((bf16[12,64,128]{2,1,0:T(8,128)(2,1)S(1)}, bf16[12,64,128]{2,1,0:T(8,128)(2,1)S(1)}, u32[]{:S(2)}, u32[]{:S(2)}) %collective-permute-start) | collective-permute-done | bytes 196640 | tf_op jit(solution)/shard_map/ppermute | solution.py:323
  10.7 0.0 collective-permute-start.1
  10.7 0.0 copy-done.3
  10.7 1.9 %collective-permute-start.5 = (bf16[2,8,64,64]{3,2,1,0:T(8,128)(2,1)S(1)}, bf16[2,8,64,64]{3,2,1,0:T(8,128)(2,1)S(1)}, u32[]{:S(2)}, u32[]{:S(2)}) collective-permute-start(bf16[2,8,64,64]{3,2,1,0:T(8,128)(2,1)S(1)} %copy-done.3), channel_id=1, source_target_pairs={{0,2},{1,3},{2,0},{3,1},{4,6},{5,7},{6,4},{7,5},{8,10},{9,11},{10,... | collective-permute-start | bytes 393224 | tf_op jit(solution)/shard_map/ppermute | solution.py:323
  12.6 0.2 collective-permute-start.4
  12.8 0.0 copy-start.1
  12.8 0.0 copy-start.4
  12.8 0.0 copy-start.5
  12.8 0.8 %collective-permute-start.2 = (bf16[8,64,128]{2,1,0:T(8,128)(2,1)S(1)}, bf16[8,64,128]{2,1,0:T(8,128)(2,1)S(1)}, u32[]{:S(2)}, u32[]{:S(2)}) collective-permute-start(bf16[8,64,128]{2,1,0:T(8,128)(2,1)S(1)} %get-tuple-element.14), channel_id=1, source_target_pairs={{1,9},{3,11},{5,13},{7,15},{9,1},{11,3},{13,5},{15,7},{17,25},{19,... | collective-permute-start | bytes 393224 | tf_op jit(solution)/shard_map/ppermute | solution.py:323
  13.6 5.9 %collective-permute-done.5.p_vec = bf16[2,8,64,64]{3,2,1,0:T(8,128)(2,1)S(1)} collective-permute-done((bf16[2,8,64,64]{3,2,1,0:T(8,128)(2,1)S(1)}, bf16[2,8,64,64]{3,2,1,0:T(8,128)(2,1)S(1)}, u32[]{:S(2)}, u32[]{:S(2)}) %collective-permute-start.5) | collective-permute-done | bytes 131104 | tf_op jit(solution)/shard_map/ppermute | solution.py:323
  19.6 0.0 collective-permute-start.6
  19.6 0.0 collective-permute-done.1.la_ref
  19.6 0.0 copy-done.2
  19.6 0.0 copy-done
  19.6 1.6 %near.1.near_ref = f32[8,64,256]{2,1,0:T(8,128)S(1)} custom-call(s32[8,16]{1,0:T(8,128)} %sources_hbm.3, bf16[64,2048]{1,0:T(8,128)(2,1)S(1)} %copy-done.2, bf16[12,64,128]{2,1,0:T(8,128)(2,1)S(1)} %collective-permute-done.a_ref, bf16[12,64,128]{2,1,0:T(8,128)(2,1)S(1)} %collective-permute-done.1.la_ref, bf16[8,4,256,256]{3,2,1,0:T(8,128)(2,1)S(1)} %copy-done), custom_call_target="tpu_custom_call" | custom-call | flops 2500000000 | bytes 1024 | tf_op jit(solution)/shard_map/near/pallas_call | solution.py:381
  21.2 0.0 collective-permute-done.2.b_ref
  21.2 1.3 %collective-permute-start.3 = (bf16[8,64,128]{2,1,0:T(8,128)(2,1)S(1)}, bf16[8,64,128]{2,1,0:T(8,128)(2,1)S(1)}, u32[]{:S(2)}, u32[]{:S(2)}) collective-permute-start(bf16[8,64,128]{2,1,0:T(8,128)(2,1)S(1)} %collective-permute-done.2.b_ref), channel_id=1, source_target_pairs={{1,0},{3,2},{5,4},{7,6},{9,8},{11,10},{13,12},{15,14},{17,16},{19,... | collective-permute-start | bytes 393224 | tf_op jit(solution)/shard_map/ppermute | solution.py:323
  22.5 0.0 collective-permute-done.4.p_lvl
  22.5 0.0 collective-permute-done.6.p_diag
  22.5 1.9 %collective-permute-done.3.lb_ref = bf16[8,64,128]{2,1,0:T(8,128)(2,1)S(1)} collective-permute-done((bf16[8,64,128]{2,1,0:T(8,128)(2,1)S(1)}, bf16[8,64,128]{2,1,0:T(8,128)(2,1)S(1)}, u32[]{:S(2)}, u32[]{:S(2)}) %collective-permute-start.3) | collective-permute-done | bytes 131104 | tf_op jit(solution)/shard_map/ppermute | solution.py:323
  24.4 1.2 %coarse.1.down_ref = bf16[64,128]{1,0:T(8,128)(2,1)S(1)} custom-call(s32[2,32]{1,0:T(2,128)} %sources_hbm.4, bf16[12,64,128]{2,1,0:T(8,128)(2,1)S(1)} %get-tuple-element.13.own_ref, bf16[12,64,128]{2,1,0:T(8,128)(2,1)S(1)} %collective-permute-done.a_ref, bf16[12,64,128]{2,1,0:T(8,128)(2,1)S(1)} %collective-permute-done.1.la_ref, ...), custom_call_target="tpu_custom_call" | custom-call | flops 1000000000 | bytes 1024 | tf_op jit(solution)/shard_map/coarse/pallas_call | solution.py:397
  25.7 0.7 %collective-permute-start.7 = (bf16[64,128]{1,0:T(8,128)(2,1)S(1)}, bf16[64,128]{1,0:T(8,128)(2,1)S(1)}, u32[]{:S(2)}, u32[]{:S(2)}) collective-permute-start(bf16[64,128]{1,0:T(8,128)(2,1)S(1)} %coarse.1.down_ref), channel_id=1, source_target_pairs={{1,13},{2,6},{3,11},{5,9},{6,2},{7,15},{9,5},{10,14},{11,3},{13,1}... | collective-permute-start | bytes 49160 | tf_op jit(solution)/shard_map/ppermute | solution.py:323
  26.3 0.0 collective-permute-done.7.got_ref
  26.3 0.0 copy-done.1
  26.4 0.0 copy-done.4
  26.4 0.0 copy-done.5
  26.4 2.7 %down.1 = (bf16[2,16,2048]{2,1,0:T(8,128)(2,1)S(1)}, f32[2,16,2048]{2,1,0:T(8,128)S(1)}) custom-call(s32[8,64]{1,0:T(8,128)} %sources_hbm.5, s32[8]{0:T(128)} %parents_hbm.3, bf16[12,64,128]{2,1,0:T(8,128)(2,1)S(1)} %get-tuple-element.13.own_ref, bf16[12,64,128]{2,1,0:T(8,128)(2,1)S(1)} %collective-permute-done.a_ref, ...), custom_call_target="tpu_custom_call" | custom-call | flops 2500000000 | bytes 1024 | tf_op jit(solution)/shard_map/down/pallas_call | solution.py:418
  29.1 6.1 %collective-permute-start.8 = (bf16[2,16,2048]{2,1,0:T(8,128)(2,1)S(1)}, bf16[2,16,2048]{2,1,0:T(8,128)(2,1)S(1)}, u32[]{:S(2)}, u32[]{:S(2)}) collective-permute-start(bf16[2,16,2048]{2,1,0:T(8,128)(2,1)S(1)} %get-tuple-element.18), channel_id=1, source_target_pairs={{0,1},{1,0},{2,3},{3,2},{4,5},{5,4},{6,7},{7,6},{8,9},{9,8},{10,11... | collective-permute-start | bytes 393224 | tf_op jit(solution)/shard_map/ppermute | solution.py:323
  35.2 1.0 %collective-permute-done.8.got_ref = bf16[2,16,2048]{2,1,0:T(8,128)(2,1)S(1)} collective-permute-done((bf16[2,16,2048]{2,1,0:T(8,128)(2,1)S(1)}, bf16[2,16,2048]{2,1,0:T(8,128)(2,1)S(1)}, u32[]{:S(2)}, u32[]{:S(2)}) %collective-permute-start.8) | collective-permute-done | bytes 131104 | tf_op jit(solution)/shard_map/ppermute | solution.py:323
  36.2 1.1 %collective-permute-start.9 = (bf16[16,2048]{1,0:T(8,128)(2,1)S(1)}, bf16[16,2048]{1,0:T(8,128)(2,1)S(1)}, u32[]{:S(2)}, u32[]{:S(2)}) collective-permute-start(bf16[16,2048]{1,0:T(8,128)(2,1)S(1)} %get-tuple-element.20), channel_id=1, source_target_pairs={{0,2},{1,3},{2,0},{3,1},{4,6},{5,7},{6,4},{7,5},{8,10},{9,11},{10,... | collective-permute-start | bytes 196616 | tf_op jit(solution)/shard_map/ppermute | solution.py:323
  37.3 3.4 %collective-permute-done.9 = bf16[16,2048]{1,0:T(8,128)(2,1)S(1)} collective-permute-done((bf16[16,2048]{1,0:T(8,128)(2,1)S(1)}, bf16[16,2048]{1,0:T(8,128)(2,1)S(1)}, u32[]{:S(2)}, u32[]{:S(2)}) %collective-permute-start.9) | collective-permute-done | bytes 65568 | tf_op jit(solution)/shard_map/ppermute | solution.py:323
  40.6 0.6 %add_convert_fusion = bf16[16,2048]{1,0:T(8,128)(2,1)} fusion(f32[16,2048]{1,0:T(8,128)S(1)} %get-tuple-element.19, bf16[16,2048]{1,0:T(8,128)(2,1)S(1)} %collective-permute-done.9), kind=kLoop, calls=%fused_computation | loop fusion | flops 98304 | bytes 262144 | tf_op jit(solution)/shard_map/convert_element_type | solution.py:451
  (1 shorter events, 0.0 us)
Async XLA Ops:
  0.0 19.6 %copy-start.2 = (bf16[64,2048]{1,0:T(8,128)(2,1)S(1)}, bf16[64,2048]{1,0:T(8,128)(2,1)}, u32[]{:S(2)}) copy-start(bf16[64,2048]{1,0:T(8,128)(2,1)} %x_ref.1) | copy-start | bytes 786436
  0.0 10.7 %copy-start.3 = (bf16[2,8,64,64]{3,2,1,0:T(8,128)(2,1)S(1)}, bf16[2,8,64,64]{3,2,1,0:T(8,128)(2,1)}, u32[]{:S(2)}) copy-start(bf16[2,8,64,64]{3,2,1,0:T(8,128)(2,1)} %p_own.1) | copy-start | bytes 393220
  0.0 19.6 %copy-start = (bf16[8,4,256,256]{3,2,1,0:T(8,128)(2,1)S(1)}, bf16[8,4,256,256]{3,2,1,0:T(8,128)(2,1)}, u32[]{:S(2)}) copy-start(bf16[8,4,256,256]{3,2,1,0:T(8,128)(2,1)} %blocks_ref.2) | copy-start | bytes 12582916
  1.8 8.9 %collective-permute-start = (bf16[12,64,128]{2,1,0:T(8,128)(2,1)S(1)}, bf16[12,64,128]{2,1,0:T(8,128)(2,1)S(1)}, u32[]{:S(2)}, u32[]{:S(2)}) collective-permute-start(bf16[12,64,128]{2,1,0:T(8,128)(2,1)S(1)} %get-tuple-element.13.own_ref), channel_id=1, source_target_pairs={{0,4},{1,13},{2,6},{3,15},{4,0},{5,9},{6,2},{7,11},{8,12},{9,5},{1... | collective-permute-start | bytes 589832 | tf_op jit(solution)/shard_map/ppermute | solution.py:323
  10.7 8.9 %collective-permute-start.1 = (bf16[12,64,128]{2,1,0:T(8,128)(2,1)S(1)}, bf16[12,64,128]{2,1,0:T(8,128)(2,1)S(1)}, u32[]{:S(2)}, u32[]{:S(2)}) collective-permute-start(bf16[12,64,128]{2,1,0:T(8,128)(2,1)S(1)} %collective-permute-done.a_ref), channel_id=1, source_target_pairs={{0,1},{1,0},{2,3},{3,2},{4,5},{5,4},{6,7},{7,6},{8,9},{9,8},{10,11... | collective-permute-start | bytes 589832 | tf_op jit(solution)/shard_map/ppermute | solution.py:323
  10.7 8.9 %collective-permute-start.5 = (bf16[2,8,64,64]{3,2,1,0:T(8,128)(2,1)S(1)}, bf16[2,8,64,64]{3,2,1,0:T(8,128)(2,1)S(1)}, u32[]{:S(2)}, u32[]{:S(2)}) collective-permute-start(bf16[2,8,64,64]{3,2,1,0:T(8,128)(2,1)S(1)} %copy-done.3), channel_id=1, source_target_pairs={{0,2},{1,3},{2,0},{3,1},{4,6},{5,7},{6,4},{7,5},{8,10},{9,11},{10,... | collective-permute-start | bytes 393224 | tf_op jit(solution)/shard_map/ppermute | solution.py:323
  12.6 9.9 %collective-permute-start.4 = (bf16[2,8,64,64]{3,2,1,0:T(8,128)(2,1)S(1)}, bf16[2,8,64,64]{3,2,1,0:T(8,128)(2,1)S(1)}, u32[]{:S(2)}, u32[]{:S(2)}) collective-permute-start(bf16[2,8,64,64]{3,2,1,0:T(8,128)(2,1)S(1)} %copy-done.3), channel_id=1, source_target_pairs={{0,1},{1,0},{2,3},{3,2},{4,5},{5,4},{6,7},{7,6},{8,9},{9,8},{10,11... | collective-permute-start | bytes 393224 | tf_op jit(solution)/shard_map/ppermute | solution.py:323
  12.8 13.5 %copy-start.1 = (bf16[8,16,64,64]{3,2,1,0:T(8,128)(2,1)S(1)}, bf16[8,16,64,64]{3,2,1,0:T(8,128)(2,1)}, u32[]{:S(2)}) copy-start(bf16[8,16,64,64]{3,2,1,0:T(8,128)(2,1)} %blocks_ref.3) | copy-start | bytes 3145732
  12.8 13.5 %copy-start.4 = (bf16[8,64,256]{2,1,0:T(8,128)(2,1)S(1)}, bf16[8,64,256]{2,1,0:T(8,128)(2,1)}, u32[]{:S(2)}) copy-start(bf16[8,64,256]{2,1,0:T(8,128)(2,1)} %basis_ref.1) | copy-start | bytes 786436
  12.8 13.5 %copy-start.5 = (bf16[8,64,64]{2,1,0:T(8,128)(2,1)S(1)}, bf16[8,64,64]{2,1,0:T(8,128)(2,1)}, u32[]{:S(2)}) copy-start(bf16[8,64,64]{2,1,0:T(8,128)(2,1)} %transfer_ref.1) | copy-start | bytes 196612
  12.8 8.4 %collective-permute-start.2 = (bf16[8,64,128]{2,1,0:T(8,128)(2,1)S(1)}, bf16[8,64,128]{2,1,0:T(8,128)(2,1)S(1)}, u32[]{:S(2)}, u32[]{:S(2)}) collective-permute-start(bf16[8,64,128]{2,1,0:T(8,128)(2,1)S(1)} %get-tuple-element.14), channel_id=1, source_target_pairs={{1,9},{3,11},{5,13},{7,15},{9,1},{11,3},{13,5},{15,7},{17,25},{19,... | collective-permute-start | bytes 393224 | tf_op jit(solution)/shard_map/ppermute | solution.py:323
  19.6 2.9 %collective-permute-start.6 = (bf16[2,8,64,64]{3,2,1,0:T(8,128)(2,1)S(1)}, bf16[2,8,64,64]{3,2,1,0:T(8,128)(2,1)S(1)}, u32[]{:S(2)}, u32[]{:S(2)}) collective-permute-start(bf16[2,8,64,64]{3,2,1,0:T(8,128)(2,1)S(1)} %collective-permute-done.5.p_vec), channel_id=1, source_target_pairs={{0,1},{1,0},{2,3},{3,2},{4,5},{5,4},{6,7},{7,6},{8,9},{9,8},{10,11... | collective-permute-start | bytes 393224 | tf_op jit(solution)/shard_map/ppermute | solution.py:323
  21.2 3.2 %collective-permute-start.3 = (bf16[8,64,128]{2,1,0:T(8,128)(2,1)S(1)}, bf16[8,64,128]{2,1,0:T(8,128)(2,1)S(1)}, u32[]{:S(2)}, u32[]{:S(2)}) collective-permute-start(bf16[8,64,128]{2,1,0:T(8,128)(2,1)S(1)} %collective-permute-done.2.b_ref), channel_id=1, source_target_pairs={{1,0},{3,2},{5,4},{7,6},{9,8},{11,10},{13,12},{15,14},{17,16},{19,... | collective-permute-start | bytes 393224 | tf_op jit(solution)/shard_map/ppermute | solution.py:323
  25.7 0.7 %collective-permute-start.7 = (bf16[64,128]{1,0:T(8,128)(2,1)S(1)}, bf16[64,128]{1,0:T(8,128)(2,1)S(1)}, u32[]{:S(2)}, u32[]{:S(2)}) collective-permute-start(bf16[64,128]{1,0:T(8,128)(2,1)S(1)} %coarse.1.down_ref), channel_id=1, source_target_pairs={{1,13},{2,6},{3,11},{5,9},{6,2},{7,15},{9,5},{10,14},{11,3},{13,1}... | collective-permute-start | bytes 49160 | tf_op jit(solution)/shard_map/ppermute | solution.py:323
  29.1 7.1 %collective-permute-start.8 = (bf16[2,16,2048]{2,1,0:T(8,128)(2,1)S(1)}, bf16[2,16,2048]{2,1,0:T(8,128)(2,1)S(1)}, u32[]{:S(2)}, u32[]{:S(2)}) collective-permute-start(bf16[2,16,2048]{2,1,0:T(8,128)(2,1)S(1)} %get-tuple-element.18), channel_id=1, source_target_pairs={{0,1},{1,0},{2,3},{3,2},{4,5},{5,4},{6,7},{7,6},{8,9},{9,8},{10,11... | collective-permute-start | bytes 393224 | tf_op jit(solution)/shard_map/ppermute | solution.py:323
  36.2 4.4 %collective-permute-start.9 = (bf16[16,2048]{1,0:T(8,128)(2,1)S(1)}, bf16[16,2048]{1,0:T(8,128)(2,1)S(1)}, u32[]{:S(2)}, u32[]{:S(2)}) collective-permute-start(bf16[16,2048]{1,0:T(8,128)(2,1)S(1)} %get-tuple-element.20), channel_id=1, source_target_pairs={{0,2},{1,3},{2,0},{3,1},{4,6},{5,7},{6,4},{7,5},{8,10},{9,11},{10,... | collective-permute-start | bytes 196616 | tf_op jit(solution)/shard_map/ppermute | solution.py:323

commit v3 on v2

--- a/solution.py
+++ b/solution.py
@@ -131,8 +131,9 @@
     return (far_out + near_sum).astype(jnp.bfloat16)
 
 
-def up_kernel(x_hbm, basis_hbm, transfer_hbm, parents_hbm, msg_ref, short_ref,
-              x_ref, basis_ref, transfer_ref, parents_ref, sums, sems):
+def up_kernel(x_hbm, basis_hbm, transfer_hbm, coarse_hbm, parents_hbm,
+              msg_ref, short_ref, packed_ref,
+              x_ref, basis_ref, transfer_ref, coarse_ref, parents_ref, sums, sems):
     copies = [
         pltpu.make_async_copy(a, b, sems.at[i])
         for i, (a, b) in enumerate((
@@ -140,6 +141,7 @@
             (basis_hbm, basis_ref),
             (parents_hbm, parents_ref),
             (transfer_hbm, transfer_ref),
+            (coarse_hbm, coarse_ref),
         ))
     ]
     for copy in copies:
@@ -170,12 +172,56 @@
     for p in range(clusters // 2):
         merged = jnp.concatenate([sums[2 * p], sums[2 * p + 1]], axis=-1).astype(BF)
         msg_ref[pairs + p] = short_ref[pairs + p] = merged
-
-
-def near_kernel(sources_hbm, x_ref, a_ref, la_ref, blocks_ref, out_ref, sources_ref, table, sem):
+    copies[4].wait()
+    for j in range(coarse_ref.shape[1]):
+        packed_ref[j] = jnp.concatenate([coarse_ref[0, j], coarse_ref[1, j]], axis=-1)
+
+
+def coarse_kernel(sources_hbm, own_ref, a_ref, la_ref, b_ref, lb_ref,
+                  p_own, p_lvl, p_vec, p_diag, out_ref, sources_ref, table, sem):
     copy = pltpu.make_async_copy(sources_hbm, sources_ref, sem)
     copy.start()
-    leaves, share, panel, _ = blocks_ref.shape
+    share, rank, wide = p_own.shape
+    vectors = out_ref.shape[0]
+    pairs = table.shape[0] // 2
+    c = lax.axis_index("lvl")
+    me = lax.axis_index("vec") * 2 + c
+    for p in range(pairs):
+        q = pairs + p
+        across = jnp.where(c == 1, b_ref[q].astype(F32), lb_ref[q].astype(F32))
+        total = (own_ref[q].astype(F32) + a_ref[q].astype(F32)) + (la_ref[q].astype(F32) + across)
+        table[p] = total.astype(BF)
+        table[pairs + p] = swap_halves(total).astype(BF)
+    low = low_half((vectors, wide))
+    acc = jnp.zeros((2 * vectors, wide), F32)
+    copy.wait()
+    for flip, blocks in enumerate((p_own, p_lvl, p_vec, p_diag)):
+        base = (me ^ flip) * share
+        rows = []
+        for cluster in range(2):
+            lanes = []
+            for j in range(0, share, 2):
+                s0 = sources_ref[cluster, base + j]
+                s1 = sources_ref[cluster, base + j + 1]
+                first = table[(s0 & 1) * pairs + (s0 >> 1)]
+                second = table[(1 - (s1 & 1)) * pairs + (s1 >> 1)]
+                lanes.append(jnp.where(low, first, second))
+            rows.append(jnp.concatenate(lanes, axis=-1))
+        acc = acc + dot(jnp.concatenate(rows, axis=0), blocks[...].reshape(share * rank, wide))
+    out_ref[...] = jnp.where(low, acc[:vectors], acc[vectors:]).astype(BF)
+
+
+def local_kernel(near_hbm, far_hbm, own_ref, a_ref, la_ref, b_ref, lb_ref, x_ref,
+                 near_blocks_ref, far_blocks_ref, near_ref, far_ref,
+                 near_sources, far_sources, panels, table, sems):
+    copies = [
+        pltpu.make_async_copy(near_hbm, near_sources, sems.at[0]),
+        pltpu.make_async_copy(far_hbm, far_sources, sems.at[1]),
+    ]
+    for copy in copies:
+        copy.start()
+    leaves, near_share, panel, _ = near_blocks_ref.shape
+    far_share, rank = far_blocks_ref.shape[1:3]
     z, c = lax.axis_index("leaf"), lax.axis_index("lvl")
     owner = lax.axis_index("vec") * 2 + c
     high = (z + c) % 2 == 0
@@ -187,70 +233,11 @@
     base = a_ref.shape[0] - REACH * parts
     for i in range(REACH):
         for w in range(parts):
-            table[at_a + i, :, w * lanes:(w + 1) * lanes] = a_ref[base + i * parts + w]
-            table[at_la + i, :, w * lanes:(w + 1) * lanes] = la_ref[base + i * parts + w]
+            panels[at_a + i, :, w * lanes:(w + 1) * lanes] = a_ref[base + i * parts + w]
+            panels[at_la + i, :, w * lanes:(w + 1) * lanes] = la_ref[base + i * parts + w]
     for l in range(leaves):
-        table[REACH + l] = x_ref[:, l * panel:(l + 1) * panel]
-    copy.wait()
-    for l in range(leaves):
-        rows = [
-            table[sources_ref[l, owner * share + j] - z * leaves + REACH] for j in range(share)
-        ]
-        out_ref[l] = dot(
-            jnp.concatenate(rows, axis=-1), blocks_ref[l].reshape(share * panel, panel)
-        )
-
-
-def coarse_kernel(sources_hbm, own_ref, a_ref, la_ref, b_ref, lb_ref,
-                  p_own, p_lvl, p_vec, p_diag, out_ref, sources_ref, table, sem):
-    copy = pltpu.make_async_copy(sources_hbm, sources_ref, sem)
-    copy.start()
-    _, share, rank, _ = p_own.shape
-    pairs = table.shape[0] // 2
-    c = lax.axis_index("lvl")
-    me = lax.axis_index("vec") * 2 + c
-    for p in range(pairs):
-        q = pairs + p
-        across = jnp.where(c == 1, b_ref[q].astype(F32), lb_ref[q].astype(F32))
-        total = (own_ref[q].astype(F32) + a_ref[q].astype(F32)) + (la_ref[q].astype(F32) + across)
-        table[p] = total.astype(BF)
-        table[pairs + p] = swap_halves(total).astype(BF)
-    low = low_half((out_ref.shape[0], 2 * rank))
-    accs = [jnp.zeros((out_ref.shape[0], rank), F32) for _ in range(2)]
-    copy.wait()
-    for flip, blocks in enumerate((p_own, p_lvl, p_vec, p_diag)):
-        base = (me ^ flip) * share
-        for cluster in range(2):
-            lanes = []
-            for j in range(0, share, 2):
-                s0 = sources_ref[cluster, base + j]
-                s1 = sources_ref[cluster, base + j + 1]
-                first = table[(s0 & 1) * pairs + (s0 >> 1)]
-                second = table[(1 - (s1 & 1)) * pairs + (s1 >> 1)]
-                lanes.append(jnp.where(low, first, second))
-            accs[cluster] = accs[cluster] + dot(
-                jnp.concatenate(lanes, axis=-1), blocks[cluster].reshape(share * rank, rank)
-            )
-    out_ref[...] = jnp.concatenate(accs, axis=-1).astype(BF)
-
-
-def down_kernel(sources_hbm, parents_hbm, own_ref, a_ref, la_ref, b_ref, lb_ref,
-                blocks_ref, down_ref, got_ref, transfer_ref, basis_ref, near_ref,
-                send_ref, keep_ref, sources_ref, parents_ref, table, total, sems):
-    copies = [
-        pltpu.make_async_copy(a, b, sems.at[i])
-        for i, (a, b) in enumerate((
-            (sources_hbm, sources_ref),
-            (parents_hbm, parents_ref),
-        ))
-    ]
-    for copy in copies:
-        copy.start()
-    leaves, share, rank, _ = blocks_ref.shape
-    panel = basis_ref.shape[2]
+        panels[REACH + l] = x_ref[:, l * panel:(l + 1) * panel]
     pairs = leaves // 2
-    z, v, c = lax.axis_index("leaf"), lax.axis_index("vec"), lax.axis_index("lvl")
-    owner = v * 2 + c
     far = jnp.where(c == 1, 3, 1)
     near = jnp.where(c == 1, 1, 3)
     count = 4 * pairs
@@ -268,28 +255,47 @@
         table[2 * pairs + p] = x.astype(BF)
         table[count + 2 * pairs + p] = swap_halves(x).astype(BF)
     low = low_half((own_ref.shape[1], 2 * rank))
-    lane = lax.broadcasted_iota(jnp.int32, low.shape, 1)
-    distance = jnp.where(c == 1, jnp.where(v == 1, 2, 3), jnp.where(v == 1, 1, 0))
-    home = z ^ distance
-    down = jnp.where(distance == 0, down_ref[...].astype(F32), got_ref[...].astype(F32))
     for copy in copies:
         copy.wait()
     for l in range(leaves):
-        lanes = []
-        for j in range(0, share, 2):
-            s0 = sources_ref[l, owner * share + j]
-            s1 = sources_ref[l, owner * share + j + 1]
+        rows = [
+            panels[near_sources[l, owner * near_share + j] - z * leaves + REACH]
+            for j in range(near_share)
+        ]
+        near_ref[l] = dot(
+            jnp.concatenate(rows, axis=-1), near_blocks_ref[l].reshape(near_share * panel, panel)
+        )
+        rows = []
+        for j in range(0, far_share, 2):
+            s0 = far_sources[l, owner * far_share + j]
+            s1 = far_sources[l, owner * far_share + j + 1]
             at0 = ((s0 // leaves) ^ z) * pairs + ((s0 % leaves) >> 1)
             at1 = ((s1 // leaves) ^ z) * pairs + ((s1 % leaves) >> 1)
             first = table[(s0 & 1) * count + at0]
             second = table[(1 - (s1 & 1)) * count + at1]
-            lanes.append(jnp.where(low, first, second))
-        part = dot(jnp.concatenate(lanes, axis=-1), blocks_ref[l].reshape(share * rank, rank))
+            rows.append(jnp.where(low, first, second))
+        far_ref[l] = dot(
+            jnp.concatenate(rows, axis=-1), far_blocks_ref[l].reshape(far_share * rank, rank)
+        )
+
+
+def down_kernel(parents_hbm, near_ref, far_ref, down_ref, got_ref, transfer_ref, basis_ref,
+                send_ref, keep_ref, parents_ref, total, sem):
+    copy = pltpu.make_async_copy(parents_hbm, parents_ref, sem)
+    copy.start()
+    leaves, rank, panel = basis_ref.shape
+    z, v, c = lax.axis_index("leaf"), lax.axis_index("vec"), lax.axis_index("lvl")
+    lane = lax.broadcasted_iota(jnp.int32, down_ref.shape, 1)
+    distance = jnp.where(c == 1, jnp.where(v == 1, 2, 3), jnp.where(v == 1, 1, 0))
+    home = z ^ distance
+    down = jnp.where(distance == 0, down_ref[...].astype(F32), got_ref[...].astype(F32))
+    copy.wait()
+    for l in range(leaves):
         parent = parents_ref[l]
         begin = jnp.where((parent >> 1) == home, (parent & 1) * rank, -2 * rank)
         pushed = jnp.where((lane >= begin) & (lane < begin + rank), down, 0.0).astype(BF)
         weight = transfer_ref[l]
-        part = part + dot_t(pushed, jnp.concatenate([weight, weight], axis=-1))
+        part = far_ref[l] + dot_t(pushed, jnp.concatenate([weight, weight], axis=-1))
         total[:, l * panel:(l + 1) * panel] = near_ref[l] + dot(part.astype(BF), basis_ref[l])
     rows = keep_ref.shape[1]
     for w in range(2):
@@ -352,47 +358,35 @@
     def other_chip(z, v, c):
         return z, 1 - v, c
 
-    p_lvl = swap(coarse_blocks, other_core)
-    p_vec = swap(coarse_blocks, other_chip)
-    msg, short = pl.pallas_call(
+    msg, short, packed = pl.pallas_call(
         up_kernel,
         out_shape=(
             jax.ShapeDtypeStruct((messages, vectors, wide), BF),
             jax.ShapeDtypeStruct((leaves // 2 + clusters // 2, vectors, wide), BF),
+            jax.ShapeDtypeStruct((coarse_blocks.shape[1], rank, wide), BF),
         ),
-        in_specs=[HBM] * 4,
-        out_specs=(VMEM,) * 2,
+        in_specs=[HBM] * 5,
+        out_specs=(VMEM,) * 3,
         scratch_shapes=[
             pltpu.VMEM(adjoint_in.shape, BF),
             pltpu.VMEM(row_basis.shape, BF),
             pltpu.VMEM(row_transfer.shape, BF),
+            pltpu.VMEM(coarse_blocks.shape, BF),
             pltpu.SMEM(parents.shape, jnp.int32),
             pltpu.VMEM((clusters, vectors, rank), F32),
-            pltpu.SemaphoreType.DMA((4,)),
+            pltpu.SemaphoreType.DMA((5,)),
         ],
         compiler_params=params,
         cost_estimate=cost(1.5),
         name="up",
-    )(*in_hbm(adjoint_in, row_basis, row_transfer, parents))
+    )(*in_hbm(adjoint_in, row_basis, row_transfer, coarse_blocks, parents))
     a = swap(msg, lambda z, v, c: (z ^ (3 if c else 1), v, c))
     b = swap(short, lambda z, v, c: (z ^ 2, v, c) if c else None)
+    p_lvl = swap(packed, other_core)
+    p_vec = swap(packed, other_chip)
     p_diag = swap(p_vec, other_core)
+    a, b = lax.optimization_barrier((a, b))
     la = swap(a, other_core)
-    near = pl.pallas_call(
-        near_kernel,
-        out_shape=jax.ShapeDtypeStruct((leaves, vectors, panel), F32),
-        in_specs=[HBM] + [VMEM] * 4,
-        out_specs=VMEM,
-        scratch_shapes=[
-            pltpu.SMEM(near_sources.shape, jnp.int32),
-            pltpu.VMEM((leaves + 2 * REACH, vectors, panel), BF),
-            pltpu.SemaphoreType.DMA(()),
-        ],
-        compiler_params=params,
-        cost_estimate=cost(2.5),
-        name="near",
-    )(*in_hbm(near_sources), adjoint_in, a, la, near_blocks)
-    b, near = lax.optimization_barrier((b, near))
     lb = swap(b, lambda z, v, c: (z, v, 0) if c else None)
     down = pl.pallas_call(
         coarse_kernel,
@@ -407,13 +401,32 @@
         compiler_params=params,
         cost_estimate=cost(1.0),
         name="coarse",
-    )(*in_hbm(coarse_sources), msg, a, la, b, lb, coarse_blocks, p_lvl, p_vec, p_diag)
+    )(*in_hbm(coarse_sources), msg, a, la, b, lb, packed, p_lvl, p_vec, p_diag)
 
     def home(z, v, c):
         distance = (2 if v else 3) if c else (1 if v else 0)
         return (z ^ distance, v, c) if distance else None
 
     got = swap(down, home)
+    near, far = pl.pallas_call(
+        local_kernel,
+        out_shape=(
+            jax.ShapeDtypeStruct((leaves, vectors, panel), F32),
+            jax.ShapeDtypeStruct((leaves, vectors, rank), F32),
+        ),
+        in_specs=[HBM] * 2 + [VMEM] * 8,
+        out_specs=(VMEM,) * 2,
+        scratch_shapes=[
+            pltpu.SMEM(near_sources.shape, jnp.int32),
+            pltpu.SMEM(far_sources.shape, jnp.int32),
+            pltpu.VMEM((leaves + 2 * REACH, vectors, panel), BF),
+            pltpu.VMEM((4 * leaves, vectors, wide), BF),
+            pltpu.SemaphoreType.DMA((2,)),
+        ],
+        compiler_params=params,
+        cost_estimate=cost(4.0),
+        name="local",
+    )(*in_hbm(near_sources, far_sources), msg, a, la, b, lb, adjoint_in, near_blocks, far_blocks)
     rows = vectors // 4
     send, keep = pl.pallas_call(
         down_kernel,
@@ -421,19 +434,17 @@
             jax.ShapeDtypeStruct((2, rows, width), BF),
             jax.ShapeDtypeStruct((2, rows, width), F32),
         ),
-        in_specs=[HBM] * 2 + [VMEM] * 11,
+        in_specs=[HBM] + [VMEM] * 6,
         out_specs=(VMEM,) * 2,
         scratch_shapes=[
-            pltpu.SMEM(far_sources.shape, jnp.int32),
             pltpu.SMEM(parents.shape, jnp.int32),
-            pltpu.VMEM((4 * leaves, vectors, wide), BF),
             pltpu.VMEM((vectors, width), F32),
-            pltpu.SemaphoreType.DMA((2,)),
+            pltpu.SemaphoreType.DMA(()),
         ],
         compiler_params=params,
-        cost_estimate=cost(2.5),
+        cost_estimate=cost(1.0),
         name="down",
-    )(*in_hbm(far_sources, parents), msg, a, la, b, lb, far_blocks, down, got, col_transfer, col_basis, near)
+    )(*in_hbm(parents), near, far, down, got, col_transfer, col_basis)
     came = swap(send, other_core)
     send, rest = pl.pallas_call(
         merge_kernel,

time: 41.5 us -> 34.1 us (0.82)
  waiting for transfers between devices: 18 us -> 9.91 us
  starting transfers between devices: 15.2 us -> 15.8 us
    ppermute x10, waiting for transfers between devices: 18 us -> 9.91 us  [swap(): return lax.ppermute(x, axes, pairs)]
    pallas_call x1, Pallas kernels: 1.59 us -> 2.31 us  [on_device_paired(): pl.pallas_call(local_kernel, out_shape=(jax.ShapeDtypeStruct((leaves, vec...]
    pallas_call x1, Pallas kernels: 2.68 us -> 1.96 us  [on_device_paired(): pl.pallas_call(down_kernel, out_shape=(jax.ShapeDtypeStruct((2, rows, wid...]
    ppermute x10, starting transfers between devices: 15.2 us -> 15.8 us  [swap(): return lax.ppermute(x, axes, pairs)]
  transfers between devices with their start and end apart: 10 -> 10, of which waited for: 5 -> 4; matrix products, arithmetic and copies ran while one was open for 0% -> 0% of each run, Pallas kernels for 4% -> 7%
where the time goes in v3:
time: 34.1 us; the launch traced here: 33.8 us
  starting transfers between devices  15.8 us (46%)
  waiting for transfers between devices  9.91 us (29%)
  Pallas kernels  7.29 us (21%)
  other arithmetic  0.64 us (2%)
    ppermute x10, starting transfers between devices, swap(): return lax.ppermute(x, axes, pairs)  15.8 us
    ppermute x10, waiting for transfers between devices, swap(): return lax.ppermute(x, axes, pairs)  9.91 us
    pallas_call x1, Pallas kernels, on_device_paired(): pl.pallas_call(local_kernel, out_shape=(jax.ShapeDtypeStruct((leaves, vec...  2.31 us
    pallas_call x1, Pallas kernels, on_device_paired(): pl.pallas_call(down_kernel, out_shape=(jax.ShapeDtypeStruct((2, rows, wid...  1.96 us
    pallas_call x1, Pallas kernels, on_device_paired(): pl.pallas_call(up_kernel, out_shape=(jax.ShapeDtypeStruct((messages, vect...  1.9 us
    pallas_call x1, Pallas kernels, on_device_paired(): pl.pallas_call(coarse_kernel, out_shape=jax.ShapeDtypeStruct((vectors, wi...  1.09 us
  transfers between devices with their start and end apart: 10, of which 4 were waited for; matrix products, arithmetic and copies ran while one was open for 0% of the time, Pallas kernels for 7%

profile of v3, /device:TPU:0, one launch (start us, length us, event | category | flops | bytes accessed | tf_op | source)
XLA Modules:
  0.0 33.8 jit_solution(3149560259293005205)
XLA Ops:
  0.0 0.0 copy-start.2
  0.0 0.0 copy-start
  0.0 0.0 copy-start.1
  0.0 1.9 %up.1 = (bf16[12,64,128]{2,1,0:T(8,128)(2,1)S(1)}, bf16[8,64,128]{2,1,0:T(8,128)(2,1)S(1)}, bf16[8,64,128]{2,1,0:T(8,128)(2,1)S(1)}) custom-call(bf16[64,2048]{1,0:T(8,128)(2,1)} %x_ref.1, bf16[8,64,256]{2,1,0:T(8,128)(2,1)} %basis_hbm.1, bf16[8,64,64]{2,1,0:T(8,128)(2,1)} %transfer_hbm.1, bf16[2,8,64,64]{3,2,1,0:T(8,128)(2,1)} %coarse_hbm.1, s32[8]{0:T(128)} %parents_hbm.3), custom_call_target="tpu_custom_call" | custom-call | flops 1500000000 | bytes 1024 | tf_op jit(solution)/shard_map/up/pallas_call | solution.py:361
  1.9 3.1 %collective-permute-start = (bf16[12,64,128]{2,1,0:T(8,128)(2,1)S(1)}, bf16[12,64,128]{2,1,0:T(8,128)(2,1)S(1)}, u32[]{:S(2)}, u32[]{:S(2)}) collective-permute-start(bf16[12,64,128]{2,1,0:T(8,128)(2,1)S(1)} %get-tuple-element.16.own_ref), channel_id=1, source_target_pairs={{0,4},{1,13},{2,6},{3,15},{4,0},{5,9},{6,2},{7,11},{8,12},{9,5},{1... | collective-permute-start | bytes 589832 | tf_op jit(solution)/shard_map/ppermute | solution.py:329
  5.0 0.7 %collective-permute-start.1 = (bf16[8,64,128]{2,1,0:T(8,128)(2,1)S(1)}, bf16[8,64,128]{2,1,0:T(8,128)(2,1)S(1)}, u32[]{:S(2)}, u32[]{:S(2)}) collective-permute-start(bf16[8,64,128]{2,1,0:T(8,128)(2,1)S(1)} %get-tuple-element.17), channel_id=1, source_target_pairs={{1,9},{3,11},{5,13},{7,15},{9,1},{11,3},{13,5},{15,7},{17,25},{19,... | collective-permute-start | bytes 393224 | tf_op jit(solution)/shard_map/ppermute | solution.py:329
  5.7 1.6 %collective-permute-start.5 = (bf16[8,64,128]{2,1,0:T(8,128)(2,1)S(1)}, bf16[8,64,128]{2,1,0:T(8,128)(2,1)S(1)}, u32[]{:S(2)}, u32[]{:S(2)}) collective-permute-start(bf16[8,64,128]{2,1,0:T(8,128)(2,1)S(1)} %get-tuple-element.22.p_own), channel_id=1, source_target_pairs={{0,2},{1,3},{2,0},{3,1},{4,6},{5,7},{6,4},{7,5},{8,10},{9,11},{10,... | collective-permute-start | bytes 393224 | tf_op jit(solution)/shard_map/ppermute | solution.py:329
  7.2 0.0 collective-permute-done.1.b_ref
  7.2 3.5 %collective-permute-done.a_ref = bf16[12,64,128]{2,1,0:T(8,128)(2,1)S(1)} collective-permute-done((bf16[12,64,128]{2,1,0:T(8,128)(2,1)S(1)}, bf16[12,64,128]{2,1,0:T(8,128)(2,1)S(1)}, u32[]{:S(2)}, u32[]{:S(2)}) %collective-permute-start) | collective-permute-done | bytes 196640 | tf_op jit(solution)/shard_map/ppermute | solution.py:329
  10.8 3.4 %collective-permute-start.2 = (bf16[12,64,128]{2,1,0:T(8,128)(2,1)S(1)}, bf16[12,64,128]{2,1,0:T(8,128)(2,1)S(1)}, u32[]{:S(2)}, u32[]{:S(2)}) collective-permute-start(bf16[12,64,128]{2,1,0:T(8,128)(2,1)S(1)} %collective-permute-done.a_ref), channel_id=1, source_target_pairs={{0,1},{1,0},{2,3},{3,2},{4,5},{5,4},{6,7},{7,6},{8,9},{9,8},{10,11... | collective-permute-start | bytes 589832 | tf_op jit(solution)/shard_map/ppermute | solution.py:329
  14.1 0.0 collective-permute-start.4
  14.1 0.0 collective-permute-done.5.p_vec
  14.1 0.5 %collective-permute-start.6 = (bf16[8,64,128]{2,1,0:T(8,128)(2,1)S(1)}, bf16[8,64,128]{2,1,0:T(8,128)(2,1)S(1)}, u32[]{:S(2)}, u32[]{:S(2)}) collective-permute-start(bf16[8,64,128]{2,1,0:T(8,128)(2,1)S(1)} %collective-permute-done.5.p_vec), channel_id=1, source_target_pairs={{0,1},{1,0},{2,3},{3,2},{4,5},{5,4},{6,7},{7,6},{8,9},{9,8},{10,11... | collective-permute-start | bytes 393224 | tf_op jit(solution)/shard_map/ppermute | solution.py:329
  14.6 1.3 %collective-permute-start.3 = (bf16[8,64,128]{2,1,0:T(8,128)(2,1)S(1)}, bf16[8,64,128]{2,1,0:T(8,128)(2,1)S(1)}, u32[]{:S(2)}, u32[]{:S(2)}) collective-permute-start(bf16[8,64,128]{2,1,0:T(8,128)(2,1)S(1)} %collective-permute-done.1.b_ref), channel_id=1, source_target_pairs={{1,0},{3,2},{5,4},{7,6},{9,8},{11,10},{13,12},{15,14},{17,16},{19,... | collective-permute-start | bytes 393224 | tf_op jit(solution)/shard_map/ppermute | solution.py:329
  15.9 0.0 collective-permute-done.4.p_lvl
  15.9 0.0 collective-permute-done.6.p_diag
  15.9 1.9 %collective-permute-done.3.lb_ref = bf16[8,64,128]{2,1,0:T(8,128)(2,1)S(1)} collective-permute-done((bf16[8,64,128]{2,1,0:T(8,128)(2,1)S(1)}, bf16[8,64,128]{2,1,0:T(8,128)(2,1)S(1)}, u32[]{:S(2)}, u32[]{:S(2)}) %collective-permute-start.3) | collective-permute-done | bytes 131104 | tf_op jit(solution)/shard_map/ppermute | solution.py:329
  17.9 0.0 collective-permute-done.2.la_ref
  17.9 1.1 %coarse.1.down_ref = bf16[64,128]{1,0:T(8,128)(2,1)S(1)} custom-call(s32[2,32]{1,0:T(2,128)} %sources_hbm.1, bf16[12,64,128]{2,1,0:T(8,128)(2,1)S(1)} %get-tuple-element.16.own_ref, bf16[12,64,128]{2,1,0:T(8,128)(2,1)S(1)} %collective-permute-done.a_ref, bf16[12,64,128]{2,1,0:T(8,128)(2,1)S(1)} %collective-permute-done.2.la_ref, ...), custom_call_target="tpu_custom_call" | custom-call | flops 1000000000 | bytes 1024 | tf_op jit(solution)/shard_map/coarse/pallas_call | solution.py:391
  19.0 0.0 copy-start.3
  19.0 0.0 copy-start.4
  19.0 0.8 %collective-permute-start.7 = (bf16[64,128]{1,0:T(8,128)(2,1)S(1)}, bf16[64,128]{1,0:T(8,128)(2,1)S(1)}, u32[]{:S(2)}, u32[]{:S(2)}) collective-permute-start(bf16[64,128]{1,0:T(8,128)(2,1)S(1)} %coarse.1.down_ref), channel_id=1, source_target_pairs={{1,13},{2,6},{3,11},{5,9},{6,2},{7,15},{9,5},{10,14},{11,3},{13,1}... | collective-permute-start | bytes 49160 | tf_op jit(solution)/shard_map/ppermute | solution.py:329
  19.8 0.0 copy-done.2
  19.8 0.0 copy-done
  19.8 0.0 copy-done.1
  19.8 2.3 %local.1 = (f32[8,64,256]{2,1,0:T(8,128)S(1)}, f32[8,64,64]{2,1,0:T(8,128)S(1)}) custom-call(s32[8,16]{1,0:T(8,128)} %near_hbm.1, s32[8,64]{1,0:T(8,128)} %far_hbm.1, bf16[12,64,128]{2,1,0:T(8,128)(2,1)S(1)} %get-tuple-element.16.own_ref, bf16[12,64,128]{2,1,0:T(8,128)(2,1)S(1)} %collective-permute-done.a_ref, ...), custom_call_target="tpu_custom_call" | custom-call | flops 4000000000 | bytes 1024 | tf_op jit(solution)/shard_map/local/pallas_call | solution.py:411
  22.2 0.0 collective-permute-done.7.got_ref
  22.2 0.0 copy-done.3
  22.2 0.0 copy-done.4
  22.2 2.0 %down.1 = (bf16[2,16,2048]{2,1,0:T(8,128)(2,1)S(1)}, f32[2,16,2048]{2,1,0:T(8,128)S(1)}) custom-call(s32[8]{0:T(128)} %parents_hbm.3, f32[8,64,256]{2,1,0:T(8,128)S(1)} %get-tuple-element.20.near_ref, f32[8,64,64]{2,1,0:T(8,128)S(1)} %get-tuple-element.21.far_ref, bf16[64,128]{1,0:T(8,128)(2,1)S(1)} %coarse.1.down_ref, ...), custom_call_target="tpu_custom_call" | custom-call | flops 1000000000 | bytes 1024 | tf_op jit(solution)/shard_map/down/pallas_call | solution.py:431
  24.2 3.6 %collective-permute-start.8 = (bf16[2,16,2048]{2,1,0:T(8,128)(2,1)S(1)}, bf16[2,16,2048]{2,1,0:T(8,128)(2,1)S(1)}, u32[]{:S(2)}, u32[]{:S(2)}) collective-permute-start(bf16[2,16,2048]{2,1,0:T(8,128)(2,1)S(1)} %get-tuple-element.24), channel_id=1, source_target_pairs={{0,1},{1,0},{2,3},{3,2},{4,5},{5,4},{6,7},{7,6},{8,9},{9,8},{10,11... | collective-permute-start | bytes 393224 | tf_op jit(solution)/shard_map/ppermute | solution.py:329
  27.8 1.0 %collective-permute-done.8.got_ref = bf16[2,16,2048]{2,1,0:T(8,128)(2,1)S(1)} collective-permute-done((bf16[2,16,2048]{2,1,0:T(8,128)(2,1)S(1)}, bf16[2,16,2048]{2,1,0:T(8,128)(2,1)S(1)}, u32[]{:S(2)}, u32[]{:S(2)}) %collective-permute-start.8) | collective-permute-done | bytes 131104 | tf_op jit(solution)/shard_map/ppermute | solution.py:329
  28.8 1.0 %collective-permute-start.9 = (bf16[16,2048]{1,0:T(8,128)(2,1)S(1)}, bf16[16,2048]{1,0:T(8,128)(2,1)S(1)}, u32[]{:S(2)}, u32[]{:S(2)}) collective-permute-start(bf16[16,2048]{1,0:T(8,128)(2,1)S(1)} %get-tuple-element.26), channel_id=1, source_target_pairs={{0,2},{1,3},{2,0},{3,1},{4,6},{5,7},{6,4},{7,5},{8,10},{9,11},{10,... | collective-permute-start | bytes 196616 | tf_op jit(solution)/shard_map/ppermute | solution.py:329
  29.7 3.5 %collective-permute-done.9 = bf16[16,2048]{1,0:T(8,128)(2,1)S(1)} collective-permute-done((bf16[16,2048]{1,0:T(8,128)(2,1)S(1)}, bf16[16,2048]{1,0:T(8,128)(2,1)S(1)}, u32[]{:S(2)}, u32[]{:S(2)}) %collective-permute-start.9) | collective-permute-done | bytes 65568 | tf_op jit(solution)/shard_map/ppermute | solution.py:329
  33.2 0.6 %add_convert_fusion = bf16[16,2048]{1,0:T(8,128)(2,1)} fusion(f32[16,2048]{1,0:T(8,128)S(1)} %get-tuple-element.25, bf16[16,2048]{1,0:T(8,128)(2,1)S(1)} %collective-permute-done.9), kind=kLoop, calls=%fused_computation | loop fusion | flops 98304 | bytes 262144 | tf_op jit(solution)/shard_map/convert_element_type | solution.py:462
  (1 shorter events, 0.0 us)
Async XLA Ops:
  0.0 19.8 %copy-start.2 = (bf16[64,2048]{1,0:T(8,128)(2,1)S(1)}, bf16[64,2048]{1,0:T(8,128)(2,1)}, u32[]{:S(2)}) copy-start(bf16[64,2048]{1,0:T(8,128)(2,1)} %x_ref.1) | copy-start | bytes 786436
  0.0 19.8 %copy-start = (bf16[8,4,256,256]{3,2,1,0:T(8,128)(2,1)S(1)}, bf16[8,4,256,256]{3,2,1,0:T(8,128)(2,1)}, u32[]{:S(2)}) copy-start(bf16[8,4,256,256]{3,2,1,0:T(8,128)(2,1)} %near_blocks_ref.1) | copy-start | bytes 12582916
  0.0 19.8 %copy-start.1 = (bf16[8,16,64,64]{3,2,1,0:T(8,128)(2,1)S(1)}, bf16[8,16,64,64]{3,2,1,0:T(8,128)(2,1)}, u32[]{:S(2)}) copy-start(bf16[8,16,64,64]{3,2,1,0:T(8,128)(2,1)} %far_blocks_ref.1) | copy-start | bytes 3145732
  1.9 8.8 %collective-permute-start = (bf16[12,64,128]{2,1,0:T(8,128)(2,1)S(1)}, bf16[12,64,128]{2,1,0:T(8,128)(2,1)S(1)}, u32[]{:S(2)}, u32[]{:S(2)}) collective-permute-start(bf16[12,64,128]{2,1,0:T(8,128)(2,1)S(1)} %get-tuple-element.16.own_ref), channel_id=1, source_target_pairs={{0,4},{1,13},{2,6},{3,15},{4,0},{5,9},{6,2},{7,11},{8,12},{9,5},{1... | collective-permute-start | bytes 589832 | tf_op jit(solution)/shard_map/ppermute | solution.py:329
  5.0 2.2 %collective-permute-start.1 = (bf16[8,64,128]{2,1,0:T(8,128)(2,1)S(1)}, bf16[8,64,128]{2,1,0:T(8,128)(2,1)S(1)}, u32[]{:S(2)}, u32[]{:S(2)}) collective-permute-start(bf16[8,64,128]{2,1,0:T(8,128)(2,1)S(1)} %get-tuple-element.17), channel_id=1, source_target_pairs={{1,9},{3,11},{5,13},{7,15},{9,1},{11,3},{13,5},{15,7},{17,25},{19,... | collective-permute-start | bytes 393224 | tf_op jit(solution)/shard_map/ppermute | solution.py:329
  5.7 8.5 %collective-permute-start.5 = (bf16[8,64,128]{2,1,0:T(8,128)(2,1)S(1)}, bf16[8,64,128]{2,1,0:T(8,128)(2,1)S(1)}, u32[]{:S(2)}, u32[]{:S(2)}) collective-permute-start(bf16[8,64,128]{2,1,0:T(8,128)(2,1)S(1)} %get-tuple-element.22.p_own), channel_id=1, source_target_pairs={{0,2},{1,3},{2,0},{3,1},{4,6},{5,7},{6,4},{7,5},{8,10},{9,11},{10,... | collective-permute-start | bytes 393224 | tf_op jit(solution)/shard_map/ppermute | solution.py:329
  10.8 7.1 %collective-permute-start.2 = (bf16[12,64,128]{2,1,0:T(8,128)(2,1)S(1)}, bf16[12,64,128]{2,1,0:T(8,128)(2,1)S(1)}, u32[]{:S(2)}, u32[]{:S(2)}) collective-permute-start(bf16[12,64,128]{2,1,0:T(8,128)(2,1)S(1)} %collective-permute-done.a_ref), channel_id=1, source_target_pairs={{0,1},{1,0},{2,3},{3,2},{4,5},{5,4},{6,7},{7,6},{8,9},{9,8},{10,11... | collective-permute-start | bytes 589832 | tf_op jit(solution)/shard_map/ppermute | solution.py:329
  14.1 1.8 %collective-permute-start.4 = (bf16[8,64,128]{2,1,0:T(8,128)(2,1)S(1)}, bf16[8,64,128]{2,1,0:T(8,128)(2,1)S(1)}, u32[]{:S(2)}, u32[]{:S(2)}) collective-permute-start(bf16[8,64,128]{2,1,0:T(8,128)(2,1)S(1)} %get-tuple-element.22.p_own), channel_id=1, source_target_pairs={{0,1},{1,0},{2,3},{3,2},{4,5},{5,4},{6,7},{7,6},{8,9},{9,8},{10,11... | collective-permute-start | bytes 393224 | tf_op jit(solution)/shard_map/ppermute | solution.py:329
  14.1 1.8 %collective-permute-start.6 = (bf16[8,64,128]{2,1,0:T(8,128)(2,1)S(1)}, bf16[8,64,128]{2,1,0:T(8,128)(2,1)S(1)}, u32[]{:S(2)}, u32[]{:S(2)}) collective-permute-start(bf16[8,64,128]{2,1,0:T(8,128)(2,1)S(1)} %collective-permute-done.5.p_vec), channel_id=1, source_target_pairs={{0,1},{1,0},{2,3},{3,2},{4,5},{5,4},{6,7},{7,6},{8,9},{9,8},{10,11... | collective-permute-start | bytes 393224 | tf_op jit(solution)/shard_map/ppermute | solution.py:329
  14.6 3.2 %collective-permute-start.3 = (bf16[8,64,128]{2,1,0:T(8,128)(2,1)S(1)}, bf16[8,64,128]{2,1,0:T(8,128)(2,1)S(1)}, u32[]{:S(2)}, u32[]{:S(2)}) collective-permute-start(bf16[8,64,128]{2,1,0:T(8,128)(2,1)S(1)} %collective-permute-done.1.b_ref), channel_id=1, source_target_pairs={{1,0},{3,2},{5,4},{7,6},{9,8},{11,10},{13,12},{15,14},{17,16},{19,... | collective-permute-start | bytes 393224 | tf_op jit(solution)/shard_map/ppermute | solution.py:329
  19.0 3.2 %copy-start.3 = (bf16[8,64,256]{2,1,0:T(8,128)(2,1)S(1)}, bf16[8,64,256]{2,1,0:T(8,128)(2,1)}, u32[]{:S(2)}) copy-start(bf16[8,64,256]{2,1,0:T(8,128)(2,1)} %basis_ref.1) | copy-start | bytes 786436
  19.0 3.2 %copy-start.4 = (bf16[8,64,64]{2,1,0:T(8,128)(2,1)S(1)}, bf16[8,64,64]{2,1,0:T(8,128)(2,1)}, u32[]{:S(2)}) copy-start(bf16[8,64,64]{2,1,0:T(8,128)(2,1)} %transfer_ref.1) | copy-start | bytes 196612
  19.0 3.2 %collective-permute-start.7 = (bf16[64,128]{1,0:T(8,128)(2,1)S(1)}, bf16[64,128]{1,0:T(8,128)(2,1)S(1)}, u32[]{:S(2)}, u32[]{:S(2)}) collective-permute-start(bf16[64,128]{1,0:T(8,128)(2,1)S(1)} %coarse.1.down_ref), channel_id=1, source_target_pairs={{1,13},{2,6},{3,11},{5,9},{6,2},{7,15},{9,5},{10,14},{11,3},{13,1}... | collective-permute-start | bytes 49160 | tf_op jit(solution)/shard_map/ppermute | solution.py:329
  24.2 4.6 %collective-permute-start.8 = (bf16[2,16,2048]{2,1,0:T(8,128)(2,1)S(1)}, bf16[2,16,2048]{2,1,0:T(8,128)(2,1)S(1)}, u32[]{:S(2)}, u32[]{:S(2)}) collective-permute-start(bf16[2,16,2048]{2,1,0:T(8,128)(2,1)S(1)} %get-tuple-element.24), channel_id=1, source_target_pairs={{0,1},{1,0},{2,3},{3,2},{4,5},{5,4},{6,7},{7,6},{8,9},{9,8},{10,11... | collective-permute-start | bytes 393224 | tf_op jit(solution)/shard_map/ppermute | solution.py:329
  28.8 4.4 %collective-permute-start.9 = (bf16[16,2048]{1,0:T(8,128)(2,1)S(1)}, bf16[16,2048]{1,0:T(8,128)(2,1)S(1)}, u32[]{:S(2)}, u32[]{:S(2)}) collective-permute-start(bf16[16,2048]{1,0:T(8,128)(2,1)S(1)} %get-tuple-element.26), channel_id=1, source_target_pairs={{0,2},{1,3},{2,0},{3,1},{4,6},{5,7},{6,4},{7,5},{8,10},{9,11},{10,... | collective-permute-start | bytes 196616 | tf_op jit(solution)/shard_map/ppermute | solution.py:329

commit v4 on v3

--- a/solution.py
+++ b/solution.py
@@ -131,9 +131,9 @@
     return (far_out + near_sum).astype(jnp.bfloat16)
 
 
-def up_kernel(x_hbm, basis_hbm, transfer_hbm, coarse_hbm, parents_hbm,
+def up_kernel(x_hbm, basis_hbm, transfer_hbm, parents_hbm, coarse_hbm,
               msg_ref, short_ref, packed_ref,
-              x_ref, basis_ref, transfer_ref, coarse_ref, parents_ref, sums, sems):
+              x_ref, basis_ref, transfer_ref, parents_ref, coarse_ref, sums, sems):
     copies = [
         pltpu.make_async_copy(a, b, sems.at[i])
         for i, (a, b) in enumerate((
@@ -166,9 +166,10 @@
         msg_ref[p] = short_ref[p] = jnp.concatenate([ups[2 * p], ups[2 * p + 1]], axis=-1)
     copies[2].wait()
     copies[3].wait()
+    branches = [dot(ups[l], transfer_ref[l]) for l in range(leaves)]
     for l in range(leaves):
         parent = parents_ref[l]
-        sums[parent] = sums[parent] + dot(ups[l], transfer_ref[l])
+        sums[parent] = sums[parent] + branches[l]
     for p in range(clusters // 2):
         merged = jnp.concatenate([sums[2 * p], sums[2 * p + 1]], axis=-1).astype(BF)
         msg_ref[pairs + p] = short_ref[pairs + p] = merged
@@ -177,25 +178,37 @@
         packed_ref[j] = jnp.concatenate([coarse_ref[0, j], coarse_ref[1, j]], axis=-1)
 
 
-def coarse_kernel(sources_hbm, own_ref, a_ref, la_ref, b_ref, lb_ref,
-                  p_own, p_lvl, p_vec, p_diag, out_ref, sources_ref, table, sem):
+def gate_kernel(after_ref, out_ref):
+    out_ref[...] = jnp.zeros_like(out_ref)
+
+
+def join_kernel(a_ref, b_ref, gate_ref, out_ref):
+    count = a_ref.shape[0]
+    out_ref[:count] = a_ref[...]
+    out_ref[count:] = b_ref[...]
+
+
+def coarse_kernel(sources_hbm, own_ref, a_ref, b_ref, other_ref, p_own, p_lvl, out_ref,
+                  sources_ref, table, sem):
     copy = pltpu.make_async_copy(sources_hbm, sources_ref, sem)
     copy.start()
     share, rank, wide = p_own.shape
     vectors = out_ref.shape[0]
     pairs = table.shape[0] // 2
-    c = lax.axis_index("lvl")
-    me = lax.axis_index("vec") * 2 + c
+    count = a_ref.shape[0]
+    me = lax.axis_index("vec") * 2 + lax.axis_index("lvl")
     for p in range(pairs):
-        q = pairs + p
-        across = jnp.where(c == 1, b_ref[q].astype(F32), lb_ref[q].astype(F32))
-        total = (own_ref[q].astype(F32) + a_ref[q].astype(F32)) + (la_ref[q].astype(F32) + across)
+        q = b_ref.shape[0] - pairs + p
+        rest = b_ref[q].astype(F32) + other_ref[count + q].astype(F32)
+        total = (own_ref[q].astype(F32) + a_ref[q].astype(F32)) + (
+            other_ref[q].astype(F32) + rest
+        )
         table[p] = total.astype(BF)
         table[pairs + p] = swap_halves(total).astype(BF)
     low = low_half((vectors, wide))
     acc = jnp.zeros((2 * vectors, wide), F32)
     copy.wait()
-    for flip, blocks in enumerate((p_own, p_lvl, p_vec, p_diag)):
+    for flip, blocks in enumerate((p_own, p_lvl)):
         base = (me ^ flip) * share
         rows = []
         for cluster in range(2):
@@ -211,8 +224,34 @@
     out_ref[...] = jnp.where(low, acc[:vectors], acc[vectors:]).astype(BF)
 
 
-def local_kernel(near_hbm, far_hbm, own_ref, a_ref, la_ref, b_ref, lb_ref, x_ref,
-                 near_blocks_ref, far_blocks_ref, near_ref, far_ref,
+def near_rows(sources, owner, z, l, leaves, share):
+    return [sources[l, owner * share + j] - z * leaves + REACH for j in range(share)]
+
+
+def prep_kernel(near_hbm, x_ref, near_blocks_ref, transfer_ref, basis_ref,
+                near_ref, weight_ref, near_sources, panels, sem):
+    copy = pltpu.make_async_copy(near_hbm, near_sources, sem)
+    copy.start()
+    leaves, share, panel, _ = near_blocks_ref.shape
+    z = lax.axis_index("leaf")
+    owner = lax.axis_index("vec") * 2 + lax.axis_index("lvl")
+    for l in range(leaves):
+        panels[REACH + l] = x_ref[:, l * panel:(l + 1) * panel]
+    for l in range(leaves):
+        weight = lax.dot_general(
+            transfer_ref[l], basis_ref[l], (((0,), (0,)), ((), ())), preferred_element_type=F32
+        ).astype(BF)
+        weight_ref[l] = jnp.concatenate([weight, weight], axis=0)
+    copy.wait()
+    for l in range(REACH, leaves - REACH):
+        rows = [panels[i] for i in near_rows(near_sources, owner, z, l, leaves, share)]
+        near_ref[l - REACH] = dot(
+            jnp.concatenate(rows, axis=-1), near_blocks_ref[l].reshape(share * panel, panel)
+        )
+
+
+def local_kernel(near_hbm, far_hbm, own_ref, a_ref, b_ref, other_ref, x_ref,
+                 near_blocks_ref, far_blocks_ref, basis_ref, near_ref, total_ref,
                  near_sources, far_sources, panels, table, sems):
     copies = [
         pltpu.make_async_copy(near_hbm, near_sources, sems.at[0]),
@@ -226,83 +265,90 @@
     owner = lax.axis_index("vec") * 2 + c
     high = (z + c) % 2 == 0
     top, bottom = leaves + REACH, 0
-    at_a = jnp.where(high, top, bottom)
-    at_la = jnp.where(high, bottom, top)
+    at_mine = jnp.where(high, top, bottom)
+    at_other = jnp.where(high, bottom, top)
     lanes = a_ref.shape[2]
+    base = b_ref.shape[0]
     parts = panel // lanes
-    base = a_ref.shape[0] - REACH * parts
+    count = a_ref.shape[0]
     for i in range(REACH):
         for w in range(parts):
-            panels[at_a + i, :, w * lanes:(w + 1) * lanes] = a_ref[base + i * parts + w]
-            panels[at_la + i, :, w * lanes:(w + 1) * lanes] = la_ref[base + i * parts + w]
+            where = slice(w * lanes, (w + 1) * lanes)
+            panels[at_mine + i, :, where] = a_ref[base + i * parts + w]
+            panels[at_other + i, :, where] = other_ref[base + i * parts + w]
     for l in range(leaves):
         panels[REACH + l] = x_ref[:, l * panel:(l + 1) * panel]
     pairs = leaves // 2
-    far = jnp.where(c == 1, 3, 1)
-    near = jnp.where(c == 1, 1, 3)
-    count = 4 * pairs
+    at_a = jnp.where(c == 1, 3, 1) * pairs
+    at_o = jnp.where(c == 1, 1, 3) * pairs
+    half = 4 * pairs
     for p in range(pairs):
-        x = own_ref[p].astype(F32)
-        table[p] = own_ref[p]
-        table[count + p] = swap_halves(x).astype(BF)
-        x = a_ref[p].astype(F32)
-        table[far * pairs + p] = a_ref[p]
-        table[count + far * pairs + p] = swap_halves(x).astype(BF)
-        x = la_ref[p].astype(F32)
-        table[near * pairs + p] = la_ref[p]
-        table[count + near * pairs + p] = swap_halves(x).astype(BF)
-        x = jnp.where(c == 1, b_ref[p].astype(F32), lb_ref[p].astype(F32))
-        table[2 * pairs + p] = x.astype(BF)
-        table[count + 2 * pairs + p] = swap_halves(x).astype(BF)
+        third = b_ref[p].astype(F32) + other_ref[count + p].astype(F32)
+        for at, x in (
+            (p, own_ref[p].astype(F32)),
+            (2 * pairs + p, third),
+            (at_a + p, a_ref[p].astype(F32)),
+            (at_o + p, other_ref[p].astype(F32)),
+        ):
+            table[at] = x.astype(BF)
+            table[half + at] = swap_halves(x).astype(BF)
+    mask = z * leaves
     low = low_half((own_ref.shape[1], 2 * rank))
     for copy in copies:
         copy.wait()
-    for l in range(leaves):
-        rows = [
-            panels[near_sources[l, owner * near_share + j] - z * leaves + REACH]
-            for j in range(near_share)
-        ]
-        near_ref[l] = dot(
-            jnp.concatenate(rows, axis=-1), near_blocks_ref[l].reshape(near_share * panel, panel)
-        )
+    parts = []
+    for l in range(leaves):
         rows = []
         for j in range(0, far_share, 2):
             s0 = far_sources[l, owner * far_share + j]
             s1 = far_sources[l, owner * far_share + j + 1]
-            at0 = ((s0 // leaves) ^ z) * pairs + ((s0 % leaves) >> 1)
-            at1 = ((s1 // leaves) ^ z) * pairs + ((s1 % leaves) >> 1)
-            first = table[(s0 & 1) * count + at0]
-            second = table[(1 - (s1 & 1)) * count + at1]
+            first = table[((s0 ^ mask) >> 1) + (s0 & 1) * half]
+            second = table[((s1 ^ mask) >> 1) + half - (s1 & 1) * half]
             rows.append(jnp.where(low, first, second))
-        far_ref[l] = dot(
-            jnp.concatenate(rows, axis=-1), far_blocks_ref[l].reshape(far_share * rank, rank)
+        parts.append(
+            dot(jnp.concatenate(rows, axis=-1), far_blocks_ref[l].reshape(far_share * rank, rank))
         )
-
-
-def down_kernel(parents_hbm, near_ref, far_ref, down_ref, got_ref, transfer_ref, basis_ref,
-                send_ref, keep_ref, parents_ref, total, sem):
+    for l in range(leaves):
+        if REACH <= l < leaves - REACH:
+            close = near_ref[l - REACH]
+        else:
+            rows = [
+                panels[i] for i in near_rows(near_sources, owner, z, l, leaves, near_share)
+            ]
+            close = dot(
+                jnp.concatenate(rows, axis=-1),
+                near_blocks_ref[l].reshape(near_share * panel, panel),
+            )
+        total_ref[l] = close + dot(parts[l].astype(BF), basis_ref[l])
+
+
+def down_kernel(parents_hbm, total_ref, down_ref, first_ref, second_ref, weight_ref,
+                send_ref, keep_ref, parents_ref, halves, sem):
     copy = pltpu.make_async_copy(parents_hbm, parents_ref, sem)
     copy.start()
-    leaves, rank, panel = basis_ref.shape
-    z, v, c = lax.axis_index("leaf"), lax.axis_index("vec"), lax.axis_index("lvl")
-    lane = lax.broadcasted_iota(jnp.int32, down_ref.shape, 1)
-    distance = jnp.where(c == 1, jnp.where(v == 1, 2, 3), jnp.where(v == 1, 1, 0))
-    home = z ^ distance
-    down = jnp.where(distance == 0, down_ref[...].astype(F32), got_ref[...].astype(F32))
+    leaves, vectors, panel = total_ref.shape
+    z, c = lax.axis_index("leaf"), lax.axis_index("lvl")
+    low = low_half(down_ref.shape)
+    zero = jnp.zeros(down_ref.shape, F32)
+    own = down_ref[...].astype(F32)
+    first = first_ref[...].astype(F32)
+    second = second_ref[...].astype(F32)
+    parts = [(0, jnp.where(c == 0, own, zero)), (1, second),
+             (2, jnp.where(c == 0, first, zero)), (3, jnp.where(c == 0, zero, first))]
+    for distance, x in parts:
+        halves[2 * distance] = jnp.where(low, x, 0.0).astype(BF)
+        halves[2 * distance + 1] = jnp.where(low, 0.0, x).astype(BF)
+    rows = vectors // 4
     copy.wait()
     for l in range(leaves):
         parent = parents_ref[l]
-        begin = jnp.where((parent >> 1) == home, (parent & 1) * rank, -2 * rank)
-        pushed = jnp.where((lane >= begin) & (lane < begin + rank), down, 0.0).astype(BF)
-        weight = transfer_ref[l]
-        part = far_ref[l] + dot_t(pushed, jnp.concatenate([weight, weight], axis=-1))
-        total[:, l * panel:(l + 1) * panel] = near_ref[l] + dot(part.astype(BF), basis_ref[l])
-    rows = keep_ref.shape[1]
-    for w in range(2):
-        mine = pl.multiple_of((w * 2 + c) * rows, rows)
-        theirs = pl.multiple_of((w * 2 + 1 - c) * rows, rows)
-        keep_ref[w] = total[pl.ds(mine, rows), :]
-        send_ref[w] = total[pl.ds(theirs, rows), :].astype(BF)
+        part = total_ref[l] + dot(halves[parent ^ (2 * z)], weight_ref[l])
+        lanes = slice(l * panel, (l + 1) * panel)
+        for w in range(2):
+            even = part[2 * w * rows:(2 * w + 1) * rows]
+            odd = part[(2 * w + 1) * rows:(2 * w + 2) * rows]
+            keep_ref[w, :, lanes] = jnp.where(c == 0, even, odd)
+            send_ref[w, :, lanes] = jnp.where(c == 0, odd, even).astype(BF)
 
 
 def merge_kernel(keep_ref, got_ref, send_ref, rest_ref):
@@ -346,11 +392,11 @@
     vectors = adjoint_in.shape[0]
     leaves, rank, panel = row_basis.shape
     clusters = coarse_sources.shape[0] * 4
-    coarse_share = coarse_blocks.shape[1]
     width = leaves * panel
     params = pltpu.CompilerParams(vmem_limit_bytes=LIMIT)
     wide = 2 * rank
-    messages = leaves // 2 + clusters // 2 + REACH * panel // wide
+    messages = leaves // 2 + clusters // 2
+    edges = REACH * panel // wide
 
     def other_core(z, v, c):
         return z, v, 1 - c
@@ -361,8 +407,8 @@
     msg, short, packed = pl.pallas_call(
         up_kernel,
         out_shape=(
+            jax.ShapeDtypeStruct((messages + edges, vectors, wide), BF),
             jax.ShapeDtypeStruct((messages, vectors, wide), BF),
-            jax.ShapeDtypeStruct((leaves // 2 + clusters // 2, vectors, wide), BF),
             jax.ShapeDtypeStruct((coarse_blocks.shape[1], rank, wide), BF),
         ),
         in_specs=[HBM] * 5,
@@ -371,27 +417,59 @@
             pltpu.VMEM(adjoint_in.shape, BF),
             pltpu.VMEM(row_basis.shape, BF),
             pltpu.VMEM(row_transfer.shape, BF),
+            pltpu.SMEM(parents.shape, jnp.int32),
             pltpu.VMEM(coarse_blocks.shape, BF),
-            pltpu.SMEM(parents.shape, jnp.int32),
             pltpu.VMEM((clusters, vectors, rank), F32),
             pltpu.SemaphoreType.DMA((5,)),
         ],
         compiler_params=params,
         cost_estimate=cost(1.5),
         name="up",
-    )(*in_hbm(adjoint_in, row_basis, row_transfer, coarse_blocks, parents))
+    )(*in_hbm(adjoint_in, row_basis, row_transfer, parents, coarse_blocks))
     a = swap(msg, lambda z, v, c: (z ^ (3 if c else 1), v, c))
     b = swap(short, lambda z, v, c: (z ^ 2, v, c) if c else None)
     p_lvl = swap(packed, other_core)
-    p_vec = swap(packed, other_chip)
-    p_diag = swap(p_vec, other_core)
-    a, b = lax.optimization_barrier((a, b))
-    la = swap(a, other_core)
-    lb = swap(b, lambda z, v, c: (z, v, 0) if c else None)
+    near, weight = pl.pallas_call(
+        prep_kernel,
+        out_shape=(
+            jax.ShapeDtypeStruct((leaves - 2 * REACH, vectors, panel), F32),
+            jax.ShapeDtypeStruct((leaves, wide, panel), BF),
+        ),
+        in_specs=[HBM] + [VMEM] * 4,
+        out_specs=(VMEM,) * 2,
+        scratch_shapes=[
+            pltpu.SMEM(near_sources.shape, jnp.int32),
+            pltpu.VMEM((leaves + 2 * REACH, vectors, panel), BF),
+            pltpu.SemaphoreType.DMA(()),
+        ],
+        compiler_params=params,
+        cost_estimate=cost(1.5),
+        name="prep",
+    )(*in_hbm(near_sources), adjoint_in, near_blocks, col_transfer, col_basis)
+    gate = pl.pallas_call(
+        gate_kernel,
+        out_shape=jax.ShapeDtypeStruct((8, 128), F32),
+        in_specs=[pl.BlockSpec(memory_space=pl.ANY)],
+        out_specs=VMEM,
+        compiler_params=params,
+        cost_estimate=cost(0.1),
+        name="gate",
+    )(p_lvl)
+    joined = pl.pallas_call(
+        join_kernel,
+        out_shape=jax.ShapeDtypeStruct((2 * messages + edges, vectors, wide), BF),
+        in_specs=[VMEM] * 3,
+        out_specs=VMEM,
+        compiler_params=params,
+        cost_estimate=cost(0.5),
+        name="join",
+    )(a, b, gate)
+    joined, near, weight = lax.optimization_barrier((joined, near, weight))
+    other = swap(joined, other_core)
     down = pl.pallas_call(
         coarse_kernel,
         out_shape=jax.ShapeDtypeStruct((vectors, wide), BF),
-        in_specs=[HBM] + [VMEM] * 9,
+        in_specs=[HBM] + [VMEM] * 6,
         out_specs=VMEM,
         scratch_shapes=[
             pltpu.SMEM(coarse_sources.shape, jnp.int32),
@@ -401,21 +479,14 @@
         compiler_params=params,
         cost_estimate=cost(1.0),
         name="coarse",
-    )(*in_hbm(coarse_sources), msg, a, la, b, lb, packed, p_lvl, p_vec, p_diag)
-
-    def home(z, v, c):
-        distance = (2 if v else 3) if c else (1 if v else 0)
-        return (z ^ distance, v, c) if distance else None
-
-    got = swap(down, home)
-    near, far = pl.pallas_call(
+    )(coarse_sources, msg, a, b, other, packed, p_lvl)
+    first = swap(down, lambda z, v, c: (z ^ (3 if c else 2), v, c))
+    second = swap(down, lambda z, v, c: (z ^ 1, v, c) if c else None)
+    total = pl.pallas_call(
         local_kernel,
-        out_shape=(
-            jax.ShapeDtypeStruct((leaves, vectors, panel), F32),
-            jax.ShapeDtypeStruct((leaves, vectors, rank), F32),
-        ),
-        in_specs=[HBM] * 2 + [VMEM] * 8,
-        out_specs=(VMEM,) * 2,
+        out_shape=jax.ShapeDtypeStruct((leaves, vectors, panel), F32),
+        in_specs=[HBM] * 2 + [VMEM] * 9,
+        out_specs=VMEM,
         scratch_shapes=[
             pltpu.SMEM(near_sources.shape, jnp.int32),
             pltpu.SMEM(far_sources.shape, jnp.int32),
@@ -426,7 +497,10 @@
         compiler_params=params,
         cost_estimate=cost(4.0),
         name="local",
-    )(*in_hbm(near_sources, far_sources), msg, a, la, b, lb, adjoint_in, near_blocks, far_blocks)
+    )(
+        near_sources, far_sources,
+        msg, a, b, other, adjoint_in, near_blocks, far_blocks, col_basis, near,
+    )
     rows = vectors // 4
     send, keep = pl.pallas_call(
         down_kernel,
@@ -434,17 +508,17 @@
             jax.ShapeDtypeStruct((2, rows, width), BF),
             jax.ShapeDtypeStruct((2, rows, width), F32),
         ),
-        in_specs=[HBM] + [VMEM] * 6,
+        in_specs=[HBM] + [VMEM] * 5,
         out_specs=(VMEM,) * 2,
         scratch_shapes=[
             pltpu.SMEM(parents.shape, jnp.int32),
-            pltpu.VMEM((vectors, width), F32),
+            pltpu.VMEM((8, vectors, wide), BF),
             pltpu.SemaphoreType.DMA(()),
         ],
         compiler_params=params,
         cost_estimate=cost(1.0),
         name="down",
-    )(*in_hbm(parents), near, far, down, got, col_transfer, col_basis)
+    )(parents, total, down, first, second, weight)
     came = swap(send, other_core)
     send, rest = pl.pallas_call(
         merge_kernel,

time: 34.1 us -> 30.2 us (0.89)
  waiting for transfers between devices: 9.91 us -> 7.81 us
  starting transfers between devices: 15.8 us -> 14.6 us
  Pallas kernels: 7.29 us -> 6.79 us
    ppermute x10 -> x8, waiting for transfers between devices: 9.91 us -> 7.81 us  [swap(): return lax.ppermute(x, axes, pairs)]
    ppermute x10 -> x8, starting transfers between devices: 15.8 us -> 14.6 us  [swap(): return lax.ppermute(x, axes, pairs)]
    pallas_call x1, Pallas kernels: 1.96 us -> 0.78 us  [on_device_paired(): pl.pallas_call(down_kernel, out_shape=(jax.ShapeDtypeStruct((2, rows, wid...]
    pallas_call x2 -> x5, Pallas kernels: 4.21 us -> 5.14 us  [the longest x1 1.98 us: on_device_paired(): pl.pallas_call(local_kernel, out_shape=jax.ShapeDtypeStruct((leaves, vect...]
  transfers between devices with their start and end apart: 10 -> 8, of which waited for: 4 -> 5; matrix products, arithmetic and copies ran while one was open for 0% -> 0% of each run, Pallas kernels for 7% -> 11%
where the time goes in v4:
time: 30.2 us; the launch traced here: 30 us
  starting transfers between devices  14.6 us (48%)
  waiting for transfers between devices  7.81 us (26%)
  Pallas kernels  6.79 us (22%)
  other arithmetic  0.64 us (2%)
    ppermute x8, starting transfers between devices, swap(): return lax.ppermute(x, axes, pairs)  14.6 us
    ppermute x8, waiting for transfers between devices, swap(): return lax.ppermute(x, axes, pairs)  7.81 us
    pallas_call x1, Pallas kernels, on_device_paired(): pl.pallas_call(local_kernel, out_shape=jax.ShapeDtypeStruct((leaves, vect...  1.98 us
    pallas_call x1, Pallas kernels, on_device_paired(): pl.pallas_call(up_kernel, out_shape=(jax.ShapeDtypeStruct((messages + edg...  1.89 us
    pallas_call x1, Pallas kernels, on_device_paired(): pl.pallas_call(prep_kernel, out_shape=(jax.ShapeDtypeStruct((leaves - 2 *...  1.24 us
    pallas_call x1, Pallas kernels, on_device_paired(): pl.pallas_call(coarse_kernel, out_shape=jax.ShapeDtypeStruct((vectors, wi...  0.84 us
    pallas_call x1, Pallas kernels, on_device_paired(): pl.pallas_call(down_kernel, out_shape=(jax.ShapeDtypeStruct((2, rows, wid...  0.78 us
    convert_element_type x1, other arithmetic, on_device_paired(): return (rest + came.astype(F32)).astype(BF)  0.64 us
  transfers between devices with their start and end apart: 8, of which 5 were waited for; matrix products, arithmetic and copies ran while one was open for 0% of the time, Pallas kernels for 11%

profile of v4, /device:TPU:0, one launch (start us, length us, event | category | flops | bytes accessed | tf_op | source)
XLA Modules:
  0.0 30.0 jit_solution(4509058306679723112)
XLA Ops:
  0.0 0.0 copy-start.2
  0.0 0.0 copy-start
  0.0 0.0 copy-start.3
  0.0 0.0 copy-start.4
  0.0 1.9 %up.1 = (bf16[12,64,128]{2,1,0:T(8,128)(2,1)S(1)}, bf16[8,64,128]{2,1,0:T(8,128)(2,1)S(1)}, bf16[8,64,128]{2,1,0:T(8,128)(2,1)S(1)}) custom-call(bf16[64,2048]{1,0:T(8,128)(2,1)} %x_ref.3, bf16[8,64,256]{2,1,0:T(8,128)(2,1)} %basis_hbm.1, bf16[8,64,64]{2,1,0:T(8,128)(2,1)} %transfer_hbm.1, s32[8]{0:T(128)} %parents_hbm.3, bf16[2,8,64,64]{3,2,1,0:T(8,128)(2,1)} %coarse_hbm.1), custom_call_target="tpu_custom_call" | custom-call | flops 1500000000 | bytes 1024 | tf_op jit(solution)/shard_map/up/pallas_call | solution.py:407
  1.9 0.0 copy-start.7
  1.9 3.1 %collective-permute-start = (bf16[12,64,128]{2,1,0:T(8,128)(2,1)S(1)}, bf16[12,64,128]{2,1,0:T(8,128)(2,1)S(1)}, u32[]{:S(2)}, u32[]{:S(2)}) collective-permute-start(bf16[12,64,128]{2,1,0:T(8,128)(2,1)S(1)} %get-tuple-element.17.own_ref), channel_id=1, source_target_pairs={{0,4},{1,13},{2,6},{3,15},{4,0},{5,9},{6,2},{7,11},{8,12},{9,5},{1... | collective-permute-start | bytes 589832 | tf_op jit(solution)/shard_map/ppermute | solution.py:375
  5.0 0.7 %collective-permute-start.1 = (bf16[8,64,128]{2,1,0:T(8,128)(2,1)S(1)}, bf16[8,64,128]{2,1,0:T(8,128)(2,1)S(1)}, u32[]{:S(2)}, u32[]{:S(2)}) collective-permute-start(bf16[8,64,128]{2,1,0:T(8,128)(2,1)S(1)} %get-tuple-element.18), channel_id=1, source_target_pairs={{1,9},{3,11},{5,13},{7,15},{9,1},{11,3},{13,5},{15,7},{17,25},{19,... | collective-permute-start | bytes 393224 | tf_op jit(solution)/shard_map/ppermute | solution.py:375
  5.7 2.9 %collective-permute-start.2 = (bf16[8,64,128]{2,1,0:T(8,128)(2,1)S(1)}, bf16[8,64,128]{2,1,0:T(8,128)(2,1)S(1)}, u32[]{:S(2)}, u32[]{:S(2)}) collective-permute-start(bf16[8,64,128]{2,1,0:T(8,128)(2,1)S(1)} %get-tuple-element.19.p_own), channel_id=1, source_target_pairs={{0,1},{1,0},{2,3},{3,2},{4,5},{5,4},{6,7},{7,6},{8,9},{9,8},{10,11... | collective-permute-start | bytes 393224 | tf_op jit(solution)/shard_map/ppermute | solution.py:375
  8.6 0.0 copy-done.2
  8.6 0.0 copy-done
  8.6 0.0 copy-done.3
  8.6 0.0 copy-done.4
  8.6 1.2 %prep.1 = (f32[4,64,256]{2,1,0:T(8,128)S(1)}, bf16[8,128,256]{2,1,0:T(8,128)(2,1)S(1)}) custom-call(s32[8,16]{1,0:T(8,128)} %near_hbm.3, bf16[64,2048]{1,0:T(8,128)(2,1)S(1)} %copy-done.2, bf16[8,4,256,256]{3,2,1,0:T(8,128)(2,1)S(1)} %copy-done, bf16[8,64,64]{2,1,0:T(8,128)(2,1)S(1)} %copy-done.4, bf16[8,64,256]{2,1,0:T(8,128)(2,1)S(1)} %copy-done.3), custom_call_target="tpu_custom_call" | custom-call | flops 1500000000 | bytes 1024 | tf_op jit(solution)/shard_map/prep/pallas_call | solution.py:432
  9.8 0.0 copy-start.1
  9.9 0.0 copy-start.5
  9.9 0.0 copy-start.6
  9.9 0.0 collective-permute-done.2.after_ref.p_lvl
  9.9 0.0 collective-permute-done.1.b_ref
  9.9 0.9 %collective-permute-done.a_ref = bf16[12,64,128]{2,1,0:T(8,128)(2,1)S(1)} collective-permute-done((bf16[12,64,128]{2,1,0:T(8,128)(2,1)S(1)}, bf16[12,64,128]{2,1,0:T(8,128)(2,1)S(1)}, u32[]{:S(2)}, u32[]{:S(2)}) %collective-permute-start) | collective-permute-done | bytes 196640 | tf_op jit(solution)/shard_map/ppermute | solution.py:375
  10.8 3.4 %collective-permute-start.3 = (bf16[20,64,128]{2,1,0:T(8,128)(2,1)S(1)}, bf16[20,64,128]{2,1,0:T(8,128)(2,1)S(1)}, u32[]{:S(2)}, u32[]{:S(2)}) collective-permute-start(bf16[20,64,128]{2,1,0:T(8,128)(2,1)S(1)} %join.1), channel_id=1, source_target_pairs={{0,1},{1,0},{2,3},{3,2},{4,5},{5,4},{6,7},{7,6},{8,9},{9,8},{10,11... | collective-permute-start | bytes 983048 | tf_op jit(solution)/shard_map/ppermute | solution.py:375
  14.2 1.3 %collective-permute-done.3.other_ref = bf16[20,64,128]{2,1,0:T(8,128)(2,1)S(1)} collective-permute-done((bf16[20,64,128]{2,1,0:T(8,128)(2,1)S(1)}, bf16[20,64,128]{2,1,0:T(8,128)(2,1)S(1)}, u32[]{:S(2)}, u32[]{:S(2)}) %collective-permute-start.3) | collective-permute-done | bytes 327712 | tf_op jit(solution)/shard_map/ppermute | solution.py:375
  15.5 0.0 copy-done.7
  15.5 0.8 %coarse.1.down_ref = bf16[64,128]{1,0:T(8,128)(2,1)S(1)} custom-call(s32[2,32]{1,0:T(2,128)S(1)} %copy-done.7, bf16[12,64,128]{2,1,0:T(8,128)(2,1)S(1)} %get-tuple-element.17.own_ref, bf16[12,64,128]{2,1,0:T(8,128)(2,1)S(1)} %collective-permute-done.a_ref, bf16[8,64,128]{2,1,0:T(8,128)(2,1)S(1)} %collective-permute-done.1.b_ref, ...), custom_call_target="tpu_custom_call" | custom-call | flops 1000000000 | bytes 1024 | tf_op jit(solution)/shard_map/coarse/pallas_call | solution.py:469
  16.3 0.0 copy-start.8
  16.4 0.7 %collective-permute-start.5 = (bf16[64,128]{1,0:T(8,128)(2,1)S(1)}, bf16[64,128]{1,0:T(8,128)(2,1)S(1)}, u32[]{:S(2)}, u32[]{:S(2)}) collective-permute-start(bf16[64,128]{1,0:T(8,128)(2,1)S(1)} %coarse.1.down_ref), channel_id=1, source_target_pairs={{1,5},{3,7},{5,1},{7,3},{9,13},{11,15},{13,9},{15,11},{17,21},{19,... | collective-permute-start | bytes 49160 | tf_op jit(solution)/shard_map/ppermute | solution.py:375
  17.0 0.9 %collective-permute-start.4 = (bf16[64,128]{1,0:T(8,128)(2,1)S(1)}, bf16[64,128]{1,0:T(8,128)(2,1)S(1)}, u32[]{:S(2)}, u32[]{:S(2)}) collective-permute-start(bf16[64,128]{1,0:T(8,128)(2,1)S(1)} %coarse.1.down_ref), channel_id=1, source_target_pairs={{0,8},{1,13},{2,10},{3,15},{4,12},{5,9},{6,14},{7,11},{8,0},{9,5},... | collective-permute-start | bytes 49160 | tf_op jit(solution)/shard_map/ppermute | solution.py:375
  17.9 0.0 copy-done.1
  17.9 0.0 copy-done.5
  17.9 0.0 copy-done.6
  17.9 2.0 %local.1.total_ref = f32[8,64,256]{2,1,0:T(8,128)S(1)} custom-call(s32[8,16]{1,0:T(8,128)S(1)} %copy-done.5, s32[8,64]{1,0:T(8,128)S(1)} %copy-done.6, bf16[12,64,128]{2,1,0:T(8,128)(2,1)S(1)} %get-tuple-element.17.own_ref, bf16[12,64,128]{2,1,0:T(8,128)(2,1)S(1)} %collective-permute-done.a_ref, bf16[8,64,128]{2,1,0:T(8,128)(2,1)S(1)} %collective-permute-done.1.b_ref, ...), custom_call_target="tpu_custom_call" | custom-call | flops 4000000000 | bytes 1024 | tf_op jit(solution)/shard_map/local/pallas_call | solution.py:485
  19.9 0.0 collective-permute-done.5.second_ref
  19.9 1.8 %collective-permute-done.4.first_ref = bf16[64,128]{1,0:T(8,128)(2,1)S(1)} collective-permute-done((bf16[64,128]{1,0:T(8,128)(2,1)S(1)}, bf16[64,128]{1,0:T(8,128)(2,1)S(1)}, u32[]{:S(2)}, u32[]{:S(2)}) %collective-permute-start.4) | collective-permute-done | bytes 16416 | tf_op jit(solution)/shard_map/ppermute | solution.py:375
  21.7 0.0 copy-done.8
  21.7 0.8 %down.1 = (bf16[2,16,2048]{2,1,0:T(8,128)(2,1)S(1)}, f32[2,16,2048]{2,1,0:T(8,128)S(1)}) custom-call(s32[8]{0:T(128)S(1)} %copy-done.8, f32[8,64,256]{2,1,0:T(8,128)S(1)} %local.1.total_ref, bf16[64,128]{1,0:T(8,128)(2,1)S(1)} %coarse.1.down_ref, bf16[64,128]{1,0:T(8,128)(2,1)S(1)} %collective-permute-done.4.first_ref, ...), custom_call_target="tpu_custom_call" | custom-call | flops 1000000000 | bytes 1024 | tf_op jit(solution)/shard_map/down/pallas_call | solution.py:505
  22.5 1.4 %collective-permute-start.6 = (bf16[2,16,2048]{2,1,0:T(8,128)(2,1)S(1)}, bf16[2,16,2048]{2,1,0:T(8,128)(2,1)S(1)}, u32[]{:S(2)}, u32[]{:S(2)}) collective-permute-start(bf16[2,16,2048]{2,1,0:T(8,128)(2,1)S(1)} %get-tuple-element.26), channel_id=1, source_target_pairs={{0,1},{1,0},{2,3},{3,2},{4,5},{5,4},{6,7},{7,6},{8,9},{9,8},{10,11... | collective-permute-start | bytes 393224 | tf_op jit(solution)/shard_map/ppermute | solution.py:375
  24.0 1.0 %collective-permute-done.6.got_ref = bf16[2,16,2048]{2,1,0:T(8,128)(2,1)S(1)} collective-permute-done((bf16[2,16,2048]{2,1,0:T(8,128)(2,1)S(1)}, bf16[2,16,2048]{2,1,0:T(8,128)(2,1)S(1)}, u32[]{:S(2)}, u32[]{:S(2)}) %collective-permute-start.6) | collective-permute-done | bytes 131104 | tf_op jit(solution)/shard_map/ppermute | solution.py:375
  25.0 1.6 %collective-permute-start.7 = (bf16[16,2048]{1,0:T(8,128)(2,1)S(1)}, bf16[16,2048]{1,0:T(8,128)(2,1)S(1)}, u32[]{:S(2)}, u32[]{:S(2)}) collective-permute-start(bf16[16,2048]{1,0:T(8,128)(2,1)S(1)} %get-tuple-element.28), channel_id=1, source_target_pairs={{0,2},{1,3},{2,0},{3,1},{4,6},{5,7},{6,4},{7,5},{8,10},{9,11},{10,... | collective-permute-start | bytes 196616 | tf_op jit(solution)/shard_map/ppermute | solution.py:375
  26.5 2.9 %collective-permute-done.7 = bf16[16,2048]{1,0:T(8,128)(2,1)S(1)} collective-permute-done((bf16[16,2048]{1,0:T(8,128)(2,1)S(1)}, bf16[16,2048]{1,0:T(8,128)(2,1)S(1)}, u32[]{:S(2)}, u32[]{:S(2)}) %collective-permute-start.7) | collective-permute-done | bytes 65568 | tf_op jit(solution)/shard_map/ppermute | solution.py:375
  29.4 0.6 %add_convert_fusion = bf16[16,2048]{1,0:T(8,128)(2,1)} fusion(f32[16,2048]{1,0:T(8,128)S(1)} %get-tuple-element.27, bf16[16,2048]{1,0:T(8,128)(2,1)S(1)} %collective-permute-done.7), kind=kLoop, calls=%fused_computation | loop fusion | flops 98304 | bytes 262144 | tf_op jit(solution)/shard_map/convert_element_type | solution.py:536
  (3 shorter events, 0.1 us)
Async XLA Ops:
  0.0 8.6 %copy-start.2 = (bf16[64,2048]{1,0:T(8,128)(2,1)S(1)}, bf16[64,2048]{1,0:T(8,128)(2,1)}, u32[]{:S(2)}) copy-start(bf16[64,2048]{1,0:T(8,128)(2,1)} %x_ref.3) | copy-start | bytes 786436
  0.0 8.6 %copy-start = (bf16[8,4,256,256]{3,2,1,0:T(8,128)(2,1)S(1)}, bf16[8,4,256,256]{3,2,1,0:T(8,128)(2,1)}, u32[]{:S(2)}) copy-start(bf16[8,4,256,256]{3,2,1,0:T(8,128)(2,1)} %near_blocks_ref.3) | copy-start | bytes 12582916
  0.0 8.6 %copy-start.3 = (bf16[8,64,256]{2,1,0:T(8,128)(2,1)S(1)}, bf16[8,64,256]{2,1,0:T(8,128)(2,1)}, u32[]{:S(2)}) copy-start(bf16[8,64,256]{2,1,0:T(8,128)(2,1)} %basis_ref.3) | copy-start | bytes 786436
  0.0 8.6 %copy-start.4 = (bf16[8,64,64]{2,1,0:T(8,128)(2,1)S(1)}, bf16[8,64,64]{2,1,0:T(8,128)(2,1)}, u32[]{:S(2)}) copy-start(bf16[8,64,64]{2,1,0:T(8,128)(2,1)} %transfer_ref.1) | copy-start | bytes 196612
  1.9 13.6 %copy-start.7 = (s32[2,32]{1,0:T(2,128)S(1)}, s32[2,32]{1,0:T(2,128)}, u32[]{:S(2)}) copy-start(s32[2,32]{1,0:T(2,128)} %sources_hbm.1) | copy-start | bytes 772
  1.9 8.9 %collective-permute-start = (bf16[12,64,128]{2,1,0:T(8,128)(2,1)S(1)}, bf16[12,64,128]{2,1,0:T(8,128)(2,1)S(1)}, u32[]{:S(2)}, u32[]{:S(2)}) collective-permute-start(bf16[12,64,128]{2,1,0:T(8,128)(2,1)S(1)} %get-tuple-element.17.own_ref), channel_id=1, source_target_pairs={{0,4},{1,13},{2,6},{3,15},{4,0},{5,9},{6,2},{7,11},{8,12},{9,5},{1... | collective-permute-start | bytes 589832 | tf_op jit(solution)/shard_map/ppermute | solution.py:375
  5.0 4.9 %collective-permute-start.1 = (bf16[8,64,128]{2,1,0:T(8,128)(2,1)S(1)}, bf16[8,64,128]{2,1,0:T(8,128)(2,1)S(1)}, u32[]{:S(2)}, u32[]{:S(2)}) collective-permute-start(bf16[8,64,128]{2,1,0:T(8,128)(2,1)S(1)} %get-tuple-element.18), channel_id=1, source_target_pairs={{1,9},{3,11},{5,13},{7,15},{9,1},{11,3},{13,5},{15,7},{17,25},{19,... | collective-permute-start | bytes 393224 | tf_op jit(solution)/shard_map/ppermute | solution.py:375
  5.7 4.2 %collective-permute-start.2 = (bf16[8,64,128]{2,1,0:T(8,128)(2,1)S(1)}, bf16[8,64,128]{2,1,0:T(8,128)(2,1)S(1)}, u32[]{:S(2)}, u32[]{:S(2)}) collective-permute-start(bf16[8,64,128]{2,1,0:T(8,128)(2,1)S(1)} %get-tuple-element.19.p_own), channel_id=1, source_target_pairs={{0,1},{1,0},{2,3},{3,2},{4,5},{5,4},{6,7},{7,6},{8,9},{9,8},{10,11... | collective-permute-start | bytes 393224 | tf_op jit(solution)/shard_map/ppermute | solution.py:375
  9.8 8.0 %copy-start.1 = (bf16[8,16,64,64]{3,2,1,0:T(8,128)(2,1)S(1)}, bf16[8,16,64,64]{3,2,1,0:T(8,128)(2,1)}, u32[]{:S(2)}) copy-start(bf16[8,16,64,64]{3,2,1,0:T(8,128)(2,1)} %far_blocks_ref.1) | copy-start | bytes 3145732
  9.9 8.0 %copy-start.5 = (s32[8,16]{1,0:T(8,128)S(1)}, s32[8,16]{1,0:T(8,128)}, u32[]{:S(2)}) copy-start(s32[8,16]{1,0:T(8,128)} %near_hbm.3) | copy-start | bytes 1540
  9.9 8.0 %copy-start.6 = (s32[8,64]{1,0:T(8,128)S(1)}, s32[8,64]{1,0:T(8,128)}, u32[]{:S(2)}) copy-start(s32[8,64]{1,0:T(8,128)} %far_hbm.1) | copy-start | bytes 6148
  10.8 4.7 %collective-permute-start.3 = (bf16[20,64,128]{2,1,0:T(8,128)(2,1)S(1)}, bf16[20,64,128]{2,1,0:T(8,128)(2,1)S(1)}, u32[]{:S(2)}, u32[]{:S(2)}) collective-permute-start(bf16[20,64,128]{2,1,0:T(8,128)(2,1)S(1)} %join.1), channel_id=1, source_target_pairs={{0,1},{1,0},{2,3},{3,2},{4,5},{5,4},{6,7},{7,6},{8,9},{9,8},{10,11... | collective-permute-start | bytes 983048 | tf_op jit(solution)/shard_map/ppermute | solution.py:375
  16.3 5.4 %copy-start.8 = (s32[8]{0:T(128)S(1)}, s32[8]{0:T(128)}, u32[]{:S(2)}) copy-start(s32[8]{0:T(128)} %parents_hbm.3) | copy-start | bytes 100
  16.4 3.5 %collective-permute-start.5 = (bf16[64,128]{1,0:T(8,128)(2,1)S(1)}, bf16[64,128]{1,0:T(8,128)(2,1)S(1)}, u32[]{:S(2)}, u32[]{:S(2)}) collective-permute-start(bf16[64,128]{1,0:T(8,128)(2,1)S(1)} %coarse.1.down_ref), channel_id=1, source_target_pairs={{1,5},{3,7},{5,1},{7,3},{9,13},{11,15},{13,9},{15,11},{17,21},{19,... | collective-permute-start | bytes 49160 | tf_op jit(solution)/shard_map/ppermute | solution.py:375
  17.0 4.7 %collective-permute-start.4 = (bf16[64,128]{1,0:T(8,128)(2,1)S(1)}, bf16[64,128]{1,0:T(8,128)(2,1)S(1)}, u32[]{:S(2)}, u32[]{:S(2)}) collective-permute-start(bf16[64,128]{1,0:T(8,128)(2,1)S(1)} %coarse.1.down_ref), channel_id=1, source_target_pairs={{0,8},{1,13},{2,10},{3,15},{4,12},{5,9},{6,14},{7,11},{8,0},{9,5},... | collective-permute-start | bytes 49160 | tf_op jit(solution)/shard_map/ppermute | solution.py:375
  22.5 2.4 %collective-permute-start.6 = (bf16[2,16,2048]{2,1,0:T(8,128)(2,1)S(1)}, bf16[2,16,2048]{2,1,0:T(8,128)(2,1)S(1)}, u32[]{:S(2)}, u32[]{:S(2)}) collective-permute-start(bf16[2,16,2048]{2,1,0:T(8,128)(2,1)S(1)} %get-tuple-element.26), channel_id=1, source_target_pairs={{0,1},{1,0},{2,3},{3,2},{4,5},{5,4},{6,7},{7,6},{8,9},{9,8},{10,11... | collective-permute-start | bytes 393224 | tf_op jit(solution)/shard_map/ppermute | solution.py:375
  25.0 4.4 %collective-permute-start.7 = (bf16[16,2048]{1,0:T(8,128)(2,1)S(1)}, bf16[16,2048]{1,0:T(8,128)(2,1)S(1)}, u32[]{:S(2)}, u32[]{:S(2)}) collective-permute-start(bf16[16,2048]{1,0:T(8,128)(2,1)S(1)} %get-tuple-element.28), channel_id=1, source_target_pairs={{0,2},{1,3},{2,0},{3,1},{4,6},{5,7},{6,4},{7,5},{8,10},{9,11},{10,... | collective-permute-start | bytes 196616 | tf_op jit(solution)/shard_map/ppermute | solution.py:375

commit v5 on v4

--- a/solution.py
+++ b/solution.py
@@ -178,71 +178,79 @@
         packed_ref[j] = jnp.concatenate([coarse_ref[0, j], coarse_ref[1, j]], axis=-1)
 
 
-def gate_kernel(after_ref, out_ref):
-    out_ref[...] = jnp.zeros_like(out_ref)
-
-
-def join_kernel(a_ref, b_ref, gate_ref, out_ref):
+def join_kernel(a_ref, b_ref, after_ref, out_ref):
     count = a_ref.shape[0]
     out_ref[:count] = a_ref[...]
     out_ref[count:] = b_ref[...]
 
 
-def coarse_kernel(sources_hbm, own_ref, a_ref, b_ref, other_ref, p_own, p_lvl, out_ref,
-                  sources_ref, table, sem):
-    copy = pltpu.make_async_copy(sources_hbm, sources_ref, sem)
-    copy.start()
-    share, rank, wide = p_own.shape
-    vectors = out_ref.shape[0]
-    pairs = table.shape[0] // 2
+def coarse_kernel(own_ref, a_ref, b_ref, other_ref, mix_ref, out_ref):
+    clusters, rank, wide = mix_ref.shape
     count = a_ref.shape[0]
-    me = lax.axis_index("vec") * 2 + lax.axis_index("lvl")
-    for p in range(pairs):
-        q = b_ref.shape[0] - pairs + p
+    lanes = []
+    for q in range(b_ref.shape[0] - clusters // 2, b_ref.shape[0]):
         rest = b_ref[q].astype(F32) + other_ref[count + q].astype(F32)
         total = (own_ref[q].astype(F32) + a_ref[q].astype(F32)) + (
             other_ref[q].astype(F32) + rest
         )
-        table[p] = total.astype(BF)
-        table[pairs + p] = swap_halves(total).astype(BF)
-    low = low_half((vectors, wide))
-    acc = jnp.zeros((2 * vectors, wide), F32)
-    copy.wait()
-    for flip, blocks in enumerate((p_own, p_lvl)):
-        base = (me ^ flip) * share
-        rows = []
-        for cluster in range(2):
-            lanes = []
-            for j in range(0, share, 2):
-                s0 = sources_ref[cluster, base + j]
-                s1 = sources_ref[cluster, base + j + 1]
-                first = table[(s0 & 1) * pairs + (s0 >> 1)]
-                second = table[(1 - (s1 & 1)) * pairs + (s1 >> 1)]
-                lanes.append(jnp.where(low, first, second))
-            rows.append(jnp.concatenate(lanes, axis=-1))
-        acc = acc + dot(jnp.concatenate(rows, axis=0), blocks[...].reshape(share * rank, wide))
-    out_ref[...] = jnp.where(low, acc[:vectors], acc[vectors:]).astype(BF)
+        lanes.append(total.astype(BF))
+    out_ref[...] = dot(
+        jnp.concatenate(lanes, axis=-1), mix_ref[...].reshape(clusters * rank, wide)
+    ).astype(BF)
 
 
 def near_rows(sources, owner, z, l, leaves, share):
     return [sources[l, owner * share + j] - z * leaves + REACH for j in range(share)]
 
 
-def prep_kernel(near_hbm, x_ref, near_blocks_ref, transfer_ref, basis_ref,
-                near_ref, weight_ref, near_sources, panels, sem):
-    copy = pltpu.make_async_copy(near_hbm, near_sources, sem)
+def mix_kernel(coarse_hbm, p_own, p_lvl, mix_ref, coarse_sources, sums, sem):
+    copy = pltpu.make_async_copy(coarse_hbm, coarse_sources, sem)
     copy.start()
+    share, rank, wide = p_own.shape
+    owner = lax.axis_index("vec") * 2 + lax.axis_index("lvl")
+    sums[...] = jnp.zeros_like(sums)
+    low = low_half((rank, wide))
+    copy.wait()
+    for flip, blocks in ((0, p_own), (1, p_lvl)):
+        base = (owner ^ flip) * share
+        for j in range(share):
+            block = blocks[j].astype(F32)
+            for cluster, part in ((0, jnp.where(low, block, 0.0)), (1, jnp.where(low, 0.0, block))):
+                source = coarse_sources[cluster, base + j]
+                sums[source] = sums[source] + part
+    mix_ref[...] = sums[...].astype(BF)
+
+
+def prep_kernel(near_hbm, parents_hbm, x_ref, near_blocks_ref, transfer_ref, basis_ref,
+                near_ref, weight_ref, near_sources, parents_ref, panels, sems):
+    copies = [
+        pltpu.make_async_copy(a, b, sems.at[i])
+        for i, (a, b) in enumerate((
+            (near_hbm, near_sources), (parents_hbm, parents_ref)
+        ))
+    ]
+    for copy in copies:
+        copy.start()
     leaves, share, panel, _ = near_blocks_ref.shape
-    z = lax.axis_index("leaf")
-    owner = lax.axis_index("vec") * 2 + lax.axis_index("lvl")
+    z, c = lax.axis_index("leaf"), lax.axis_index("lvl")
+    owner = lax.axis_index("vec") * 2 + c
+    weight_ref[...] = jnp.zeros_like(weight_ref)
     for l in range(leaves):
         panels[REACH + l] = x_ref[:, l * panel:(l + 1) * panel]
-    for l in range(leaves):
-        weight = lax.dot_general(
+    weights = [
+        lax.dot_general(
             transfer_ref[l], basis_ref[l], (((0,), (0,)), ((), ())), preferred_element_type=F32
-        ).astype(BF)
-        weight_ref[l] = jnp.concatenate([weight, weight], axis=0)
-    copy.wait()
+        )
+        for l in range(leaves)
+    ]
+    for copy in copies:
+        copy.wait()
+    for l in range(leaves):
+        parent = parents_ref[l]
+        distance = (parent >> 1) ^ z
+        here = (distance & 1) == c
+        slot = jnp.where(here, 2 * ((distance >> 1) ^ c) + (parent & 1), 0)
+        weight_ref[l, slot] = jnp.where(here, weights[l], 0.0).astype(BF)
     for l in range(REACH, leaves - REACH):
         rows = [panels[i] for i in near_rows(near_sources, owner, z, l, leaves, share)]
         near_ref[l - REACH] = dot(
@@ -322,27 +330,16 @@
         total_ref[l] = close + dot(parts[l].astype(BF), basis_ref[l])
 
 
-def down_kernel(parents_hbm, total_ref, down_ref, first_ref, second_ref, weight_ref,
-                send_ref, keep_ref, parents_ref, halves, sem):
-    copy = pltpu.make_async_copy(parents_hbm, parents_ref, sem)
-    copy.start()
+def down_kernel(total_ref, down_ref, first_ref, second_ref, weight_ref, send_ref, keep_ref):
     leaves, vectors, panel = total_ref.shape
-    z, c = lax.axis_index("leaf"), lax.axis_index("lvl")
-    low = low_half(down_ref.shape)
-    zero = jnp.zeros(down_ref.shape, F32)
-    own = down_ref[...].astype(F32)
-    first = first_ref[...].astype(F32)
-    second = second_ref[...].astype(F32)
-    parts = [(0, jnp.where(c == 0, own, zero)), (1, second),
-             (2, jnp.where(c == 0, first, zero)), (3, jnp.where(c == 0, zero, first))]
-    for distance, x in parts:
-        halves[2 * distance] = jnp.where(low, x, 0.0).astype(BF)
-        halves[2 * distance + 1] = jnp.where(low, 0.0, x).astype(BF)
+    c = lax.axis_index("lvl")
+    own, first, second = (r[...].astype(F32) for r in (down_ref, first_ref, second_ref))
+    sources = jnp.concatenate(
+        [jnp.where(c == 0, own, first), jnp.where(c == 0, first, second)], axis=-1
+    ).astype(BF)
     rows = vectors // 4
-    copy.wait()
-    for l in range(leaves):
-        parent = parents_ref[l]
-        part = total_ref[l] + dot(halves[parent ^ (2 * z)], weight_ref[l])
+    for l in range(leaves):
+        part = total_ref[l] + dot(sources, weight_ref[l].reshape(sources.shape[1], panel))
         lanes = slice(l * panel, (l + 1) * panel)
         for w in range(2):
             even = part[2 * w * rows:(2 * w + 1) * rows]
@@ -433,53 +430,56 @@
         prep_kernel,
         out_shape=(
             jax.ShapeDtypeStruct((leaves - 2 * REACH, vectors, panel), F32),
-            jax.ShapeDtypeStruct((leaves, wide, panel), BF),
+            jax.ShapeDtypeStruct((leaves, 4, rank, panel), BF),
         ),
-        in_specs=[HBM] + [VMEM] * 4,
+        in_specs=[HBM] * 2 + [VMEM] * 4,
         out_specs=(VMEM,) * 2,
         scratch_shapes=[
             pltpu.SMEM(near_sources.shape, jnp.int32),
+            pltpu.SMEM(parents.shape, jnp.int32),
             pltpu.VMEM((leaves + 2 * REACH, vectors, panel), BF),
+            pltpu.SemaphoreType.DMA((2,)),
+        ],
+        compiler_params=params,
+        cost_estimate=cost(1.5),
+        name="prep",
+    )(
+        *in_hbm(near_sources, parents), adjoint_in, near_blocks, col_transfer, col_basis
+    )
+    mix = pl.pallas_call(
+        mix_kernel,
+        out_shape=jax.ShapeDtypeStruct((clusters, rank, wide), BF),
+        in_specs=[HBM] + [VMEM] * 2,
+        out_specs=VMEM,
+        scratch_shapes=[
+            pltpu.SMEM(coarse_sources.shape, jnp.int32),
+            pltpu.VMEM((clusters, rank, wide), F32),
             pltpu.SemaphoreType.DMA(()),
         ],
         compiler_params=params,
-        cost_estimate=cost(1.5),
-        name="prep",
-    )(*in_hbm(near_sources), adjoint_in, near_blocks, col_transfer, col_basis)
-    gate = pl.pallas_call(
-        gate_kernel,
-        out_shape=jax.ShapeDtypeStruct((8, 128), F32),
-        in_specs=[pl.BlockSpec(memory_space=pl.ANY)],
-        out_specs=VMEM,
-        compiler_params=params,
         cost_estimate=cost(0.1),
-        name="gate",
-    )(p_lvl)
+        name="mix",
+    )(*in_hbm(coarse_sources), packed, p_lvl)
     joined = pl.pallas_call(
         join_kernel,
         out_shape=jax.ShapeDtypeStruct((2 * messages + edges, vectors, wide), BF),
-        in_specs=[VMEM] * 3,
+        in_specs=[VMEM] * 2 + [pl.BlockSpec(memory_space=pl.ANY)],
         out_specs=VMEM,
         compiler_params=params,
         cost_estimate=cost(0.5),
         name="join",
-    )(a, b, gate)
+    )(a, b, mix)
     joined, near, weight = lax.optimization_barrier((joined, near, weight))
     other = swap(joined, other_core)
     down = pl.pallas_call(
         coarse_kernel,
         out_shape=jax.ShapeDtypeStruct((vectors, wide), BF),
-        in_specs=[HBM] + [VMEM] * 6,
+        in_specs=[VMEM] * 5,
         out_specs=VMEM,
-        scratch_shapes=[
-            pltpu.SMEM(coarse_sources.shape, jnp.int32),
-            pltpu.VMEM((clusters, vectors, wide), BF),
-            pltpu.SemaphoreType.DMA(()),
-        ],
-        compiler_params=params,
-        cost_estimate=cost(1.0),
+        compiler_params=params,
+        cost_estimate=cost(0.5),
         name="coarse",
-    )(coarse_sources, msg, a, b, other, packed, p_lvl)
+    )(msg, a, b, other, mix)
     first = swap(down, lambda z, v, c: (z ^ (3 if c else 2), v, c))
     second = swap(down, lambda z, v, c: (z ^ 1, v, c) if c else None)
     total = pl.pallas_call(
@@ -508,17 +508,12 @@
             jax.ShapeDtypeStruct((2, rows, width), BF),
             jax.ShapeDtypeStruct((2, rows, width), F32),
         ),
-        in_specs=[HBM] + [VMEM] * 5,
+        in_specs=[VMEM] * 5,
         out_specs=(VMEM,) * 2,
-        scratch_shapes=[
-            pltpu.SMEM(parents.shape, jnp.int32),
-            pltpu.VMEM((8, vectors, wide), BF),
-            pltpu.SemaphoreType.DMA(()),
-        ],
         compiler_params=params,
         cost_estimate=cost(1.0),
         name="down",
-    )(parents, total, down, first, second, weight)
+    )(total, down, first, second, weight)
     came = swap(send, other_core)
     send, rest = pl.pallas_call(
         merge_kernel,

time: 30.2 us -> 29 us (0.960)
  waiting for transfers between devices: 7.81 us -> 6.97 us
    pallas_call x1, Pallas kernels: 0.01 us -> 0.89 us  [on_device_paired(): pl.pallas_call(mix_kernel, out_shape=jax.ShapeDtypeStruct((clusters, rank...]
    ppermute x8, waiting for transfers between devices: 7.81 us -> 6.97 us  [swap(): return lax.ppermute(x, axes, pairs)]
    pallas_call x1, Pallas kernels: 0.84 us -> 0.17 us  [on_device_paired(): pl.pallas_call(coarse_kernel, out_shape=jax.ShapeDtypeStruct((vectors, wi...]
    pallas_call x1, Pallas kernels: 0.78 us -> 0.3 us  [on_device_paired(): pl.pallas_call(down_kernel, out_shape=(jax.ShapeDtypeStruct((2, rows, wid...]
  transfers between devices with their start and end apart: 8 -> 8, of which waited for: 5 -> 4; matrix products, arithmetic and copies ran while one was open for 0% -> 0% of each run, Pallas kernels for 11% -> 14%
where the time goes in v5:
time: 29 us; the launch traced here: 28.9 us
  starting transfers between devices  14.5 us (50%)
  waiting for transfers between devices  6.97 us (24%)
  Pallas kernels  6.57 us (23%)
  other arithmetic  0.64 us (2%)
    ppermute x8, starting transfers between devices, swap(): return lax.ppermute(x, axes, pairs)  14.5 us
    ppermute x8, waiting for transfers between devices, swap(): return lax.ppermute(x, axes, pairs)  6.97 us
    pallas_call x1, Pallas kernels, on_device_paired(): pl.pallas_call(local_kernel, out_shape=jax.ShapeDtypeStruct((leaves, vect...  1.96 us
    pallas_call x1, Pallas kernels, on_device_paired(): pl.pallas_call(up_kernel, out_shape=(jax.ShapeDtypeStruct((messages + edg...  1.9 us
    pallas_call x1, Pallas kernels, on_device_paired(): pl.pallas_call(prep_kernel, out_shape=(jax.ShapeDtypeStruct((leaves - 2 *...  1.31 us
    pallas_call x1, Pallas kernels, on_device_paired(): pl.pallas_call(mix_kernel, out_shape=jax.ShapeDtypeStruct((clusters, rank...  0.89 us
    convert_element_type x1, other arithmetic, on_device_paired(): return (rest + came.astype(F32)).astype(BF)  0.64 us
  transfers between devices with their start and end apart: 8, of which 4 were waited for; matrix products, arithmetic and copies ran while one was open for 0% of the time, Pallas kernels for 14%

profile of v5, /device:TPU:0, one launch (start us, length us, event | category | flops | bytes accessed | tf_op | source)
XLA Modules:
  0.0 28.9 jit_solution(13073456236927601675)
XLA Ops:
  0.0 0.0 copy-start.2
  0.0 0.0 copy-start
  0.0 0.0 copy-start.3
  0.0 0.0 copy-start.4
  0.0 1.9 %up.1 = (bf16[12,64,128]{2,1,0:T(8,128)(2,1)S(1)}, bf16[8,64,128]{2,1,0:T(8,128)(2,1)S(1)}, bf16[8,64,128]{2,1,0:T(8,128)(2,1)S(1)}) custom-call(bf16[64,2048]{1,0:T(8,128)(2,1)} %x_ref.3, bf16[8,64,256]{2,1,0:T(8,128)(2,1)} %basis_hbm.1, bf16[8,64,64]{2,1,0:T(8,128)(2,1)} %transfer_hbm.1, s32[8]{0:T(128)} %parents_hbm.3, bf16[2,8,64,64]{3,2,1,0:T(8,128)(2,1)} %coarse_hbm.2), custom_call_target="tpu_custom_call" | custom-call | flops 1500000000 | bytes 1024 | tf_op jit(solution)/shard_map/up/pallas_call | solution.py:404
  1.9 3.1 %collective-permute-start = (bf16[12,64,128]{2,1,0:T(8,128)(2,1)S(1)}, bf16[12,64,128]{2,1,0:T(8,128)(2,1)S(1)}, u32[]{:S(2)}, u32[]{:S(2)}) collective-permute-start(bf16[12,64,128]{2,1,0:T(8,128)(2,1)S(1)} %get-tuple-element.17.own_ref), channel_id=1, source_target_pairs={{0,4},{1,13},{2,6},{3,15},{4,0},{5,9},{6,2},{7,11},{8,12},{9,5},{1... | collective-permute-start | bytes 589832 | tf_op jit(solution)/shard_map/ppermute | solution.py:372
  5.0 0.7 %collective-permute-start.1 = (bf16[8,64,128]{2,1,0:T(8,128)(2,1)S(1)}, bf16[8,64,128]{2,1,0:T(8,128)(2,1)S(1)}, u32[]{:S(2)}, u32[]{:S(2)}) collective-permute-start(bf16[8,64,128]{2,1,0:T(8,128)(2,1)S(1)} %get-tuple-element.18), channel_id=1, source_target_pairs={{1,9},{3,11},{5,13},{7,15},{9,1},{11,3},{13,5},{15,7},{17,25},{19,... | collective-permute-start | bytes 393224 | tf_op jit(solution)/shard_map/ppermute | solution.py:372
  5.7 0.0 copy-start.1
  5.7 0.0 copy-start.5
  5.7 0.0 copy-start.6
  5.7 2.9 %collective-permute-start.2 = (bf16[8,64,128]{2,1,0:T(8,128)(2,1)S(1)}, bf16[8,64,128]{2,1,0:T(8,128)(2,1)S(1)}, u32[]{:S(2)}, u32[]{:S(2)}) collective-permute-start(bf16[8,64,128]{2,1,0:T(8,128)(2,1)S(1)} %get-tuple-element.19.p_own), channel_id=1, source_target_pairs={{0,1},{1,0},{2,3},{3,2},{4,5},{5,4},{6,7},{7,6},{8,9},{9,8},{10,11... | collective-permute-start | bytes 393224 | tf_op jit(solution)/shard_map/ppermute | solution.py:372
  8.6 0.0 copy-done.2
  8.6 0.0 copy-done
  8.6 0.0 copy-done.3
  8.6 0.0 copy-done.4
  8.6 1.3 %prep.1 = (f32[4,64,256]{2,1,0:T(8,128)S(1)}, bf16[8,4,64,256]{3,2,1,0:T(8,128)(2,1)S(1)}) custom-call(s32[8,16]{1,0:T(8,128)} %near_hbm.3, s32[8]{0:T(128)} %parents_hbm.3, bf16[64,2048]{1,0:T(8,128)(2,1)S(1)} %copy-done.2, bf16[8,4,256,256]{3,2,1,0:T(8,128)(2,1)S(1)} %copy-done, bf16[8,64,64]{2,1,0:T(8,128)(2,1)S(1)} %copy-done.4, ...), custom_call_target="tpu_custom_call" | custom-call | flops 1500000000 | bytes 1024 | tf_op jit(solution)/shard_map/prep/pallas_call | solution.py:429
  9.9 0.0 collective-permute-done.2.p_lvl
  10.0 0.9 %mix.1.after_ref.mix_ref = bf16[8,64,128]{2,1,0:T(8,128)(2,1)S(1)} custom-call(s32[2,32]{1,0:T(2,128)} %coarse_hbm.3, bf16[8,64,128]{2,1,0:T(8,128)(2,1)S(1)} %get-tuple-element.19.p_own, bf16[8,64,128]{2,1,0:T(8,128)(2,1)S(1)} %collective-permute-done.2.p_lvl), custom_call_target="tpu_custom_call" | custom-call | flops 100000000 | bytes 1024 | tf_op jit(solution)/shard_map/mix/pallas_call | solution.py:449
  10.9 0.0 collective-permute-done.1.b_ref
  10.9 0.0 collective-permute-done.a_ref
  10.9 3.3 %collective-permute-start.3 = (bf16[20,64,128]{2,1,0:T(8,128)(2,1)S(1)}, bf16[20,64,128]{2,1,0:T(8,128)(2,1)S(1)}, u32[]{:S(2)}, u32[]{:S(2)}) collective-permute-start(bf16[20,64,128]{2,1,0:T(8,128)(2,1)S(1)} %join.1), channel_id=1, source_target_pairs={{0,1},{1,0},{2,3},{3,2},{4,5},{5,4},{6,7},{7,6},{8,9},{9,8},{10,11... | collective-permute-start | bytes 983048 | tf_op jit(solution)/shard_map/ppermute | solution.py:372
  14.2 1.3 %collective-permute-done.3.other_ref = bf16[20,64,128]{2,1,0:T(8,128)(2,1)S(1)} collective-permute-done((bf16[20,64,128]{2,1,0:T(8,128)(2,1)S(1)}, bf16[20,64,128]{2,1,0:T(8,128)(2,1)S(1)}, u32[]{:S(2)}, u32[]{:S(2)}) %collective-permute-start.3) | collective-permute-done | bytes 327712 | tf_op jit(solution)/shard_map/ppermute | solution.py:372
  15.5 0.2 coarse.1.down_ref
  15.7 0.7 %collective-permute-start.5 = (bf16[64,128]{1,0:T(8,128)(2,1)S(1)}, bf16[64,128]{1,0:T(8,128)(2,1)S(1)}, u32[]{:S(2)}, u32[]{:S(2)}) collective-permute-start(bf16[64,128]{1,0:T(8,128)(2,1)S(1)} %coarse.1.down_ref), channel_id=1, source_target_pairs={{1,5},{3,7},{5,1},{7,3},{9,13},{11,15},{13,9},{15,11},{17,21},{19,... | collective-permute-start | bytes 49160 | tf_op jit(solution)/shard_map/ppermute | solution.py:372
  16.3 0.9 %collective-permute-start.4 = (bf16[64,128]{1,0:T(8,128)(2,1)S(1)}, bf16[64,128]{1,0:T(8,128)(2,1)S(1)}, u32[]{:S(2)}, u32[]{:S(2)}) collective-permute-start(bf16[64,128]{1,0:T(8,128)(2,1)S(1)} %coarse.1.down_ref), channel_id=1, source_target_pairs={{0,8},{1,13},{2,10},{3,15},{4,12},{5,9},{6,14},{7,11},{8,0},{9,5},... | collective-permute-start | bytes 49160 | tf_op jit(solution)/shard_map/ppermute | solution.py:372
  17.2 0.0 copy-done.1
  17.2 0.0 copy-done.5
  17.2 0.0 copy-done.6
  17.2 2.0 %local.1.total_ref = f32[8,64,256]{2,1,0:T(8,128)S(1)} custom-call(s32[8,16]{1,0:T(8,128)S(1)} %copy-done.5, s32[8,64]{1,0:T(8,128)S(1)} %copy-done.6, bf16[12,64,128]{2,1,0:T(8,128)(2,1)S(1)} %get-tuple-element.17.own_ref, bf16[12,64,128]{2,1,0:T(8,128)(2,1)S(1)} %collective-permute-done.a_ref, bf16[8,64,128]{2,1,0:T(8,128)(2,1)S(1)} %collective-permute-done.1.b_ref, ...), custom_call_target="tpu_custom_call" | custom-call | flops 4000000000 | bytes 1024 | tf_op jit(solution)/shard_map/local/pallas_call | solution.py:485
  19.1 0.0 collective-permute-done.5.second_ref
  19.2 1.9 %collective-permute-done.4.first_ref = bf16[64,128]{1,0:T(8,128)(2,1)S(1)} collective-permute-done((bf16[64,128]{1,0:T(8,128)(2,1)S(1)}, bf16[64,128]{1,0:T(8,128)(2,1)S(1)}, u32[]{:S(2)}, u32[]{:S(2)}) %collective-permute-start.4) | collective-permute-done | bytes 16416 | tf_op jit(solution)/shard_map/ppermute | solution.py:372
  21.0 0.3 %down.1 = (bf16[2,16,2048]{2,1,0:T(8,128)(2,1)S(1)}, f32[2,16,2048]{2,1,0:T(8,128)S(1)}) custom-call(f32[8,64,256]{2,1,0:T(8,128)S(1)} %local.1.total_ref, bf16[64,128]{1,0:T(8,128)(2,1)S(1)} %coarse.1.down_ref, bf16[64,128]{1,0:T(8,128)(2,1)S(1)} %collective-permute-done.4.first_ref, bf16[64,128]{1,0:T(8,128)(2,1)S(1)} %collective-permute-done.5.second_ref, ...), custom_call_target="tpu_custom_call" | custom-call | flops 1000000000 | bytes 1024 | tf_op jit(solution)/shard_map/down/pallas_call | solution.py:505
  21.3 1.4 %collective-permute-start.6 = (bf16[2,16,2048]{2,1,0:T(8,128)(2,1)S(1)}, bf16[2,16,2048]{2,1,0:T(8,128)(2,1)S(1)}, u32[]{:S(2)}, u32[]{:S(2)}) collective-permute-start(bf16[2,16,2048]{2,1,0:T(8,128)(2,1)S(1)} %get-tuple-element.26), channel_id=1, source_target_pairs={{0,1},{1,0},{2,3},{3,2},{4,5},{5,4},{6,7},{7,6},{8,9},{9,8},{10,11... | collective-permute-start | bytes 393224 | tf_op jit(solution)/shard_map/ppermute | solution.py:372
  22.8 1.0 %collective-permute-done.6.got_ref = bf16[2,16,2048]{2,1,0:T(8,128)(2,1)S(1)} collective-permute-done((bf16[2,16,2048]{2,1,0:T(8,128)(2,1)S(1)}, bf16[2,16,2048]{2,1,0:T(8,128)(2,1)S(1)}, u32[]{:S(2)}, u32[]{:S(2)}) %collective-permute-start.6) | collective-permute-done | bytes 131104 | tf_op jit(solution)/shard_map/ppermute | solution.py:372
  23.8 1.6 %collective-permute-start.7 = (bf16[16,2048]{1,0:T(8,128)(2,1)S(1)}, bf16[16,2048]{1,0:T(8,128)(2,1)S(1)}, u32[]{:S(2)}, u32[]{:S(2)}) collective-permute-start(bf16[16,2048]{1,0:T(8,128)(2,1)S(1)} %get-tuple-element.28), channel_id=1, source_target_pairs={{0,2},{1,3},{2,0},{3,1},{4,6},{5,7},{6,4},{7,5},{8,10},{9,11},{10,... | collective-permute-start | bytes 196616 | tf_op jit(solution)/shard_map/ppermute | solution.py:372
  25.4 2.9 %collective-permute-done.7 = bf16[16,2048]{1,0:T(8,128)(2,1)S(1)} collective-permute-done((bf16[16,2048]{1,0:T(8,128)(2,1)S(1)}, bf16[16,2048]{1,0:T(8,128)(2,1)S(1)}, u32[]{:S(2)}, u32[]{:S(2)}) %collective-permute-start.7) | collective-permute-done | bytes 65568 | tf_op jit(solution)/shard_map/ppermute | solution.py:372
  28.2 0.6 %add_convert_fusion = bf16[16,2048]{1,0:T(8,128)(2,1)} fusion(f32[16,2048]{1,0:T(8,128)S(1)} %get-tuple-element.27, bf16[16,2048]{1,0:T(8,128)(2,1)S(1)} %collective-permute-done.7), kind=kLoop, calls=%fused_computation | loop fusion | flops 98304 | bytes 262144 | tf_op jit(solution)/shard_map/convert_element_type | solution.py:531
  (2 shorter events, 0.0 us)
Async XLA Ops:
  0.0 8.6 %copy-start.2 = (bf16[64,2048]{1,0:T(8,128)(2,1)S(1)}, bf16[64,2048]{1,0:T(8,128)(2,1)}, u32[]{:S(2)}) copy-start(bf16[64,2048]{1,0:T(8,128)(2,1)} %x_ref.3) | copy-start | bytes 786436
  0.0 8.6 %copy-start = (bf16[8,4,256,256]{3,2,1,0:T(8,128)(2,1)S(1)}, bf16[8,4,256,256]{3,2,1,0:T(8,128)(2,1)}, u32[]{:S(2)}) copy-start(bf16[8,4,256,256]{3,2,1,0:T(8,128)(2,1)} %near_blocks_ref.3) | copy-start | bytes 12582916
  0.0 8.6 %copy-start.3 = (bf16[8,64,256]{2,1,0:T(8,128)(2,1)S(1)}, bf16[8,64,256]{2,1,0:T(8,128)(2,1)}, u32[]{:S(2)}) copy-start(bf16[8,64,256]{2,1,0:T(8,128)(2,1)} %basis_ref.3) | copy-start | bytes 786436
  0.0 8.6 %copy-start.4 = (bf16[8,64,64]{2,1,0:T(8,128)(2,1)S(1)}, bf16[8,64,64]{2,1,0:T(8,128)(2,1)}, u32[]{:S(2)}) copy-start(bf16[8,64,64]{2,1,0:T(8,128)(2,1)} %transfer_ref.1) | copy-start | bytes 196612
  1.9 9.0 %collective-permute-start = (bf16[12,64,128]{2,1,0:T(8,128)(2,1)S(1)}, bf16[12,64,128]{2,1,0:T(8,128)(2,1)S(1)}, u32[]{:S(2)}, u32[]{:S(2)}) collective-permute-start(bf16[12,64,128]{2,1,0:T(8,128)(2,1)S(1)} %get-tuple-element.17.own_ref), channel_id=1, source_target_pairs={{0,4},{1,13},{2,6},{3,15},{4,0},{5,9},{6,2},{7,11},{8,12},{9,5},{1... | collective-permute-start | bytes 589832 | tf_op jit(solution)/shard_map/ppermute | solution.py:372
  5.0 5.8 %collective-permute-start.1 = (bf16[8,64,128]{2,1,0:T(8,128)(2,1)S(1)}, bf16[8,64,128]{2,1,0:T(8,128)(2,1)S(1)}, u32[]{:S(2)}, u32[]{:S(2)}) collective-permute-start(bf16[8,64,128]{2,1,0:T(8,128)(2,1)S(1)} %get-tuple-element.18), channel_id=1, source_target_pairs={{1,9},{3,11},{5,13},{7,15},{9,1},{11,3},{13,5},{15,7},{17,25},{19,... | collective-permute-start | bytes 393224 | tf_op jit(solution)/shard_map/ppermute | solution.py:372
  5.7 11.5 %copy-start.1 = (bf16[8,16,64,64]{3,2,1,0:T(8,128)(2,1)S(1)}, bf16[8,16,64,64]{3,2,1,0:T(8,128)(2,1)}, u32[]{:S(2)}) copy-start(bf16[8,16,64,64]{3,2,1,0:T(8,128)(2,1)} %far_blocks_ref.1) | copy-start | bytes 3145732
  5.7 11.5 %copy-start.5 = (s32[8,16]{1,0:T(8,128)S(1)}, s32[8,16]{1,0:T(8,128)}, u32[]{:S(2)}) copy-start(s32[8,16]{1,0:T(8,128)} %near_hbm.3) | copy-start | bytes 1540
  5.7 11.5 %copy-start.6 = (s32[8,64]{1,0:T(8,128)S(1)}, s32[8,64]{1,0:T(8,128)}, u32[]{:S(2)}) copy-start(s32[8,64]{1,0:T(8,128)} %far_hbm.1) | copy-start | bytes 6148
  5.7 4.2 %collective-permute-start.2 = (bf16[8,64,128]{2,1,0:T(8,128)(2,1)S(1)}, bf16[8,64,128]{2,1,0:T(8,128)(2,1)S(1)}, u32[]{:S(2)}, u32[]{:S(2)}) collective-permute-start(bf16[8,64,128]{2,1,0:T(8,128)(2,1)S(1)} %get-tuple-element.19.p_own), channel_id=1, source_target_pairs={{0,1},{1,0},{2,3},{3,2},{4,5},{5,4},{6,7},{7,6},{8,9},{9,8},{10,11... | collective-permute-start | bytes 393224 | tf_op jit(solution)/shard_map/ppermute | solution.py:372
  10.9 4.6 %collective-permute-start.3 = (bf16[20,64,128]{2,1,0:T(8,128)(2,1)S(1)}, bf16[20,64,128]{2,1,0:T(8,128)(2,1)S(1)}, u32[]{:S(2)}, u32[]{:S(2)}) collective-permute-start(bf16[20,64,128]{2,1,0:T(8,128)(2,1)S(1)} %join.1), channel_id=1, source_target_pairs={{0,1},{1,0},{2,3},{3,2},{4,5},{5,4},{6,7},{7,6},{8,9},{9,8},{10,11... | collective-permute-start | bytes 983048 | tf_op jit(solution)/shard_map/ppermute | solution.py:372
  15.7 3.5 %collective-permute-start.5 = (bf16[64,128]{1,0:T(8,128)(2,1)S(1)}, bf16[64,128]{1,0:T(8,128)(2,1)S(1)}, u32[]{:S(2)}, u32[]{:S(2)}) collective-permute-start(bf16[64,128]{1,0:T(8,128)(2,1)S(1)} %coarse.1.down_ref), channel_id=1, source_target_pairs={{1,5},{3,7},{5,1},{7,3},{9,13},{11,15},{13,9},{15,11},{17,21},{19,... | collective-permute-start | bytes 49160 | tf_op jit(solution)/shard_map/ppermute | solution.py:372
  16.3 4.7 %collective-permute-start.4 = (bf16[64,128]{1,0:T(8,128)(2,1)S(1)}, bf16[64,128]{1,0:T(8,128)(2,1)S(1)}, u32[]{:S(2)}, u32[]{:S(2)}) collective-permute-start(bf16[64,128]{1,0:T(8,128)(2,1)S(1)} %coarse.1.down_ref), channel_id=1, source_target_pairs={{0,8},{1,13},{2,10},{3,15},{4,12},{5,9},{6,14},{7,11},{8,0},{9,5},... | collective-permute-start | bytes 49160 | tf_op jit(solution)/shard_map/ppermute | solution.py:372
  21.3 2.4 %collective-permute-start.6 = (bf16[2,16,2048]{2,1,0:T(8,128)(2,1)S(1)}, bf16[2,16,2048]{2,1,0:T(8,128)(2,1)S(1)}, u32[]{:S(2)}, u32[]{:S(2)}) collective-permute-start(bf16[2,16,2048]{2,1,0:T(8,128)(2,1)S(1)} %get-tuple-element.26), channel_id=1, source_target_pairs={{0,1},{1,0},{2,3},{3,2},{4,5},{5,4},{6,7},{7,6},{8,9},{9,8},{10,11... | collective-permute-start | bytes 393224 | tf_op jit(solution)/shard_map/ppermute | solution.py:372
  23.8 4.4 %collective-permute-start.7 = (bf16[16,2048]{1,0:T(8,128)(2,1)S(1)}, bf16[16,2048]{1,0:T(8,128)(2,1)S(1)}, u32[]{:S(2)}, u32[]{:S(2)}) collective-permute-start(bf16[16,2048]{1,0:T(8,128)(2,1)S(1)} %get-tuple-element.28), channel_id=1, source_target_pairs={{0,2},{1,3},{2,0},{3,1},{4,6},{5,7},{6,4},{7,5},{8,10},{9,11},{10,... | collective-permute-start | bytes 196616 | tf_op jit(solution)/shard_map/ppermute | solution.py:372

commit v6 on v5

--- a/solution.py
+++ b/solution.py
@@ -178,21 +178,15 @@
         packed_ref[j] = jnp.concatenate([coarse_ref[0, j], coarse_ref[1, j]], axis=-1)
 
 
-def join_kernel(a_ref, b_ref, after_ref, out_ref):
-    count = a_ref.shape[0]
-    out_ref[:count] = a_ref[...]
-    out_ref[count:] = b_ref[...]
-
-
-def coarse_kernel(own_ref, a_ref, b_ref, other_ref, mix_ref, out_ref):
+def coarse_kernel(*refs):
+    pieces, (mix_ref, out_ref) = refs[:-2], refs[-2:]
     clusters, rank, wide = mix_ref.shape
-    count = a_ref.shape[0]
+    first = clusters // 2
     lanes = []
-    for q in range(b_ref.shape[0] - clusters // 2, b_ref.shape[0]):
-        rest = b_ref[q].astype(F32) + other_ref[count + q].astype(F32)
-        total = (own_ref[q].astype(F32) + a_ref[q].astype(F32)) + (
-            other_ref[q].astype(F32) + rest
-        )
+    for q in range(first, 2 * first):
+        total = pieces[0][q].astype(F32)
+        for piece in pieces[1:]:
+            total = total + piece[q].astype(F32)
         lanes.append(total.astype(BF))
     out_ref[...] = dot(
         jnp.concatenate(lanes, axis=-1), mix_ref[...].reshape(clusters * rank, wide)
@@ -248,8 +242,8 @@
     for l in range(leaves):
         parent = parents_ref[l]
         distance = (parent >> 1) ^ z
-        here = (distance & 1) == c
-        slot = jnp.where(here, 2 * ((distance >> 1) ^ c) + (parent & 1), 0)
+        here = ((distance ^ (distance >> 1)) & 1) == c
+        slot = jnp.where(here, 2 * (distance >> 1) + (parent & 1), 0)
         weight_ref[l, slot] = jnp.where(here, weights[l], 0.0).astype(BF)
     for l in range(REACH, leaves - REACH):
         rows = [panels[i] for i in near_rows(near_sources, owner, z, l, leaves, share)]
@@ -258,7 +252,7 @@
         )
 
 
-def local_kernel(near_hbm, far_hbm, own_ref, a_ref, b_ref, other_ref, x_ref,
+def local_kernel(near_hbm, far_hbm, own_ref, a_ref, b_ref, la_ref, lb_ref, x_ref,
                  near_blocks_ref, far_blocks_ref, basis_ref, near_ref, total_ref,
                  near_sources, far_sources, panels, table, sems):
     copies = [
@@ -278,12 +272,11 @@
     lanes = a_ref.shape[2]
     base = b_ref.shape[0]
     parts = panel // lanes
-    count = a_ref.shape[0]
     for i in range(REACH):
         for w in range(parts):
             where = slice(w * lanes, (w + 1) * lanes)
             panels[at_mine + i, :, where] = a_ref[base + i * parts + w]
-            panels[at_other + i, :, where] = other_ref[base + i * parts + w]
+            panels[at_other + i, :, where] = la_ref[base + i * parts + w]
     for l in range(leaves):
         panels[REACH + l] = x_ref[:, l * panel:(l + 1) * panel]
     pairs = leaves // 2
@@ -291,12 +284,12 @@
     at_o = jnp.where(c == 1, 1, 3) * pairs
     half = 4 * pairs
     for p in range(pairs):
-        third = b_ref[p].astype(F32) + other_ref[count + p].astype(F32)
+        third = b_ref[p].astype(F32) + lb_ref[p].astype(F32)
         for at, x in (
             (p, own_ref[p].astype(F32)),
             (2 * pairs + p, third),
             (at_a + p, a_ref[p].astype(F32)),
-            (at_o + p, other_ref[p].astype(F32)),
+            (at_o + p, la_ref[p].astype(F32)),
         ):
             table[at] = x.astype(BF)
             table[half + at] = swap_halves(x).astype(BF)
@@ -460,32 +453,28 @@
         cost_estimate=cost(0.1),
         name="mix",
     )(*in_hbm(coarse_sources), packed, p_lvl)
-    joined = pl.pallas_call(
-        join_kernel,
-        out_shape=jax.ShapeDtypeStruct((2 * messages + edges, vectors, wide), BF),
-        in_specs=[VMEM] * 2 + [pl.BlockSpec(memory_space=pl.ANY)],
-        out_specs=VMEM,
-        compiler_params=params,
-        cost_estimate=cost(0.5),
-        name="join",
-    )(a, b, mix)
-    joined, near, weight = lax.optimization_barrier((joined, near, weight))
-    other = swap(joined, other_core)
-    down = pl.pallas_call(
-        coarse_kernel,
-        out_shape=jax.ShapeDtypeStruct((vectors, wide), BF),
-        in_specs=[VMEM] * 5,
-        out_specs=VMEM,
-        compiler_params=params,
-        cost_estimate=cost(0.5),
-        name="coarse",
-    )(msg, a, b, other, mix)
-    first = swap(down, lambda z, v, c: (z ^ (3 if c else 2), v, c))
-    second = swap(down, lambda z, v, c: (z ^ 1, v, c) if c else None)
+    a, near, weight, mix = lax.optimization_barrier((a, near, weight, mix))
+    la = swap(a, other_core)
+    lb = swap(b, other_core)
+
+    def coarse(*pieces):
+        return pl.pallas_call(
+            coarse_kernel,
+            out_shape=jax.ShapeDtypeStruct((vectors, wide), BF),
+            in_specs=[VMEM] * (len(pieces) + 1),
+            out_specs=VMEM,
+            compiler_params=params,
+            cost_estimate=cost(0.2),
+            name="coarse",
+        )(*pieces, mix)
+
+    down = coarse(msg, a, la, b, lb)
+    first = swap(down, lambda z, v, c: (z ^ (1 if c else 3), v, c))
+    second = swap(down, lambda z, v, c: (z ^ 2, v, c) if c else None)
     total = pl.pallas_call(
         local_kernel,
         out_shape=jax.ShapeDtypeStruct((leaves, vectors, panel), F32),
-        in_specs=[HBM] * 2 + [VMEM] * 9,
+        in_specs=[HBM] * 2 + [VMEM] * 10,
         out_specs=VMEM,
         scratch_shapes=[
             pltpu.SMEM(near_sources.shape, jnp.int32),
@@ -499,7 +488,7 @@
         name="local",
     )(
         near_sources, far_sources,
-        msg, a, b, other, adjoint_in, near_blocks, far_blocks, col_basis, near,
+        msg, a, b, la, lb, adjoint_in, near_blocks, far_blocks, col_basis, near,
     )
     rows = vectors // 4
     send, keep = pl.pallas_call(

time: 29 us -> 28.8 us (level)
  waiting for transfers between devices: 6.97 us -> 5.97 us
  starting transfers between devices: 14.5 us -> 15.2 us
    ppermute x8 -> x9, waiting for transfers between devices: 6.97 us -> 5.97 us  [swap(): return lax.ppermute(x, axes, pairs)]
    ppermute x8 -> x9, starting transfers between devices: 14.5 us -> 15.2 us  [swap(): return lax.ppermute(x, axes, pairs)]
  transfers between devices with their start and end apart: 8 -> 9, of which waited for: 4 -> 4; matrix products, arithmetic and copies ran while one was open for 0% -> 0% of each run, Pallas kernels for 14% -> 15%
where the time goes in v6:
time: 28.8 us; the launch traced here: 28.6 us
  starting transfers between devices  15.2 us (53%)
  Pallas kernels  6.55 us (23%)
  waiting for transfers between devices  5.97 us (21%)
  other arithmetic  0.64 us (2%)
    ppermute x9, starting transfers between devices, swap(): return lax.ppermute(x, axes, pairs)  15.2 us
    ppermute x9, waiting for transfers between devices, swap(): return lax.ppermute(x, axes, pairs)  5.97 us
    pallas_call x1, Pallas kernels, on_device_paired(): pl.pallas_call(local_kernel, out_shape=jax.ShapeDtypeStruct((leaves, vect...  1.95 us
    pallas_call x1, Pallas kernels, on_device_paired(): pl.pallas_call(up_kernel, out_shape=(jax.ShapeDtypeStruct((messages + edg...  1.9 us
    pallas_call x1, Pallas kernels, on_device_paired(): pl.pallas_call(prep_kernel, out_shape=(jax.ShapeDtypeStruct((leaves - 2 *...  1.31 us
    pallas_call x1, Pallas kernels, on_device_paired(): pl.pallas_call(mix_kernel, out_shape=jax.ShapeDtypeStruct((clusters, rank...  0.89 us
    convert_element_type x1, other arithmetic, on_device_paired(): return (rest + came.astype(F32)).astype(BF)  0.64 us
  transfers between devices with their start and end apart: 9, of which 4 were waited for; matrix products, arithmetic and copies ran while one was open for 0% of the time, Pallas kernels for 15%

profile of v6, /device:TPU:0, one launch (start us, length us, event | category | flops | bytes accessed | tf_op | source)
XLA Modules:
  0.0 28.6 jit_solution(15067380062076571647)
XLA Ops:
  0.0 0.0 copy-start.2
  0.0 0.0 copy-start
  0.0 0.0 copy-start.3
  0.0 0.0 copy-start.4
  0.0 1.9 %up.1 = (bf16[12,64,128]{2,1,0:T(8,128)(2,1)S(1)}, bf16[8,64,128]{2,1,0:T(8,128)(2,1)S(1)}, bf16[8,64,128]{2,1,0:T(8,128)(2,1)S(1)}) custom-call(bf16[64,2048]{1,0:T(8,128)(2,1)} %x_ref.3, bf16[8,64,256]{2,1,0:T(8,128)(2,1)} %basis_hbm.1, bf16[8,64,64]{2,1,0:T(8,128)(2,1)} %transfer_hbm.1, s32[8]{0:T(128)} %parents_hbm.3, bf16[2,8,64,64]{3,2,1,0:T(8,128)(2,1)} %coarse_hbm.2), custom_call_target="tpu_custom_call" | custom-call | flops 1500000000 | bytes 1024 | tf_op jit(solution)/shard_map/up/pallas_call | solution.py:397
  1.9 0.0 copy-start.1
  1.9 0.0 copy-start.5
  1.9 0.0 copy-start.6
  2.0 3.1 %collective-permute-start = (bf16[12,64,128]{2,1,0:T(8,128)(2,1)S(1)}, bf16[12,64,128]{2,1,0:T(8,128)(2,1)S(1)}, u32[]{:S(2)}, u32[]{:S(2)}) collective-permute-start(bf16[12,64,128]{2,1,0:T(8,128)(2,1)S(1)} %get-tuple-element.18.own_ref.refs_0_), channel_id=1, source_target_pairs={{0,4},{1,13},{2,6},{3,15},{4,0},{5,9},{6,2},{7,11},{8,12},{9,5},{1... | collective-permute-start | bytes 589832 | tf_op jit(solution)/shard_map/ppermute | solution.py:365
  5.1 0.7 %collective-permute-start.2 = (bf16[8,64,128]{2,1,0:T(8,128)(2,1)S(1)}, bf16[8,64,128]{2,1,0:T(8,128)(2,1)S(1)}, u32[]{:S(2)}, u32[]{:S(2)}) collective-permute-start(bf16[8,64,128]{2,1,0:T(8,128)(2,1)S(1)} %get-tuple-element.23), channel_id=1, source_target_pairs={{1,9},{3,11},{5,13},{7,15},{9,1},{11,3},{13,5},{15,7},{17,25},{19,... | collective-permute-start | bytes 393224 | tf_op jit(solution)/shard_map/ppermute | solution.py:365
  5.7 2.9 %collective-permute-start.1 = (bf16[8,64,128]{2,1,0:T(8,128)(2,1)S(1)}, bf16[8,64,128]{2,1,0:T(8,128)(2,1)S(1)}, u32[]{:S(2)}, u32[]{:S(2)}) collective-permute-start(bf16[8,64,128]{2,1,0:T(8,128)(2,1)S(1)} %get-tuple-element.21.p_own), channel_id=1, source_target_pairs={{0,1},{1,0},{2,3},{3,2},{4,5},{5,4},{6,7},{7,6},{8,9},{9,8},{10,11... | collective-permute-start | bytes 393224 | tf_op jit(solution)/shard_map/ppermute | solution.py:365
  8.6 0.0 copy-done.2
  8.6 0.0 copy-done
  8.6 0.0 copy-done.3
  8.6 0.0 copy-done.4
  8.6 1.3 %prep.1 = (f32[4,64,256]{2,1,0:T(8,128)S(1)}, bf16[8,4,64,256]{3,2,1,0:T(8,128)(2,1)S(1)}) custom-call(s32[8,16]{1,0:T(8,128)} %near_hbm.3, s32[8]{0:T(128)} %parents_hbm.3, bf16[64,2048]{1,0:T(8,128)(2,1)S(1)} %copy-done.2, bf16[8,4,256,256]{3,2,1,0:T(8,128)(2,1)S(1)} %copy-done, bf16[8,64,64]{2,1,0:T(8,128)(2,1)S(1)} %copy-done.4, ...), custom_call_target="tpu_custom_call" | custom-call | flops 1500000000 | bytes 1024 | tf_op jit(solution)/shard_map/prep/pallas_call | solution.py:422
  9.9 0.0 collective-permute-done.1.p_lvl
  10.0 0.9 %mix.1.refs_5_ = bf16[8,64,128]{2,1,0:T(8,128)(2,1)S(1)} custom-call(s32[2,32]{1,0:T(2,128)} %coarse_hbm.3, bf16[8,64,128]{2,1,0:T(8,128)(2,1)S(1)} %get-tuple-element.21.p_own, bf16[8,64,128]{2,1,0:T(8,128)(2,1)S(1)} %collective-permute-done.1.p_lvl), custom_call_target="tpu_custom_call" | custom-call | flops 100000000 | bytes 1024 | tf_op jit(solution)/shard_map/mix/pallas_call | solution.py:442
  10.9 0.0 collective-permute-done.a_ref.refs_1_
  10.9 0.1 collective-permute-start.3
  11.0 0.0 collective-permute-done.2.b_ref.refs_3_
  11.0 3.2 %collective-permute-start.4 = (bf16[8,64,128]{2,1,0:T(8,128)(2,1)S(1)}, bf16[8,64,128]{2,1,0:T(8,128)(2,1)S(1)}, u32[]{:S(2)}, u32[]{:S(2)}) collective-permute-start(bf16[8,64,128]{2,1,0:T(8,128)(2,1)S(1)} %collective-permute-done.2.b_ref.refs_3_), channel_id=1, source_target_pairs={{0,1},{1,0},{2,3},{3,2},{4,5},{5,4},{6,7},{7,6},{8,9},{9,8},{10,11... | collective-permute-start | bytes 393224 | tf_op jit(solution)/shard_map/ppermute | solution.py:365
  14.2 1.0 %collective-permute-done.4.lb_ref.refs_4_ = bf16[8,64,128]{2,1,0:T(8,128)(2,1)S(1)} collective-permute-done((bf16[8,64,128]{2,1,0:T(8,128)(2,1)S(1)}, bf16[8,64,128]{2,1,0:T(8,128)(2,1)S(1)}, u32[]{:S(2)}, u32[]{:S(2)}) %collective-permute-start.4) | collective-permute-done | bytes 131104 | tf_op jit(solution)/shard_map/ppermute | solution.py:365
  15.1 0.0 collective-permute-done.3.la_ref.refs_2_
  15.2 0.2 coarse.1.down_ref
  15.3 0.7 %collective-permute-start.6 = (bf16[64,128]{1,0:T(8,128)(2,1)S(1)}, bf16[64,128]{1,0:T(8,128)(2,1)S(1)}, u32[]{:S(2)}, u32[]{:S(2)}) collective-permute-start(bf16[64,128]{1,0:T(8,128)(2,1)S(1)} %coarse.1.down_ref), channel_id=1, source_target_pairs={{1,9},{3,11},{5,13},{7,15},{9,1},{11,3},{13,5},{15,7},{17,25},{19,... | collective-permute-start | bytes 49160 | tf_op jit(solution)/shard_map/ppermute | solution.py:365
  16.0 2.5 %collective-permute-start.5 = (bf16[64,128]{1,0:T(8,128)(2,1)S(1)}, bf16[64,128]{1,0:T(8,128)(2,1)S(1)}, u32[]{:S(2)}, u32[]{:S(2)}) collective-permute-start(bf16[64,128]{1,0:T(8,128)(2,1)S(1)} %coarse.1.down_ref), channel_id=1, source_target_pairs={{0,12},{1,5},{2,14},{3,7},{4,8},{5,1},{6,10},{7,3},{8,4},{9,13},{1... | collective-permute-start | bytes 49160 | tf_op jit(solution)/shard_map/ppermute | solution.py:365
  18.5 0.0 copy-done.1
  18.5 0.0 copy-done.5
  18.5 0.0 copy-done.6
  18.5 2.0 %local.1.total_ref = f32[8,64,256]{2,1,0:T(8,128)S(1)} custom-call(s32[8,16]{1,0:T(8,128)S(1)} %copy-done.5, s32[8,64]{1,0:T(8,128)S(1)} %copy-done.6, bf16[12,64,128]{2,1,0:T(8,128)(2,1)S(1)} %get-tuple-element.18.own_ref.refs_0_, bf16[12,64,128]{2,1,0:T(8,128)(2,1)S(1)} %collective-permute-done.a_ref.refs_1_, ...), custom_call_target="tpu_custom_call" | custom-call | flops 4000000000 | bytes 1024 | tf_op jit(solution)/shard_map/local/pallas_call | solution.py:474
  20.5 0.0 collective-permute-done.6.second_ref
  20.5 1.1 %collective-permute-done.5.first_ref = bf16[64,128]{1,0:T(8,128)(2,1)S(1)} collective-permute-done((bf16[64,128]{1,0:T(8,128)(2,1)S(1)}, bf16[64,128]{1,0:T(8,128)(2,1)S(1)}, u32[]{:S(2)}, u32[]{:S(2)}) %collective-permute-start.5) | collective-permute-done | bytes 16416 | tf_op jit(solution)/shard_map/ppermute | solution.py:365
  21.6 0.3 %down.1 = (bf16[2,16,2048]{2,1,0:T(8,128)(2,1)S(1)}, f32[2,16,2048]{2,1,0:T(8,128)S(1)}) custom-call(f32[8,64,256]{2,1,0:T(8,128)S(1)} %local.1.total_ref, bf16[64,128]{1,0:T(8,128)(2,1)S(1)} %coarse.1.down_ref, bf16[64,128]{1,0:T(8,128)(2,1)S(1)} %collective-permute-done.5.first_ref, bf16[64,128]{1,0:T(8,128)(2,1)S(1)} %collective-permute-done.6.second_ref, ...), custom_call_target="tpu_custom_call" | custom-call | flops 1000000000 | bytes 1024 | tf_op jit(solution)/shard_map/down/pallas_call | solution.py:494
  21.9 0.6 %collective-permute-start.7 = (bf16[2,16,2048]{2,1,0:T(8,128)(2,1)S(1)}, bf16[2,16,2048]{2,1,0:T(8,128)(2,1)S(1)}, u32[]{:S(2)}, u32[]{:S(2)}) collective-permute-start(bf16[2,16,2048]{2,1,0:T(8,128)(2,1)S(1)} %get-tuple-element.28), channel_id=1, source_target_pairs={{0,1},{1,0},{2,3},{3,2},{4,5},{5,4},{6,7},{7,6},{8,9},{9,8},{10,11... | collective-permute-start | bytes 393224 | tf_op jit(solution)/shard_map/ppermute | solution.py:365
  22.5 1.0 %collective-permute-done.7.got_ref = bf16[2,16,2048]{2,1,0:T(8,128)(2,1)S(1)} collective-permute-done((bf16[2,16,2048]{2,1,0:T(8,128)(2,1)S(1)}, bf16[2,16,2048]{2,1,0:T(8,128)(2,1)S(1)}, u32[]{:S(2)}, u32[]{:S(2)}) %collective-permute-start.7) | collective-permute-done | bytes 131104 | tf_op jit(solution)/shard_map/ppermute | solution.py:365
  23.5 1.6 %collective-permute-start.8 = (bf16[16,2048]{1,0:T(8,128)(2,1)S(1)}, bf16[16,2048]{1,0:T(8,128)(2,1)S(1)}, u32[]{:S(2)}, u32[]{:S(2)}) collective-permute-start(bf16[16,2048]{1,0:T(8,128)(2,1)S(1)} %get-tuple-element.30), channel_id=1, source_target_pairs={{0,2},{1,3},{2,0},{3,1},{4,6},{5,7},{6,4},{7,5},{8,10},{9,11},{10,... | collective-permute-start | bytes 196616 | tf_op jit(solution)/shard_map/ppermute | solution.py:365
  25.1 2.9 %collective-permute-done.8 = bf16[16,2048]{1,0:T(8,128)(2,1)S(1)} collective-permute-done((bf16[16,2048]{1,0:T(8,128)(2,1)S(1)}, bf16[16,2048]{1,0:T(8,128)(2,1)S(1)}, u32[]{:S(2)}, u32[]{:S(2)}) %collective-permute-start.8) | collective-permute-done | bytes 65568 | tf_op jit(solution)/shard_map/ppermute | solution.py:365
  27.9 0.6 %add_convert_fusion = bf16[16,2048]{1,0:T(8,128)(2,1)} fusion(f32[16,2048]{1,0:T(8,128)S(1)} %get-tuple-element.29, bf16[16,2048]{1,0:T(8,128)(2,1)S(1)} %collective-permute-done.8), kind=kLoop, calls=%fused_computation | loop fusion | flops 98304 | bytes 262144 | tf_op jit(solution)/shard_map/convert_element_type | solution.py:520
  (1 shorter events, 0.0 us)
Async XLA Ops:
  0.0 8.6 %copy-start.2 = (bf16[64,2048]{1,0:T(8,128)(2,1)S(1)}, bf16[64,2048]{1,0:T(8,128)(2,1)}, u32[]{:S(2)}) copy-start(bf16[64,2048]{1,0:T(8,128)(2,1)} %x_ref.3) | copy-start | bytes 786436
  0.0 8.6 %copy-start = (bf16[8,4,256,256]{3,2,1,0:T(8,128)(2,1)S(1)}, bf16[8,4,256,256]{3,2,1,0:T(8,128)(2,1)}, u32[]{:S(2)}) copy-start(bf16[8,4,256,256]{3,2,1,0:T(8,128)(2,1)} %near_blocks_ref.3) | copy-start | bytes 12582916
  0.0 8.6 %copy-start.3 = (bf16[8,64,256]{2,1,0:T(8,128)(2,1)S(1)}, bf16[8,64,256]{2,1,0:T(8,128)(2,1)}, u32[]{:S(2)}) copy-start(bf16[8,64,256]{2,1,0:T(8,128)(2,1)} %basis_ref.3) | copy-start | bytes 786436
  0.0 8.6 %copy-start.4 = (bf16[8,64,64]{2,1,0:T(8,128)(2,1)S(1)}, bf16[8,64,64]{2,1,0:T(8,128)(2,1)}, u32[]{:S(2)}) copy-start(bf16[8,64,64]{2,1,0:T(8,128)(2,1)} %transfer_ref.1) | copy-start | bytes 196612
  1.9 16.6 %copy-start.1 = (bf16[8,16,64,64]{3,2,1,0:T(8,128)(2,1)S(1)}, bf16[8,16,64,64]{3,2,1,0:T(8,128)(2,1)}, u32[]{:S(2)}) copy-start(bf16[8,16,64,64]{3,2,1,0:T(8,128)(2,1)} %far_blocks_ref.1) | copy-start | bytes 3145732
  1.9 16.6 %copy-start.5 = (s32[8,16]{1,0:T(8,128)S(1)}, s32[8,16]{1,0:T(8,128)}, u32[]{:S(2)}) copy-start(s32[8,16]{1,0:T(8,128)} %near_hbm.3) | copy-start | bytes 1540
  1.9 16.6 %copy-start.6 = (s32[8,64]{1,0:T(8,128)S(1)}, s32[8,64]{1,0:T(8,128)}, u32[]{:S(2)}) copy-start(s32[8,64]{1,0:T(8,128)} %far_hbm.1) | copy-start | bytes 6148
  2.0 8.9 %collective-permute-start = (bf16[12,64,128]{2,1,0:T(8,128)(2,1)S(1)}, bf16[12,64,128]{2,1,0:T(8,128)(2,1)S(1)}, u32[]{:S(2)}, u32[]{:S(2)}) collective-permute-start(bf16[12,64,128]{2,1,0:T(8,128)(2,1)S(1)} %get-tuple-element.18.own_ref.refs_0_), channel_id=1, source_target_pairs={{0,4},{1,13},{2,6},{3,15},{4,0},{5,9},{6,2},{7,11},{8,12},{9,5},{1... | collective-permute-start | bytes 589832 | tf_op jit(solution)/shard_map/ppermute | solution.py:365
  5.1 5.9 %collective-permute-start.2 = (bf16[8,64,128]{2,1,0:T(8,128)(2,1)S(1)}, bf16[8,64,128]{2,1,0:T(8,128)(2,1)S(1)}, u32[]{:S(2)}, u32[]{:S(2)}) collective-permute-start(bf16[8,64,128]{2,1,0:T(8,128)(2,1)S(1)} %get-tuple-element.23), channel_id=1, source_target_pairs={{1,9},{3,11},{5,13},{7,15},{9,1},{11,3},{13,5},{15,7},{17,25},{19,... | collective-permute-start | bytes 393224 | tf_op jit(solution)/shard_map/ppermute | solution.py:365
  5.7 4.2 %collective-permute-start.1 = (bf16[8,64,128]{2,1,0:T(8,128)(2,1)S(1)}, bf16[8,64,128]{2,1,0:T(8,128)(2,1)S(1)}, u32[]{:S(2)}, u32[]{:S(2)}) collective-permute-start(bf16[8,64,128]{2,1,0:T(8,128)(2,1)S(1)} %get-tuple-element.21.p_own), channel_id=1, source_target_pairs={{0,1},{1,0},{2,3},{3,2},{4,5},{5,4},{6,7},{7,6},{8,9},{9,8},{10,11... | collective-permute-start | bytes 393224 | tf_op jit(solution)/shard_map/ppermute | solution.py:365
  10.9 4.3 %collective-permute-start.3 = (bf16[12,64,128]{2,1,0:T(8,128)(2,1)S(1)}, bf16[12,64,128]{2,1,0:T(8,128)(2,1)S(1)}, u32[]{:S(2)}, u32[]{:S(2)}) collective-permute-start(bf16[12,64,128]{2,1,0:T(8,128)(2,1)S(1)} %collective-permute-done.a_ref.refs_1_), channel_id=1, source_target_pairs={{0,1},{1,0},{2,3},{3,2},{4,5},{5,4},{6,7},{7,6},{8,9},{9,8},{10,11... | collective-permute-start | bytes 589832 | tf_op jit(solution)/shard_map/ppermute | solution.py:365
  11.0 4.2 %collective-permute-start.4 = (bf16[8,64,128]{2,1,0:T(8,128)(2,1)S(1)}, bf16[8,64,128]{2,1,0:T(8,128)(2,1)S(1)}, u32[]{:S(2)}, u32[]{:S(2)}) collective-permute-start(bf16[8,64,128]{2,1,0:T(8,128)(2,1)S(1)} %collective-permute-done.2.b_ref.refs_3_), channel_id=1, source_target_pairs={{0,1},{1,0},{2,3},{3,2},{4,5},{5,4},{6,7},{7,6},{8,9},{9,8},{10,11... | collective-permute-start | bytes 393224 | tf_op jit(solution)/shard_map/ppermute | solution.py:365
  15.3 5.1 %collective-permute-start.6 = (bf16[64,128]{1,0:T(8,128)(2,1)S(1)}, bf16[64,128]{1,0:T(8,128)(2,1)S(1)}, u32[]{:S(2)}, u32[]{:S(2)}) collective-permute-start(bf16[64,128]{1,0:T(8,128)(2,1)S(1)} %coarse.1.down_ref), channel_id=1, source_target_pairs={{1,9},{3,11},{5,13},{7,15},{9,1},{11,3},{13,5},{15,7},{17,25},{19,... | collective-permute-start | bytes 49160 | tf_op jit(solution)/shard_map/ppermute | solution.py:365
  16.0 5.6 %collective-permute-start.5 = (bf16[64,128]{1,0:T(8,128)(2,1)S(1)}, bf16[64,128]{1,0:T(8,128)(2,1)S(1)}, u32[]{:S(2)}, u32[]{:S(2)}) collective-permute-start(bf16[64,128]{1,0:T(8,128)(2,1)S(1)} %coarse.1.down_ref), channel_id=1, source_target_pairs={{0,12},{1,5},{2,14},{3,7},{4,8},{5,1},{6,10},{7,3},{8,4},{9,13},{1... | collective-permute-start | bytes 49160 | tf_op jit(solution)/shard_map/ppermute | solution.py:365
  21.9 1.6 %collective-permute-start.7 = (bf16[2,16,2048]{2,1,0:T(8,128)(2,1)S(1)}, bf16[2,16,2048]{2,1,0:T(8,128)(2,1)S(1)}, u32[]{:S(2)}, u32[]{:S(2)}) collective-permute-start(bf16[2,16,2048]{2,1,0:T(8,128)(2,1)S(1)} %get-tuple-element.28), channel_id=1, source_target_pairs={{0,1},{1,0},{2,3},{3,2},{4,5},{5,4},{6,7},{7,6},{8,9},{9,8},{10,11... | collective-permute-start | bytes 393224 | tf_op jit(solution)/shard_map/ppermute | solution.py:365
  23.5 4.4 %collective-permute-start.8 = (bf16[16,2048]{1,0:T(8,128)(2,1)S(1)}, bf16[16,2048]{1,0:T(8,128)(2,1)S(1)}, u32[]{:S(2)}, u32[]{:S(2)}) collective-permute-start(bf16[16,2048]{1,0:T(8,128)(2,1)S(1)} %get-tuple-element.30), channel_id=1, source_target_pairs={{0,2},{1,3},{2,0},{3,1},{4,6},{5,7},{6,4},{7,5},{8,10},{9,11},{10,... | collective-permute-start | bytes 196616 | tf_op jit(solution)/shard_map/ppermute | solution.py:365

commit v7 on v6

--- a/solution.py
+++ b/solution.py
@@ -437,7 +437,7 @@
         cost_estimate=cost(1.5),
         name="prep",
     )(
-        *in_hbm(near_sources, parents), adjoint_in, near_blocks, col_transfer, col_basis
+        *in_hbm(near_sources, parents), adjoint_in, *in_hbm(near_blocks), col_transfer, col_basis
     )
     mix = pl.pallas_call(
         mix_kernel,

time: 28.8 us -> 28.8 us (level)
  Pallas kernels: 6.55 us -> 8.71 us
  starting transfers between devices: 15.2 us -> 13.1 us
    pallas_call x1, Pallas kernels: 1.31 us -> 3.55 us  [on_device_paired(): pl.pallas_call(prep_kernel, out_shape=(jax.ShapeDtypeStruct((leaves - 2 *...]
    ppermute x9, starting transfers between devices: 15.2 us -> 13.1 us  [swap(): return lax.ppermute(x, axes, pairs)]
  transfers between devices with their start and end apart: 9 -> 9, of which waited for: 4 -> 4; matrix products, arithmetic and copies ran while one was open for 0% -> 0% of each run, Pallas kernels for 15% -> 22%
where the time goes in v7:
time: 28.8 us; the launch traced here: 28.5 us
  starting transfers between devices  13.1 us (45%)
  Pallas kernels  8.71 us (30%)
  waiting for transfers between devices  5.95 us (21%)
  other arithmetic  0.64 us (2%)
    ppermute x9, starting transfers between devices, swap(): return lax.ppermute(x, axes, pairs)  13.1 us
    ppermute x9, waiting for transfers between devices, swap(): return lax.ppermute(x, axes, pairs)  5.95 us
    pallas_call x1, Pallas kernels, on_device_paired(): pl.pallas_call(prep_kernel, out_shape=(jax.ShapeDtypeStruct((leaves - 2 *...  3.55 us
    pallas_call x1, Pallas kernels, on_device_paired(): pl.pallas_call(local_kernel, out_shape=jax.ShapeDtypeStruct((leaves, vect...  1.95 us
    pallas_call x1, Pallas kernels, on_device_paired(): pl.pallas_call(up_kernel, out_shape=(jax.ShapeDtypeStruct((messages + edg...  1.82 us
    pallas_call x1, Pallas kernels, on_device_paired(): pl.pallas_call(mix_kernel, out_shape=jax.ShapeDtypeStruct((clusters, rank...  0.9 us
    convert_element_type x1, other arithmetic, on_device_paired(): return (rest + came.astype(F32)).astype(BF)  0.64 us
  transfers between devices with their start and end apart: 9, of which 4 were waited for; matrix products, arithmetic and copies ran while one was open for 0% of the time, Pallas kernels for 22%

profile of v7, /device:TPU:0, one launch (start us, length us, event | category | flops | bytes accessed | tf_op | source)
XLA Modules:
  0.0 28.5 jit_solution(10169278874856344582)
XLA Ops:
  0.0 0.0 copy-start.2
  0.0 0.0 copy-start.3
  0.0 0.0 copy-start.4
  0.0 1.8 %up.1 = (bf16[12,64,128]{2,1,0:T(8,128)(2,1)S(1)}, bf16[8,64,128]{2,1,0:T(8,128)(2,1)S(1)}, bf16[8,64,128]{2,1,0:T(8,128)(2,1)S(1)}) custom-call(bf16[64,2048]{1,0:T(8,128)(2,1)} %x_ref.3, bf16[8,64,256]{2,1,0:T(8,128)(2,1)} %basis_hbm.1, bf16[8,64,64]{2,1,0:T(8,128)(2,1)} %transfer_hbm.1, s32[8]{0:T(128)} %parents_hbm.3, bf16[2,8,64,64]{3,2,1,0:T(8,128)(2,1)} %coarse_hbm.2), custom_call_target="tpu_custom_call" | custom-call | flops 1500000000 | bytes 1024 | tf_op jit(solution)/shard_map/up/pallas_call | solution.py:397
  1.8 0.0 copy-start
  1.8 0.0 copy-start.1
  1.9 0.0 copy-start.5
  1.9 0.0 copy-start.6
  1.9 3.1 %collective-permute-start = (bf16[12,64,128]{2,1,0:T(8,128)(2,1)S(1)}, bf16[12,64,128]{2,1,0:T(8,128)(2,1)S(1)}, u32[]{:S(2)}, u32[]{:S(2)}) collective-permute-start(bf16[12,64,128]{2,1,0:T(8,128)(2,1)S(1)} %get-tuple-element.18.own_ref.refs_0_), channel_id=1, source_target_pairs={{0,4},{1,13},{2,6},{3,15},{4,0},{5,9},{6,2},{7,11},{8,12},{9,5},{1... | collective-permute-start | bytes 589832 | tf_op jit(solution)/shard_map/ppermute | solution.py:365
  5.0 0.7 %collective-permute-start.2 = (bf16[8,64,128]{2,1,0:T(8,128)(2,1)S(1)}, bf16[8,64,128]{2,1,0:T(8,128)(2,1)S(1)}, u32[]{:S(2)}, u32[]{:S(2)}) collective-permute-start(bf16[8,64,128]{2,1,0:T(8,128)(2,1)S(1)} %get-tuple-element.23), channel_id=1, source_target_pairs={{1,9},{3,11},{5,13},{7,15},{9,1},{11,3},{13,5},{15,7},{17,25},{19,... | collective-permute-start | bytes 393224 | tf_op jit(solution)/shard_map/ppermute | solution.py:365
  5.6 2.9 %collective-permute-start.1 = (bf16[8,64,128]{2,1,0:T(8,128)(2,1)S(1)}, bf16[8,64,128]{2,1,0:T(8,128)(2,1)S(1)}, u32[]{:S(2)}, u32[]{:S(2)}) collective-permute-start(bf16[8,64,128]{2,1,0:T(8,128)(2,1)S(1)} %get-tuple-element.21.p_own), channel_id=1, source_target_pairs={{0,1},{1,0},{2,3},{3,2},{4,5},{5,4},{6,7},{7,6},{8,9},{9,8},{10,11... | collective-permute-start | bytes 393224 | tf_op jit(solution)/shard_map/ppermute | solution.py:365
  8.5 0.0 copy-done.2
  8.5 0.0 copy-done.3
  8.5 0.0 copy-done.4
  8.5 3.6 %prep.1 = (f32[4,64,256]{2,1,0:T(8,128)S(1)}, bf16[8,4,64,256]{3,2,1,0:T(8,128)(2,1)S(1)}) custom-call(s32[8,16]{1,0:T(8,128)} %near_hbm.3, s32[8]{0:T(128)} %parents_hbm.3, bf16[64,2048]{1,0:T(8,128)(2,1)S(1)} %copy-done.2, bf16[8,4,256,256]{3,2,1,0:T(8,128)(2,1)} %near_blocks_ref.3, bf16[8,64,64]{2,1,0:T(8,128)(2,1)S(1)} %copy-done.4, ...), custom_call_target="tpu_custom_call" | custom-call | flops 1500000000 | bytes 1024 | tf_op jit(solution)/shard_map/prep/pallas_call | solution.py:422
  12.1 0.0 collective-permute-done.1.p_lvl
  12.1 0.9 %mix.1.refs_5_ = bf16[8,64,128]{2,1,0:T(8,128)(2,1)S(1)} custom-call(s32[2,32]{1,0:T(2,128)} %coarse_hbm.3, bf16[8,64,128]{2,1,0:T(8,128)(2,1)S(1)} %get-tuple-element.21.p_own, bf16[8,64,128]{2,1,0:T(8,128)(2,1)S(1)} %collective-permute-done.1.p_lvl), custom_call_target="tpu_custom_call" | custom-call | flops 100000000 | bytes 1024 | tf_op jit(solution)/shard_map/mix/pallas_call | solution.py:442
  13.0 0.0 collective-permute-done.a_ref.refs_1_
  13.0 0.1 collective-permute-start.3
  13.1 0.0 collective-permute-done.2.b_ref.refs_3_
  13.1 1.0 %collective-permute-start.4 = (bf16[8,64,128]{2,1,0:T(8,128)(2,1)S(1)}, bf16[8,64,128]{2,1,0:T(8,128)(2,1)S(1)}, u32[]{:S(2)}, u32[]{:S(2)}) collective-permute-start(bf16[8,64,128]{2,1,0:T(8,128)(2,1)S(1)} %collective-permute-done.2.b_ref.refs_3_), channel_id=1, source_target_pairs={{0,1},{1,0},{2,3},{3,2},{4,5},{5,4},{6,7},{7,6},{8,9},{9,8},{10,11... | collective-permute-start | bytes 393224 | tf_op jit(solution)/shard_map/ppermute | solution.py:365
  14.1 1.0 %collective-permute-done.4.lb_ref.refs_4_ = bf16[8,64,128]{2,1,0:T(8,128)(2,1)S(1)} collective-permute-done((bf16[8,64,128]{2,1,0:T(8,128)(2,1)S(1)}, bf16[8,64,128]{2,1,0:T(8,128)(2,1)S(1)}, u32[]{:S(2)}, u32[]{:S(2)}) %collective-permute-start.4) | collective-permute-done | bytes 131104 | tf_op jit(solution)/shard_map/ppermute | solution.py:365
  15.1 0.0 collective-permute-done.3.la_ref.refs_2_
  15.1 0.2 coarse.1.down_ref
  15.3 0.7 %collective-permute-start.6 = (bf16[64,128]{1,0:T(8,128)(2,1)S(1)}, bf16[64,128]{1,0:T(8,128)(2,1)S(1)}, u32[]{:S(2)}, u32[]{:S(2)}) collective-permute-start(bf16[64,128]{1,0:T(8,128)(2,1)S(1)} %coarse.1.down_ref), channel_id=1, source_target_pairs={{1,9},{3,11},{5,13},{7,15},{9,1},{11,3},{13,5},{15,7},{17,25},{19,... | collective-permute-start | bytes 49160 | tf_op jit(solution)/shard_map/ppermute | solution.py:365
  16.0 2.5 %collective-permute-start.5 = (bf16[64,128]{1,0:T(8,128)(2,1)S(1)}, bf16[64,128]{1,0:T(8,128)(2,1)S(1)}, u32[]{:S(2)}, u32[]{:S(2)}) collective-permute-start(bf16[64,128]{1,0:T(8,128)(2,1)S(1)} %coarse.1.down_ref), channel_id=1, source_target_pairs={{0,12},{1,5},{2,14},{3,7},{4,8},{5,1},{6,10},{7,3},{8,4},{9,13},{1... | collective-permute-start | bytes 49160 | tf_op jit(solution)/shard_map/ppermute | solution.py:365
  18.5 0.0 copy-done
  18.5 0.0 copy-done.1
  18.5 0.0 copy-done.5
  18.5 0.0 copy-done.6
  18.5 1.9 %local.1.total_ref = f32[8,64,256]{2,1,0:T(8,128)S(1)} custom-call(s32[8,16]{1,0:T(8,128)S(1)} %copy-done.5, s32[8,64]{1,0:T(8,128)S(1)} %copy-done.6, bf16[12,64,128]{2,1,0:T(8,128)(2,1)S(1)} %get-tuple-element.18.own_ref.refs_0_, bf16[12,64,128]{2,1,0:T(8,128)(2,1)S(1)} %collective-permute-done.a_ref.refs_1_, ...), custom_call_target="tpu_custom_call" | custom-call | flops 4000000000 | bytes 1024 | tf_op jit(solution)/shard_map/local/pallas_call | solution.py:474
  20.5 0.0 collective-permute-done.6.second_ref
  20.5 1.1 %collective-permute-done.5.first_ref = bf16[64,128]{1,0:T(8,128)(2,1)S(1)} collective-permute-done((bf16[64,128]{1,0:T(8,128)(2,1)S(1)}, bf16[64,128]{1,0:T(8,128)(2,1)S(1)}, u32[]{:S(2)}, u32[]{:S(2)}) %collective-permute-start.5) | collective-permute-done | bytes 16416 | tf_op jit(solution)/shard_map/ppermute | solution.py:365
  21.6 0.3 %down.1 = (bf16[2,16,2048]{2,1,0:T(8,128)(2,1)S(1)}, f32[2,16,2048]{2,1,0:T(8,128)S(1)}) custom-call(f32[8,64,256]{2,1,0:T(8,128)S(1)} %local.1.total_ref, bf16[64,128]{1,0:T(8,128)(2,1)S(1)} %coarse.1.down_ref, bf16[64,128]{1,0:T(8,128)(2,1)S(1)} %collective-permute-done.5.first_ref, bf16[64,128]{1,0:T(8,128)(2,1)S(1)} %collective-permute-done.6.second_ref, ...), custom_call_target="tpu_custom_call" | custom-call | flops 1000000000 | bytes 1024 | tf_op jit(solution)/shard_map/down/pallas_call | solution.py:494
  21.9 0.6 %collective-permute-start.7 = (bf16[2,16,2048]{2,1,0:T(8,128)(2,1)S(1)}, bf16[2,16,2048]{2,1,0:T(8,128)(2,1)S(1)}, u32[]{:S(2)}, u32[]{:S(2)}) collective-permute-start(bf16[2,16,2048]{2,1,0:T(8,128)(2,1)S(1)} %get-tuple-element.28), channel_id=1, source_target_pairs={{0,1},{1,0},{2,3},{3,2},{4,5},{5,4},{6,7},{7,6},{8,9},{9,8},{10,11... | collective-permute-start | bytes 393224 | tf_op jit(solution)/shard_map/ppermute | solution.py:365
  22.5 1.0 %collective-permute-done.7.got_ref = bf16[2,16,2048]{2,1,0:T(8,128)(2,1)S(1)} collective-permute-done((bf16[2,16,2048]{2,1,0:T(8,128)(2,1)S(1)}, bf16[2,16,2048]{2,1,0:T(8,128)(2,1)S(1)}, u32[]{:S(2)}, u32[]{:S(2)}) %collective-permute-start.7) | collective-permute-done | bytes 131104 | tf_op jit(solution)/shard_map/ppermute | solution.py:365
  23.5 1.6 %collective-permute-start.8 = (bf16[16,2048]{1,0:T(8,128)(2,1)S(1)}, bf16[16,2048]{1,0:T(8,128)(2,1)S(1)}, u32[]{:S(2)}, u32[]{:S(2)}) collective-permute-start(bf16[16,2048]{1,0:T(8,128)(2,1)S(1)} %get-tuple-element.30), channel_id=1, source_target_pairs={{0,2},{1,3},{2,0},{3,1},{4,6},{5,7},{6,4},{7,5},{8,10},{9,11},{10,... | collective-permute-start | bytes 196616 | tf_op jit(solution)/shard_map/ppermute | solution.py:365
  25.1 2.8 %collective-permute-done.8 = bf16[16,2048]{1,0:T(8,128)(2,1)S(1)} collective-permute-done((bf16[16,2048]{1,0:T(8,128)(2,1)S(1)}, bf16[16,2048]{1,0:T(8,128)(2,1)S(1)}, u32[]{:S(2)}, u32[]{:S(2)}) %collective-permute-start.8) | collective-permute-done | bytes 65568 | tf_op jit(solution)/shard_map/ppermute | solution.py:365
  27.9 0.6 %add_convert_fusion = bf16[16,2048]{1,0:T(8,128)(2,1)} fusion(f32[16,2048]{1,0:T(8,128)S(1)} %get-tuple-element.29, bf16[16,2048]{1,0:T(8,128)(2,1)S(1)} %collective-permute-done.8), kind=kLoop, calls=%fused_computation | loop fusion | flops 98304 | bytes 262144 | tf_op jit(solution)/shard_map/convert_element_type | solution.py:520
  (1 shorter events, 0.0 us)
Async XLA Ops:
  0.0 8.5 %copy-start.2 = (bf16[64,2048]{1,0:T(8,128)(2,1)S(1)}, bf16[64,2048]{1,0:T(8,128)(2,1)}, u32[]{:S(2)}) copy-start(bf16[64,2048]{1,0:T(8,128)(2,1)} %x_ref.3) | copy-start | bytes 786436
  0.0 8.5 %copy-start.3 = (bf16[8,64,256]{2,1,0:T(8,128)(2,1)S(1)}, bf16[8,64,256]{2,1,0:T(8,128)(2,1)}, u32[]{:S(2)}) copy-start(bf16[8,64,256]{2,1,0:T(8,128)(2,1)} %basis_ref.3) | copy-start | bytes 786436
  0.0 8.5 %copy-start.4 = (bf16[8,64,64]{2,1,0:T(8,128)(2,1)S(1)}, bf16[8,64,64]{2,1,0:T(8,128)(2,1)}, u32[]{:S(2)}) copy-start(bf16[8,64,64]{2,1,0:T(8,128)(2,1)} %transfer_ref.1) | copy-start | bytes 196612
  1.8 16.7 %copy-start = (bf16[8,4,256,256]{3,2,1,0:T(8,128)(2,1)S(1)}, bf16[8,4,256,256]{3,2,1,0:T(8,128)(2,1)}, u32[]{:S(2)}) copy-start(bf16[8,4,256,256]{3,2,1,0:T(8,128)(2,1)} %near_blocks_ref.3) | copy-start | bytes 12582916
  1.8 16.6 %copy-start.1 = (bf16[8,16,64,64]{3,2,1,0:T(8,128)(2,1)S(1)}, bf16[8,16,64,64]{3,2,1,0:T(8,128)(2,1)}, u32[]{:S(2)}) copy-start(bf16[8,16,64,64]{3,2,1,0:T(8,128)(2,1)} %far_blocks_ref.1) | copy-start | bytes 3145732
  1.9 16.6 %copy-start.5 = (s32[8,16]{1,0:T(8,128)S(1)}, s32[8,16]{1,0:T(8,128)}, u32[]{:S(2)}) copy-start(s32[8,16]{1,0:T(8,128)} %near_hbm.3) | copy-start | bytes 1540
  1.9 16.6 %copy-start.6 = (s32[8,64]{1,0:T(8,128)S(1)}, s32[8,64]{1,0:T(8,128)}, u32[]{:S(2)}) copy-start(s32[8,64]{1,0:T(8,128)} %far_hbm.1) | copy-start | bytes 6148
  1.9 11.1 %collective-permute-start = (bf16[12,64,128]{2,1,0:T(8,128)(2,1)S(1)}, bf16[12,64,128]{2,1,0:T(8,128)(2,1)S(1)}, u32[]{:S(2)}, u32[]{:S(2)}) collective-permute-start(bf16[12,64,128]{2,1,0:T(8,128)(2,1)S(1)} %get-tuple-element.18.own_ref.refs_0_), channel_id=1, source_target_pairs={{0,4},{1,13},{2,6},{3,15},{4,0},{5,9},{6,2},{7,11},{8,12},{9,5},{1... | collective-permute-start | bytes 589832 | tf_op jit(solution)/shard_map/ppermute | solution.py:365
  5.0 8.2 %collective-permute-start.2 = (bf16[8,64,128]{2,1,0:T(8,128)(2,1)S(1)}, bf16[8,64,128]{2,1,0:T(8,128)(2,1)S(1)}, u32[]{:S(2)}, u32[]{:S(2)}) collective-permute-start(bf16[8,64,128]{2,1,0:T(8,128)(2,1)S(1)} %get-tuple-element.23), channel_id=1, source_target_pairs={{1,9},{3,11},{5,13},{7,15},{9,1},{11,3},{13,5},{15,7},{17,25},{19,... | collective-permute-start | bytes 393224 | tf_op jit(solution)/shard_map/ppermute | solution.py:365
  5.6 6.5 %collective-permute-start.1 = (bf16[8,64,128]{2,1,0:T(8,128)(2,1)S(1)}, bf16[8,64,128]{2,1,0:T(8,128)(2,1)S(1)}, u32[]{:S(2)}, u32[]{:S(2)}) collective-permute-start(bf16[8,64,128]{2,1,0:T(8,128)(2,1)S(1)} %get-tuple-element.21.p_own), channel_id=1, source_target_pairs={{0,1},{1,0},{2,3},{3,2},{4,5},{5,4},{6,7},{7,6},{8,9},{9,8},{10,11... | collective-permute-start | bytes 393224 | tf_op jit(solution)/shard_map/ppermute | solution.py:365
  13.0 2.1 %collective-permute-start.3 = (bf16[12,64,128]{2,1,0:T(8,128)(2,1)S(1)}, bf16[12,64,128]{2,1,0:T(8,128)(2,1)S(1)}, u32[]{:S(2)}, u32[]{:S(2)}) collective-permute-start(bf16[12,64,128]{2,1,0:T(8,128)(2,1)S(1)} %collective-permute-done.a_ref.refs_1_), channel_id=1, source_target_pairs={{0,1},{1,0},{2,3},{3,2},{4,5},{5,4},{6,7},{7,6},{8,9},{9,8},{10,11... | collective-permute-start | bytes 589832 | tf_op jit(solution)/shard_map/ppermute | solution.py:365
  13.1 2.0 %collective-permute-start.4 = (bf16[8,64,128]{2,1,0:T(8,128)(2,1)S(1)}, bf16[8,64,128]{2,1,0:T(8,128)(2,1)S(1)}, u32[]{:S(2)}, u32[]{:S(2)}) collective-permute-start(bf16[8,64,128]{2,1,0:T(8,128)(2,1)S(1)} %collective-permute-done.2.b_ref.refs_3_), channel_id=1, source_target_pairs={{0,1},{1,0},{2,3},{3,2},{4,5},{5,4},{6,7},{7,6},{8,9},{9,8},{10,11... | collective-permute-start | bytes 393224 | tf_op jit(solution)/shard_map/ppermute | solution.py:365
  15.3 5.1 %collective-permute-start.6 = (bf16[64,128]{1,0:T(8,128)(2,1)S(1)}, bf16[64,128]{1,0:T(8,128)(2,1)S(1)}, u32[]{:S(2)}, u32[]{:S(2)}) collective-permute-start(bf16[64,128]{1,0:T(8,128)(2,1)S(1)} %coarse.1.down_ref), channel_id=1, source_target_pairs={{1,9},{3,11},{5,13},{7,15},{9,1},{11,3},{13,5},{15,7},{17,25},{19,... | collective-permute-start | bytes 49160 | tf_op jit(solution)/shard_map/ppermute | solution.py:365
  16.0 5.6 %collective-permute-start.5 = (bf16[64,128]{1,0:T(8,128)(2,1)S(1)}, bf16[64,128]{1,0:T(8,128)(2,1)S(1)}, u32[]{:S(2)}, u32[]{:S(2)}) collective-permute-start(bf16[64,128]{1,0:T(8,128)(2,1)S(1)} %coarse.1.down_ref), channel_id=1, source_target_pairs={{0,12},{1,5},{2,14},{3,7},{4,8},{5,1},{6,10},{7,3},{8,4},{9,13},{1... | collective-permute-start | bytes 49160 | tf_op jit(solution)/shard_map/ppermute | solution.py:365
  21.9 1.6 %collective-permute-start.7 = (bf16[2,16,2048]{2,1,0:T(8,128)(2,1)S(1)}, bf16[2,16,2048]{2,1,0:T(8,128)(2,1)S(1)}, u32[]{:S(2)}, u32[]{:S(2)}) collective-permute-start(bf16[2,16,2048]{2,1,0:T(8,128)(2,1)S(1)} %get-tuple-element.28), channel_id=1, source_target_pairs={{0,1},{1,0},{2,3},{3,2},{4,5},{5,4},{6,7},{7,6},{8,9},{9,8},{10,11... | collective-permute-start | bytes 393224 | tf_op jit(solution)/shard_map/ppermute | solution.py:365
  23.5 4.4 %collective-permute-start.8 = (bf16[16,2048]{1,0:T(8,128)(2,1)S(1)}, bf16[16,2048]{1,0:T(8,128)(2,1)S(1)}, u32[]{:S(2)}, u32[]{:S(2)}) collective-permute-start(bf16[16,2048]{1,0:T(8,128)(2,1)S(1)} %get-tuple-element.30), channel_id=1, source_target_pairs={{0,2},{1,3},{2,0},{3,1},{4,6},{5,7},{6,4},{7,5},{8,10},{9,11},{10,... | collective-permute-start | bytes 196616 | tf_op jit(solution)/shard_map/ppermute | solution.py:365
